TPU v7x, 32 devices: a whole 2x2x4 slice. The times are simulated.
32 devices in a mesh: curve: 8 (over y, x, core), group: 4 (over z).
Axes of the slice: x: 2, y: 2, z: 4, core: 2. Of those that a mesh axis runs over, the one named last changes fastest.
Arguments:
- points: bfloat16 [65536, 256], P(('curve', 'group')), may hold values from -9 to 9
- qkv_one: bfloat16 [256, 768], replicated, may hold values from -1.25 to 1.25
- proj_one: bfloat16 [256, 256], replicated, may hold values from -0.375 to 0.375
- up_one: bfloat16 [256, 1024], replicated, may hold values from -0.375 to 0.375
- down_one: bfloat16 [1024, 256], replicated, may hold values from -0.1875 to 0.1875
- hilbert_device: int32 [65536], P(('curve', 'group')), may hold values from 0 to 31, as said below
- hilbert_position: int32 [65536], P(('curve', 'group')), may hold values from 0 to 2047, as said below
- neighbors: int32 [65536, 27], P(('curve', 'group')), may hold values from -1 to 4096, as said below
- conv_two: bfloat16 [6912, 256], replicated, may hold values from -0.09375 to 0.09375
- linear_two: bfloat16 [256, 256], replicated, may hold values from -0.375 to 0.375
Outputs:
- features: bfloat16 [65536, 256], P(('curve', 'group'))
Inputs may be any that keep to these rules, and one draw needn't show every extreme that they name: `hilbert_device`: together with hilbert_position it is a permutation of the points; every device's span receives 2048 points; the number of points that device s sends to device d depends only on (d - s) modulo the number of devices, is at most 128, and equals 128 for some pairs in every draw. `hilbert_position`: distinct for the points that go to one device. `neighbors`: -1 marks a missing neighbour; otherwise the neighbour is a point of the crop. Offset 27 // 2 is the point itself; offset 0 is the point 2048 rows before and offset 27 - 1 the point 2048 rows after, where those lie in the crop.
All inputs are finite; a program needn't handle non-finite values.
Results may differ from a plain program's by a relative error of at most 0.015.
The roundings to bfloat16 on the way count: a program that leaves them out, or rounds other values in their place, can miss the bound.
Values may be sent and summed in bfloat16 or wider, within the bound.
No kernel may reach another device: no remote copies, remote signals or barrier semaphores. Data moves between devices by JAX's collectives and lax.ppermute only.
A program may use at most 128 MiB of HBM per device.

v0:
```python
import jax
import jax.numpy as jnp
from jax import lax
from jax.sharding import PartitionSpec as P

HEADS = 16
HEAD_DIM = 16
PATCH = 1024


EPS = 1e-05


def with_halo(cells, sides, width, closed):
    for axis, dim in sides:
        count = lax.axis_size(axis)
        ends = count if closed else count - 1
        head = lax.slice_in_dim(cells, 0, width, axis=dim)
        tail = lax.slice_in_dim(cells, cells.shape[dim] - width, cells.shape[dim], axis=dim)
        cells = jnp.concatenate(
            [
                lax.ppermute(tail, axis, [(i, (i + 1) % count) for i in range(ends)]),
                cells,
                lax.ppermute(head, axis, [((i + 1) % count, i) for i in range(ends)]),
            ],
            axis=dim,
        )
    return cells


def layer_norm(values):
    values = values.astype(jnp.float32)
    center = jnp.mean(values, axis=-1, keepdims=True)
    spread = jnp.mean((values - center) ** 2, axis=-1, keepdims=True)
    return (values - center) * lax.rsqrt(spread + EPS)


def block_attention(queries, keys_all, values_all):
    row_count = queries.shape[0]
    half_patch = PATCH // 2
    block_count = row_count // half_patch
    group_heads = HEADS // 2
    span = group_heads * HEAD_DIM

    def one_block(block_index):
        query_rows = lax.dynamic_slice_in_dim(queries, block_index * half_patch, half_patch, 0)
        start = PATCH * ((block_index + 1) // 2)
        key_rows = lax.dynamic_slice_in_dim(keys_all, start, PATCH, 0)
        value_rows = lax.dynamic_slice_in_dim(values_all, start, PATCH, 0)
        pieces = []
        for group in range(2):
            lower = group * span
            query_group = query_rows[:, lower : lower + span].reshape(
                half_patch, group_heads, HEAD_DIM
            )
            key_group = key_rows[:, lower : lower + span].reshape(PATCH, group_heads, HEAD_DIM)
            value_group = value_rows[:, lower : lower + span].reshape(PATCH, group_heads, HEAD_DIM)
            scores = jnp.einsum(
                "qhd,khd->hqk", query_group, key_group, preferred_element_type=jnp.float32
            ) * HEAD_DIM ** (-0.5)
            weights = jax.nn.softmax(scores, axis=-1).astype(jnp.bfloat16)
            result = jnp.einsum(
                "hqk,khd->qhd", weights, value_group, preferred_element_type=jnp.float32
            ).astype(jnp.bfloat16)
            pieces.append(result.reshape(half_patch, span))
        return jnp.concatenate(pieces, axis=1)

    mixed = lax.map(one_block, jnp.arange(block_count, dtype=jnp.int32))
    return mixed.reshape(row_count, -1)


def finish(residual, mixed, proj_w, up_w, down_w):
    after = (
        residual.astype(jnp.float32) + jnp.dot(mixed, proj_w, preferred_element_type=jnp.float32)
    ).astype(jnp.bfloat16)
    normed = layer_norm(after).astype(jnp.bfloat16)
    hidden = jax.nn.gelu(
        jnp.dot(normed, up_w, preferred_element_type=jnp.float32), approximate=False
    ).astype(jnp.bfloat16)
    return (
        after.astype(jnp.float32) + jnp.dot(hidden, down_w, preferred_element_type=jnp.float32)
    ).astype(jnp.bfloat16)


def on_device(
    points,
    qkv_one,
    proj_one,
    up_one,
    down_one,
    hilbert_device,
    hilbert_position,
    neighbors,
    conv_two,
    linear_two,
):
    row_count = points.shape[0]
    channels = points.shape[1]
    half_patch = PATCH // 2
    normed = layer_norm(points).astype(jnp.bfloat16)
    projected = jnp.dot(normed, qkv_one, preferred_element_type=jnp.float32).astype(jnp.bfloat16)
    extended = with_halo(projected[:, channels:], ((("curve", "group"), 0),), half_patch, True)
    mixed = block_attention(projected[:, :channels], extended[:, :channels], extended[:, channels:])
    z_out = finish(points, mixed, proj_one, up_one, down_one)
    devices = lax.axis_size(("curve", "group"))
    capacity = 2 * row_count // devices
    onehot = (hilbert_device[:, None] == jnp.arange(devices, dtype=jnp.int32)[None, :]).astype(
        jnp.int32
    )
    running = jnp.cumsum(onehot, axis=0)
    slot_index = jnp.sum(onehot * running, axis=1) - 1
    send_index = hilbert_device * capacity + slot_index
    send_rows = jnp.zeros((devices * capacity, channels), jnp.bfloat16).at[send_index].set(z_out)
    send_place = jnp.full((devices * capacity,), -1, jnp.int32).at[send_index].set(hilbert_position)
    got_rows, got_place = (
        lax.all_to_all(
            send_rows.reshape(devices, capacity, channels),
            ("curve", "group"),
            split_axis=0,
            concat_axis=0,
            tiled=True,
        ),
        lax.all_to_all(
            send_place.reshape(devices, capacity),
            ("curve", "group"),
            split_axis=0,
            concat_axis=0,
            tiled=True,
        ),
    )
    flat_place = got_place.reshape(-1)
    target = jnp.where(flat_place < 0, row_count, flat_place)
    serial = (
        jnp.zeros((row_count, channels), jnp.bfloat16)
        .at[target]
        .set(got_rows.reshape(-1, channels), mode="drop")
    )
    reach_ext = with_halo(serial, ((("curve", "group"), 0),), row_count, False)
    conv_block = min(512, row_count)

    def conv_piece(block_index):
        start = block_index * conv_block
        near = lax.dynamic_slice_in_dim(neighbors, start, conv_block, 0)
        valid = near >= 0
        index_rows = (
            start + jnp.arange(conv_block, dtype=jnp.int32)[:, None] + jnp.where(valid, near, 0)
        )
        gathered = jnp.where(valid[..., None], reach_ext[index_rows], jnp.zeros((), jnp.bfloat16))
        return jnp.dot(
            gathered.reshape(conv_block, -1), conv_two, preferred_element_type=jnp.float32
        ).astype(jnp.bfloat16)

    conv = lax.map(conv_piece, jnp.arange(row_count // conv_block, dtype=jnp.int32)).reshape(
        row_count, channels
    )
    linear = jnp.dot(conv, linear_two, preferred_element_type=jnp.float32)
    return (serial.astype(jnp.float32) + layer_norm(linear)).astype(jnp.bfloat16)


def solution(mesh):
    return jax.shard_map(
        on_device,
        mesh=mesh,
        in_specs=(
            P(("curve", "group"), None),
            P(),
            P(),
            P(),
            P(),
            P(("curve", "group")),
            P(("curve", "group")),
            P(("curve", "group"), None),
            P(),
            P(),
        ),
        out_specs=P(("curve", "group"), None),
        check_vma=False,
    )
```

profile of v0, /device:TPU:1, one launch (start us, length us, event | category | flops | bytes accessed | tf_op | source)
XLA Modules:
  0.0 648.1 jit_solution(13930971436551916883)
XLA Ops:
  0.0 1.6 copy.23
  2.1 2.1 convolution_convert_fusion.1
  4.2 1.7 copy-done.5
  6.9 2.1 collective-permute-start
  9.0 2.6 collective-permute-start.1
  11.6 9.1 %reduce-window.6 = s32[32,16,128]{2,1,0:T(8,128)S(1)} reduce-window(s32[32,16,128]{2,1,0:T(8,128)S(1)} %fusion.87, s32[]{:T(128)} %constant.151.clone.1), window={size=1x1x128 pad=0_0x0_0x127_0}, to_apply=%region_0.0 | reduce-window | flops 8323072 | bytes 524292 | tf_op jit(solution)/shard_map/reduce-window
  21.5 8.8 %scatter_custom_fusion = s32[4096]{0:T(1024)} fusion(s32[2048]{0:T(1024)S(1)} %compare_select_fusion.3, s32[2048]{0:T(1024)} %param.20, s32[]{:T(128)} %constant.149.clone.1), kind=kCustom, calls=%fused_computation.105 | custom fusion | bytes 16896 | tf_op jit(solution)/shard_map/scatter | solution.py:114
  30.3 4.5 all-to-all-start
  34.8 2.3 slice.78
  37.1 1.7 slice.75
  39.1 1.9 fusion.122
  42.0 109.0 %while.22 = (s32[]{:T(128)}, bf16[4,512,256]{2,1,0:T(8,128)(2,1)}, s32[4]{0:T(128)S(1)}, bf16[3072,256]{1,0:T(8,128)(2,1)}, bf16[2048,256]{1,0:T(8,128)(2,1)}, /...) while((s32[]{:T(128)}, bf16[4,512,256]{2,1,0:T(8,128)(2,1)}, ...), condition=%wide.region_11.12_spmd, body=%wide.region_6.11_spmd.sunk | while | flops 864694272 | bytes 9241023 | solution.py:68
  46.9 4.9 fusion.183
  51.8 5.7 fusion.184
  57.8 4.9 fusion.185
  62.7 5.7 fusion.186
  74.0 4.9 fusion.183
  78.9 5.7 fusion.184
  84.9 4.9 fusion.185
  89.8 5.7 fusion.186
  101.1 4.9 fusion.183
  106.0 5.7 fusion.184
  112.0 4.9 fusion.185
  116.9 5.7 fusion.186
  128.2 4.9 fusion.183
  133.1 5.7 fusion.184
  139.2 4.9 fusion.185
  144.0 5.7 fusion.186
  151.0 1.7 convert_reduce_fusion
  153.1 20.8 %fusion.61 = bf16[2048,256]{0,1:T(8,128)(2,1)S(1)} fusion(bf16[1024,256]{1,0:T(8,128)(2,1)S(1)} %copy-done, bf16[256,1024]{1,0:T(8,128)(2,1)} %param.17, bf16[2048,256]{0,1:T(8,128)(2,1)S(1)} %get-tuple-element.178, f32[2048]{0:T(1024)S(1)} %add_rsqrt_fusion.1, f32[2048]{0:T(1024)S(1)} %broadcast_multiply_fusion.1), kind=kOutput, calls=%fused_computation.73 | convolution fusion | flops 2287468544 | bytes 3162112 | tf_op jit(solution)/shard_map/dot_general | solution.py:81
  174.4 11.2 %scatter_custom_fusion.1 = bf16[4096,256]{1,0:T(8,128)(2,1)} fusion(s32[2048]{0:T(1024)} %copy-done.9, bf16[2048,256]{1,0:T(8,128)(2,1)S(1)} %copy.30, bf16[]{:T(256)} %constant.148.clone.1), kind=kCustom, calls=%fused_computation.88 | custom fusion | bytes 2097664 | tf_op jit(solution)/shard_map/scatter | solution.py:113
  185.7 6.0 all-to-all-start.1
  192.4 47.5 %all-to-all-done.1 = bf16[32,128,256]{2,1,0:T(8,128)(2,1)S(1)} async-done(((bf16[32,128,256]{2,1,0:T(8,128)(2,1)}), bf16[32,128,256]{2,1,0:T(8,128)(2,1)S(1)}, u32[]{:S(2)}, u32[]{:S(2)}) %all-to-all-start.1) | async-done | bytes 2097184 | tf_op jit(solution)/shard_map/all_to_all | solution.py:116
  239.9 18.1 %scatter_custom_fusion.2 = bf16[2048,256]{1,0:T(8,128)(2,1)S(1)} fusion(s32[4096]{0:T(1024)S(1)} %bitcast.149, bf16[4096,256]{1,0:T(8,128)(2,1)S(1)} %bitcast.144, bf16[]{:T(256)} %constant.148.clone.1), kind=kCustom, calls=%fused_computation.90 | custom fusion | bytes 1048578 | tf_op jit(solution)/shard_map/scatter | solution.py:136
  258.0 3.7 collective-permute-start.3
  261.7 1.9 collective-permute-start.2
  263.6 1.4 copy.31
  265.1 19.0 %collective-permute-done.3 = bf16[2048,256]{1,0:T(8,128)(2,1)S(1)} collective-permute-done((bf16[2048,256]{1,0:T(8,128)(2,1)S(1)}, bf16[2048,256]{1,0:T(8,128)(2,1)S(1)}, u32[]{:S(2)}, u32[]{:S(2)}) %collective-permute-start.3) | collective-permute-done | bytes 1048608 | tf_op jit(solution)/shard_map/ppermute | solution.py:24
  285.0 23.4 %collective-permute-done.2 = bf16[2048,256]{1,0:T(8,128)(2,1)} collective-permute-done((bf16[2048,256]{1,0:T(8,128)(2,1)S(1)}, bf16[2048,256]{1,0:T(8,128)(2,1)}, u32[]{:S(2)}, u32[]{:S(2)}) %collective-permute-start.2) | collective-permute-done | bytes 1048608 | tf_op jit(solution)/shard_map/ppermute | solution.py:22
  308.4 2.1 pad_maximum_fusion.1
  311.6 331.3 %while.23 = (s32[]{:T(128)}, bf16[4,512,256]{2,1,0:T(8,128)(2,1)}, s32[4]{0:T(128)S(1)}, s32[2048,27]{0,1:T(8,128)}, bf16[6144,256]{1,0:T(8,128)(2,1)S(1)}, /*in...) while((s32[]{:T(128)}, bf16[4,512,256]{2,1,0:T(8,128)(2,1)}, ...), condition=%wide.region_17.18_spmd, body=%wide.region_16.17_spmd.sunk | while | flops 1815720960 | bytes 68199608 | solution.py:153
  316.1 38.8 %gather_fusion = bf16[13824,256]{1,0:T(8,128)(2,1)} fusion(bf16[6144,256]{1,0:T(8,128)(2,1)S(1)} %get-tuple-element.336, s32[14336]{0:T(1024)S(1)} %pad_clamp_fusion.2), kind=kCustom, calls=%fused_computation.clone.1 | custom fusion | bytes 14211072 | tf_op jit(solution)/shard_map/while/body/eval_jaxpr/gather | solution.py:148
  354.8 11.3 %reshape.224 = bf16[512,27,256]{2,1,0:T(8,128)(2,1)} reshape(bf16[13824,256]{1,0:T(8,128)(2,1)} %gather_fusion) | data formatting | bytes 14155776 | tf_op jit(solution)/shard_map/while/body/eval_jaxpr/gather | solution.py:148
  366.1 8.0 %broadcast_select_fusion.2 = bf16[512,27,256]{2,1,0:T(8,128)(2,1)} fusion(bf16[512,27,256]{2,1,0:T(8,128)(2,1)} %reshape.224, pred[512,27]{1,0:T(8,128)(4,1)S(1)} %broadcast_compare_fusion.2), kind=kLoop, calls=%fused_computation.33.clone.1 | loop fusion | flops 3538944 | bytes 14169600 | tf_op jit(solution)/shard_map/while/body/eval_jaxpr/jit(_where)/select_n | solution.py:148
  374.1 13.6 %copy.67 = bf16[512,27,256]{0,2,1:T(8,128)(2,1)} copy(bf16[512,27,256]{2,1,0:T(8,128)(2,1)} %broadcast_select_fusion.2) | data formatting | bytes 14155776 | tf_op jit(solution)/shard_map/while/body/eval_jaxpr/jit(_where)/select_n | solution.py:148
  387.7 6.7 %fusion.189 = bf16[4,512,256]{2,1,0:T(8,128)(2,1)} fusion(bf16[4,512,256]{2,1,0:T(8,128)(2,1)} %get-tuple-element.323, s32[]{:T(128)S(6)} %copy.78, bf16[512,6912]{0,1:T(8,128)(2,1)} %bitcast.129, bf16[6912,256]{1,0:T(8,128)(2,1)} %get-tuple-element.337), kind=kOutput, calls=%fused_computation.36.clone.1 | convolution fusion | flops 1812070400 | bytes 10878980 | tf_op jit(solution)/shard_map/while/body/eval_jaxpr/dot_general | solution.py:149
  398.9 38.8 %gather_fusion = bf16[13824,256]{1,0:T(8,128)(2,1)} fusion(bf16[6144,256]{1,0:T(8,128)(2,1)S(1)} %get-tuple-element.336, s32[14336]{0:T(1024)S(1)} %pad_clamp_fusion.2), kind=kCustom, calls=%fused_computation.clone.1 | custom fusion | bytes 14211072 | tf_op jit(solution)/shard_map/while/body/eval_jaxpr/gather | solution.py:148
  437.6 11.3 %reshape.224 = bf16[512,27,256]{2,1,0:T(8,128)(2,1)} reshape(bf16[13824,256]{1,0:T(8,128)(2,1)} %gather_fusion) | data formatting | bytes 14155776 | tf_op jit(solution)/shard_map/while/body/eval_jaxpr/gather | solution.py:148
  448.9 8.0 %broadcast_select_fusion.2 = bf16[512,27,256]{2,1,0:T(8,128)(2,1)} fusion(bf16[512,27,256]{2,1,0:T(8,128)(2,1)} %reshape.224, pred[512,27]{1,0:T(8,128)(4,1)S(1)} %broadcast_compare_fusion.2), kind=kLoop, calls=%fused_computation.33.clone.1 | loop fusion | flops 3538944 | bytes 14169600 | tf_op jit(solution)/shard_map/while/body/eval_jaxpr/jit(_where)/select_n | solution.py:148
  456.9 13.6 %copy.67 = bf16[512,27,256]{0,2,1:T(8,128)(2,1)} copy(bf16[512,27,256]{2,1,0:T(8,128)(2,1)} %broadcast_select_fusion.2) | data formatting | bytes 14155776 | tf_op jit(solution)/shard_map/while/body/eval_jaxpr/jit(_where)/select_n | solution.py:148
  470.5 6.8 %fusion.189 = bf16[4,512,256]{2,1,0:T(8,128)(2,1)} fusion(bf16[4,512,256]{2,1,0:T(8,128)(2,1)} %get-tuple-element.323, s32[]{:T(128)S(6)} %copy.78, bf16[512,6912]{0,1:T(8,128)(2,1)} %bitcast.129, bf16[6912,256]{1,0:T(8,128)(2,1)} %get-tuple-element.337), kind=kOutput, calls=%fused_computation.36.clone.1 | convolution fusion | flops 1812070400 | bytes 10878980 | tf_op jit(solution)/shard_map/while/body/eval_jaxpr/dot_general | solution.py:149
  481.7 38.8 %gather_fusion = bf16[13824,256]{1,0:T(8,128)(2,1)} fusion(bf16[6144,256]{1,0:T(8,128)(2,1)S(1)} %get-tuple-element.336, s32[14336]{0:T(1024)S(1)} %pad_clamp_fusion.2), kind=kCustom, calls=%fused_computation.clone.1 | custom fusion | bytes 14211072 | tf_op jit(solution)/shard_map/while/body/eval_jaxpr/gather | solution.py:148
  520.5 11.3 %reshape.224 = bf16[512,27,256]{2,1,0:T(8,128)(2,1)} reshape(bf16[13824,256]{1,0:T(8,128)(2,1)} %gather_fusion) | data formatting | bytes 14155776 | tf_op jit(solution)/shard_map/while/body/eval_jaxpr/gather | solution.py:148
  531.8 8.0 %broadcast_select_fusion.2 = bf16[512,27,256]{2,1,0:T(8,128)(2,1)} fusion(bf16[512,27,256]{2,1,0:T(8,128)(2,1)} %reshape.224, pred[512,27]{1,0:T(8,128)(4,1)S(1)} %broadcast_compare_fusion.2), kind=kLoop, calls=%fused_computation.33.clone.1 | loop fusion | flops 3538944 | bytes 14169600 | tf_op jit(solution)/shard_map/while/body/eval_jaxpr/jit(_where)/select_n | solution.py:148
  539.8 13.6 %copy.67 = bf16[512,27,256]{0,2,1:T(8,128)(2,1)} copy(bf16[512,27,256]{2,1,0:T(8,128)(2,1)} %broadcast_select_fusion.2) | data formatting | bytes 14155776 | tf_op jit(solution)/shard_map/while/body/eval_jaxpr/jit(_where)/select_n | solution.py:148
  553.3 6.8 %fusion.189 = bf16[4,512,256]{2,1,0:T(8,128)(2,1)} fusion(bf16[4,512,256]{2,1,0:T(8,128)(2,1)} %get-tuple-element.323, s32[]{:T(128)S(6)} %copy.78, bf16[512,6912]{0,1:T(8,128)(2,1)} %bitcast.129, bf16[6912,256]{1,0:T(8,128)(2,1)} %get-tuple-element.337), kind=kOutput, calls=%fused_computation.36.clone.1 | convolution fusion | flops 1812070400 | bytes 10878980 | tf_op jit(solution)/shard_map/while/body/eval_jaxpr/dot_general | solution.py:149
  564.5 38.8 %gather_fusion = bf16[13824,256]{1,0:T(8,128)(2,1)} fusion(bf16[6144,256]{1,0:T(8,128)(2,1)S(1)} %get-tuple-element.336, s32[14336]{0:T(1024)S(1)} %pad_clamp_fusion.2), kind=kCustom, calls=%fused_computation.clone.1 | custom fusion | bytes 14211072 | tf_op jit(solution)/shard_map/while/body/eval_jaxpr/gather | solution.py:148
  603.3 11.3 %reshape.224 = bf16[512,27,256]{2,1,0:T(8,128)(2,1)} reshape(bf16[13824,256]{1,0:T(8,128)(2,1)} %gather_fusion) | data formatting | bytes 14155776 | tf_op jit(solution)/shard_map/while/body/eval_jaxpr/gather | solution.py:148
  614.6 8.0 %broadcast_select_fusion.2 = bf16[512,27,256]{2,1,0:T(8,128)(2,1)} fusion(bf16[512,27,256]{2,1,0:T(8,128)(2,1)} %reshape.224, pred[512,27]{1,0:T(8,128)(4,1)S(1)} %broadcast_compare_fusion.2), kind=kLoop, calls=%fused_computation.33.clone.1 | loop fusion | flops 3538944 | bytes 14169600 | tf_op jit(solution)/shard_map/while/body/eval_jaxpr/jit(_where)/select_n | solution.py:148
  622.6 13.6 %copy.67 = bf16[512,27,256]{0,2,1:T(8,128)(2,1)} copy(bf16[512,27,256]{2,1,0:T(8,128)(2,1)} %broadcast_select_fusion.2) | data formatting | bytes 14155776 | tf_op jit(solution)/shard_map/while/body/eval_jaxpr/jit(_where)/select_n | solution.py:148
  636.2 6.8 %fusion.189 = bf16[4,512,256]{2,1,0:T(8,128)(2,1)} fusion(bf16[4,512,256]{2,1,0:T(8,128)(2,1)} %get-tuple-element.323, s32[]{:T(128)S(6)} %copy.78, bf16[512,6912]{0,1:T(8,128)(2,1)} %bitcast.129, bf16[6912,256]{1,0:T(8,128)(2,1)} %get-tuple-element.337), kind=kOutput, calls=%fused_computation.36.clone.1 | convolution fusion | flops 1812070400 | bytes 10878980 | tf_op jit(solution)/shard_map/while/body/eval_jaxpr/dot_general | solution.py:149
  642.9 1.8 fusion.124
  645.0 1.6 add_convert_fusion
  646.6 1.3 copy.33
  (127 shorter events, 40.7 us)
Async XLA Ops:
  0.0 153.1 %copy-start = (bf16[1024,256]{1,0:T(8,128)(2,1)S(1)}, bf16[1024,256]{1,0:T(8,128)(2,1)}, u32[]{:S(2)}) copy-start(bf16[1024,256]{1,0:T(8,128)(2,1)} %param.18) | copy-start | bytes 1572868
  0.0 11.6 %copy-start.8 = (s32[2048]{0:T(1024)S(1)}, s32[2048]{0:T(1024)}, u32[]{:S(2)}) copy-start(s32[2048]{0:T(1024)} %param.19) | copy-start | bytes 24580
  1.6 35.5 %copy-start.2 = (bf16[2048,256]{0,1:T(8,128)(2,1)}, bf16[2048,256]{0,1:T(8,128)(2,1)S(1)}, u32[]{:S(2)}) copy-start(bf16[2048,256]{0,1:T(8,128)(2,1)S(1)} %copy.23) | copy-start | bytes 3145732
  4.1 1.7 copy-start.5
  6.9 31.9 %collective-permute-start = (bf16[512,512]{1,0:T(8,128)(2,1)}, bf16[512,512]{1,0:T(8,128)(2,1)S(1)}, u32[]{:S(2)}, u32[]{:S(2)}) collective-permute-start(bf16[512,512]{1,0:T(8,128)(2,1)} %get-tuple-element.175), channel_id=1, source_target_pairs={{0,1},{1,2},{2,3},{3,4},{4,5},{5,6},{6,7},{7,8},{8,9},{9,10},{10,1... | collective-permute-start | bytes 1572872 | tf_op jit(solution)/shard_map/ppermute | solution.py:22
  9.0 29.8 %collective-permute-start.1 = (bf16[512,512]{1,0:T(8,128)(2,1)}, bf16[512,512]{1,0:T(8,128)(2,1)S(1)}, u32[]{:S(2)}, u32[]{:S(2)}) collective-permute-start(bf16[512,512]{1,0:T(8,128)(2,1)} %get-tuple-element.176), channel_id=1, source_target_pairs={{1,0},{2,1},{3,2},{4,3},{5,4},{6,5},{7,6},{8,7},{9,8},{10,9},{11,1... | collective-permute-start | bytes 1572872 | tf_op jit(solution)/shard_map/ppermute | solution.py:24
  21.5 19.4 %copy-start.9 = (s32[2048]{0:T(1024)}, s32[2048]{0:T(1024)S(1)}, u32[]{:S(2)}) copy-start(s32[2048]{0:T(1024)S(1)} %compare_select_fusion.3) | copy-start | bytes 24580
  30.3 155.3 %all-to-all-start = ((s32[32,1,128]{2,1,0:T(1,128)}), s32[32,1,128]{2,1,0:T(1,128)}, u32[]{:S(2)}, u32[]{:S(2)}) async-start(s32[32,1,128]{2,1,0:T(1,128)} %bitcast.20), calls=%async_computation | async-start | bytes 32768 | tf_op jit(solution)/shard_map/all_to_all | solution.py:123
  42.0 109.0 %copy-start.3 = (bf16[2048,256]{0,1:T(8,128)(2,1)S(1)}, bf16[2048,256]{0,1:T(8,128)(2,1)}, u32[]{:S(2)}) copy-start(bf16[2048,256]{0,1:T(8,128)(2,1)} %copy-done.2) | copy-start | bytes 3145732
  42.0 109.0 %copy-start.7 = (bf16[256,256]{1,0:T(8,128)(2,1)S(1)}, bf16[256,256]{1,0:T(8,128)(2,1)}, u32[]{:S(2)}) copy-start(bf16[256,256]{1,0:T(8,128)(2,1)} %param.16) | copy-start | bytes 393220
  185.7 54.2 %all-to-all-start.1 = ((bf16[32,128,256]{2,1,0:T(8,128)(2,1)}), bf16[32,128,256]{2,1,0:T(8,128)(2,1)S(1)}, u32[]{:S(2)}, u32[]{:S(2)}) async-start(bf16[32,128,256]{2,1,0:T(8,128)(2,1)} %bitcast.24), calls=%async_computation.1 | async-start | bytes 4194304 | tf_op jit(solution)/shard_map/all_to_all | solution.py:116
  258.0 26.0 %copy-start.4 = (bf16[2048,256]{1,0:T(8,128)(2,1)}, bf16[2048,256]{1,0:T(8,128)(2,1)S(1)}, u32[]{:S(2)}) copy-start(bf16[2048,256]{1,0:T(8,128)(2,1)S(1)} %scatter_custom_fusion.2) | copy-start | bytes 3145732
  258.0 26.0 %collective-permute-start.3 = (bf16[2048,256]{1,0:T(8,128)(2,1)S(1)}, bf16[2048,256]{1,0:T(8,128)(2,1)S(1)}, u32[]{:S(2)}, u32[]{:S(2)}) collective-permute-start(bf16[2048,256]{1,0:T(8,128)(2,1)S(1)} %scatter_custom_fusion.2), channel_id=1, source_target_pairs={{1,0},{2,1},{3,2},{4,3},{5,4},{6,5},{7,6},{8,7},{9,8},{10,9},{11,1... | collective-permute-start | bytes 3145736 | tf_op jit(solution)/shard_map/ppermute | solution.py:24
  261.7 46.7 %collective-permute-start.2 = (bf16[2048,256]{1,0:T(8,128)(2,1)S(1)}, bf16[2048,256]{1,0:T(8,128)(2,1)}, u32[]{:S(2)}, u32[]{:S(2)}) collective-permute-start(bf16[2048,256]{1,0:T(8,128)(2,1)S(1)} %scatter_custom_fusion.2), channel_id=1, source_target_pairs={{0,1},{1,2},{2,3},{3,4},{4,5},{5,6},{6,7},{7,8},{8,9},{9,10},{10,1... | collective-permute-start | bytes 3145736 | tf_op jit(solution)/shard_map/ppermute | solution.py:22
  284.0 1.0 copy-start.6
  642.9 5.0 copy-start.1
where the time goes:
time: 656 us; the launch traced here: 648 us
  local copies, waits for them, and re-layouts  339 us (52%)
  matrix products  138 us (21%)
  waiting for transfers between devices  89.9 us (14%)
  other arithmetic  51 us (8%)
  starting transfers between devices  20.7 us (3%)
  loops' own time  9.03 us (1%)
    gather x8, local copies, waits for them, and re-layouts, conv_piece(): reach_ext[index_rows]  200 us
    select_n x4, local copies, waits for them, and re-layouts, conv_piece(): jnp.where(valid[..., None], reach_ext[index_rows], jnp.zeros((), jnp.bflo...  54.4 us
    all_to_all x1, waiting for transfers between devices, on_device(): lax.all_to_all(send_rows.reshape(devices, capacity, channels), ('curve',...  47.5 us
    dot_general x8, matrix products, one_block(): jnp.einsum('hqk,khd->qhd', weights, value_group, preferred_element_type=j...  45.5 us
    sub x8, matrix products, one_block(): weights = jax.nn.softmax(scores, axis=-1).astype(jnp.bfloat16)  39.1 us
    select_n x4, other arithmetic, conv_piece(): jnp.where(valid[..., None], reach_ext[index_rows], jnp.zeros((), jnp.bflo...  32 us
    dot_general x4, matrix products, conv_piece(): jnp.dot(gathered.reshape(conv_block, -1), conv_two, preferred_element_typ...  27 us
    ppermute x2, waiting for transfers between devices, with_halo(): lax.ppermute(tail, axis, [(i, (i + 1) % count) for i in range(ends)])  23.4 us
  transfers between devices with their start and end apart: 6, of which 3 were waited for; matrix products, arithmetic and copies ran while one was open for 26% of the time, Pallas kernels for 0%

commit v1 on v0

--- a/solution.py
+++ b/solution.py
@@ -1,6 +1,10 @@
+import functools
+
 import jax
 import jax.numpy as jnp
 from jax import lax
+from jax.experimental import pallas as pl
+from jax.experimental.pallas import tpu as pltpu
 from jax.sharding import PartitionSpec as P
 
 HEADS = 16
@@ -80,6 +84,64 @@
     return (
         after.astype(jnp.float32) + jnp.dot(hidden, down_w, preferred_element_type=jnp.float32)
     ).astype(jnp.bfloat16)
+
+
+def conv_kernel(block, offs, rows, idx_ref, left_ref, own_ref, right_ref, w_ref, lin_ref, out_ref, tab, buf, lhs):
+    step = pl.program_id(0)
+    lanes = 128
+
+    @pl.when(step == 0)
+    def _():
+        for part, ref in enumerate((left_ref, own_ref, right_ref)):
+            for half in range(2):
+                tab[pl.ds(2 * part * rows + half, rows, stride=2), :] = ref[:, half * lanes:(half + 1) * lanes].astype(jnp.float32)
+        tab[pl.ds(6 * rows, 8), :] = jnp.zeros((8, lanes), jnp.float32)
+
+    start = pl.multiple_of(step * block, block)
+    width = 2 * lanes
+    mid = offs // 2
+    for k, ref in ((0, left_ref), (mid, own_ref), (offs - 1, right_ref)):
+        lhs[:, k * width:(k + 1) * width] = ref[pl.ds(start, block), :]
+
+    def one(o):
+        base = o * block
+        for j in range(block):
+            buf[2 * j:2 * j + 2, :] = tab[pl.ds(pl.multiple_of(idx_ref[0, 0, base + j], 2), 2), :]
+        for half in range(2):
+            lhs[:, pl.ds(pl.multiple_of(o * width + half * lanes, lanes), lanes)] = buf[pl.ds(half, block, stride=2), :].astype(jnp.bfloat16)
+
+    def body(o, carry):
+        one(o)
+        return carry
+    lax.fori_loop(1, mid, body, 0)
+    lax.fori_loop(mid + 1, offs - 1, body, 0)
+    conv = jnp.dot(lhs[...], w_ref[...], preferred_element_type=jnp.float32).astype(jnp.bfloat16)
+    linear = jnp.dot(conv, lin_ref[...], preferred_element_type=jnp.float32)
+    center = jnp.mean(linear, axis=-1, keepdims=True)
+    d = linear - center
+    spread = jnp.mean(d * d, axis=-1, keepdims=True)
+    normed = d * lax.rsqrt(spread + EPS)
+    out_ref[...] = (own_ref[pl.ds(start, block), :].astype(jnp.float32) + normed).astype(jnp.bfloat16)
+
+def position_conv(idx, left, own, right, w, lin, block):
+    rows, ch = own.shape
+    offs = w.shape[0] // ch
+    vm = pl.BlockSpec(memory_space=pltpu.VMEM)
+    return pl.pallas_call(
+        functools.partial(conv_kernel, block, offs, rows),
+        out_shape=jax.ShapeDtypeStruct((rows, ch), jnp.bfloat16),
+        grid=(rows // block,),
+        in_specs=[pl.BlockSpec((1, 1, offs * block), lambda i: (i, 0, 0), memory_space=pltpu.SMEM), vm, vm, vm, vm, vm],
+        out_specs=pl.BlockSpec((block, ch), lambda i: (i, 0)),
+        scratch_shapes=[pltpu.VMEM((6 * rows + 8, 128), jnp.float32), pltpu.VMEM((2 * block, 128), jnp.float32), pltpu.VMEM((block, offs * ch), jnp.bfloat16)],
+        compiler_params=pltpu.CompilerParams(vmem_limit_bytes=56 << 20),
+    )(idx, left, own, right, w, lin)
+
+def gather_rows(near, block):
+    rows, offs = near.shape
+    h = jnp.arange(rows, dtype=jnp.int32)[:, None]
+    idx = 2 * jnp.where(near < 0, 3 * rows, near + h)
+    return idx.reshape(rows // block, block, offs).transpose(0, 2, 1).reshape(rows // block, 1, offs * block)
 
 
 def on_device(
@@ -135,26 +197,13 @@
         .at[target]
         .set(got_rows.reshape(-1, channels), mode="drop")
     )
-    reach_ext = with_halo(serial, ((("curve", "group"), 0),), row_count, False)
-    conv_block = min(512, row_count)
-
-    def conv_piece(block_index):
-        start = block_index * conv_block
-        near = lax.dynamic_slice_in_dim(neighbors, start, conv_block, 0)
-        valid = near >= 0
-        index_rows = (
-            start + jnp.arange(conv_block, dtype=jnp.int32)[:, None] + jnp.where(valid, near, 0)
-        )
-        gathered = jnp.where(valid[..., None], reach_ext[index_rows], jnp.zeros((), jnp.bfloat16))
-        return jnp.dot(
-            gathered.reshape(conv_block, -1), conv_two, preferred_element_type=jnp.float32
-        ).astype(jnp.bfloat16)
-
-    conv = lax.map(conv_piece, jnp.arange(row_count // conv_block, dtype=jnp.int32)).reshape(
-        row_count, channels
-    )
-    linear = jnp.dot(conv, linear_two, preferred_element_type=jnp.float32)
-    return (serial.astype(jnp.float32) + layer_norm(linear)).astype(jnp.bfloat16)
+    axes = ("curve", "group")
+    ups = [(i, i + 1) for i in range(devices - 1)]
+    downs = [(i + 1, i) for i in range(devices - 1)]
+    left = lax.ppermute(serial, axes, ups)
+    right = lax.ppermute(serial, axes, downs)
+    block = min(512, row_count)
+    return position_conv(gather_rows(neighbors, block), left, serial, right, conv_two, linear_two, block)
 
 
 def solution(mesh):

time: 656 us -> 367 us (0.56)
  local copies, waits for them, and re-layouts: 339 us -> 67.9 us
  Pallas kernels: 0 us -> 57.4 us
  other arithmetic: 51 us -> 11.5 us
  matrix products: 138 us -> 107 us
    gather x8 -> x0, local copies, waits for them, and re-layouts: 200 us -> none  [conv_piece(): reach_ext[index_rows]]
    pallas_call x0 -> x1, Pallas kernels: none -> 57.4 us  [position_conv(): pl.pallas_call(functools.partial(conv_kernel, block, offs, rows), out_sha...]
    select_n x4 -> x0, local copies, waits for them, and re-layouts: 54.4 us -> none  [conv_piece(): jnp.where(valid[..., None], reach_ext[index_rows], jnp.zeros((), jnp.bflo...]
    ppermute x0 -> x2, waiting for transfers between devices: none -> 43.5 us  [the longest x1 24.4 us: on_device(): left = lax.ppermute(serial, axes, ups)]
    select_n x8 -> x0, other arithmetic: 35.3 us -> none  [the longest x4 32 us: conv_piece(): jnp.where(valid[..., None], reach_ext[index_rows], jnp.zeros((), jnp.bflo...]
    dot_general x5 -> x0, matrix products: 28.8 us -> none  [the longest x4 27 us: conv_piece(): jnp.dot(gathered.reshape(conv_block, -1), conv_two, preferred_element_typ...]
    ppermute x2 -> x1, waiting for transfers between devices: 23.4 us -> 0.01 us  [with_halo(): lax.ppermute(tail, axis, [(i, (i + 1) % count) for i in range(ends)])]
    ppermute x2 -> x1, waiting for transfers between devices: 19 us -> 0.01 us  [with_halo(): lax.ppermute(head, axis, [((i + 1) % count, i) for i in range(ends)])]
  transfers between devices with their start and end apart: 6 -> 6, of which waited for: 3 -> 3; matrix products, arithmetic and copies ran while one was open for 26% -> 45% of each run, Pallas kernels for 0% -> 0%
where the time goes in v1:
time: 367 us; the launch traced here: 362 us
  matrix products  107 us (29%)
  waiting for transfers between devices  91.1 us (25%)
  local copies, waits for them, and re-layouts  67.9 us (19%)
  Pallas kernels  57.4 us (16%)
  starting transfers between devices  20.8 us (6%)
  other arithmetic  11.5 us (3%)
  loops' own time  5.86 us (2%)
    pallas_call x1, Pallas kernels, position_conv(): pl.pallas_call(functools.partial(conv_kernel, block, offs, rows), out_sha...  57.4 us
    all_to_all x1, waiting for transfers between devices, on_device(): lax.all_to_all(send_rows.reshape(devices, capacity, channels), ('curve',...  47.5 us
    dot_general x8, matrix products, one_block(): jnp.einsum('hqk,khd->qhd', weights, value_group, preferred_element_type=j...  45.5 us
    sub x8, matrix products, one_block(): weights = jax.nn.softmax(scores, axis=-1).astype(jnp.bfloat16)  39.1 us
    ppermute x1, waiting for transfers between devices, on_device(): left = lax.ppermute(serial, axes, ups)  24.4 us
    dot_general x1, matrix products, finish(): jnp.dot(hidden, down_w, preferred_element_type=jnp.float32)  19.7 us
    ppermute x1, waiting for transfers between devices, on_device(): right = lax.ppermute(serial, axes, downs)  19.1 us
    scatter x1, local copies, waits for them, and re-layouts, on_device(): serial = jnp.zeros((row_count, channels), jnp.bfloat16).at[target].set(go...  18.4 us
  transfers between devices with their start and end apart: 6, of which 3 were waited for; matrix products, arithmetic and copies ran while one was open for 45% of the time, Pallas kernels for 0%

profile of v1, /device:TPU:1, one launch (start us, length us, event | category | flops | bytes accessed | tf_op | source)
XLA Modules:
  0.0 362.2 jit_solution(7937985744790522879)
XLA Ops:
  0.0 1.6 copy.20
  1.6 0.2 convert_reduce_fusion.1
  1.8 0.3 fusion.68
  2.1 1.1 convolution_convert_fusion
  3.3 1.6 copy-done.3
  4.9 2.1 collective-permute-start
  7.0 2.6 collective-permute-start.1
  9.6 9.1 %reduce-window.6 = s32[32,16,128]{2,1,0:T(8,128)S(1)} reduce-window(s32[32,16,128]{2,1,0:T(8,128)S(1)} %fusion.85, s32[]{:T(128)} %constant.132.clone.1), window={size=1x1x128 pad=0_0x0_0x127_0}, to_apply=%region_0.0 | reduce-window | flops 8323072 | bytes 524292 | tf_op jit(solution)/shard_map/reduce-window
  18.8 0.2 copy.29
  19.1 0.2 reduce-window.9
  19.5 8.8 %scatter_custom_fusion = s32[4096]{0:T(1024)} fusion(s32[2048]{0:T(1024)S(1)} %compare_select_fusion.2, s32[2048]{0:T(1024)} %param.18, s32[]{:T(128)} %constant.136.clone.1), kind=kCustom, calls=%fused_computation.93 | custom fusion | bytes 16896 | tf_op jit(solution)/shard_map/scatter | solution.py:176
  28.3 4.5 %all-to-all-start = ((s32[32,1,128]{2,1,0:T(1,128)}), s32[32,1,128]{2,1,0:T(1,128)}, u32[]{:S(2)}, u32[]{:S(2)}) async-start(s32[32,1,128]{2,1,0:T(1,128)} %bitcast.18), calls=%async_computation | async-start | bytes 32768 | tf_op jit(solution)/shard_map/all_to_all | solution.py:185
  32.8 2.3 slice.76
  35.1 1.7 slice.73
  36.8 0.3 pad_maximum_fusion
  37.1 1.9 fusion.120
  39.0 108.7 %while.12 = (s32[]{:T(128)}, bf16[4,512,256]{2,1,0:T(8,128)(2,1)}, s32[4]{0:T(128)S(1)}, bf16[3072,256]{1,0:T(8,128)(2,1)}, bf16[2048,256]{1,0:T(8,128)(2,1)}, /...) while((s32[]{:T(128)}, bf16[4,512,256]{2,1,0:T(8,128)(2,1)}, ...), condition=%wide.region_11.12_spmd, body=%wide.region_6.11_spmd.sunk | while | flops 864694272 | bytes 9241023 | solution.py:72
  39.1 0.6 dynamic_slice.26
  41.0 1.0 constant_dynamic-slice_fusion.6
  42.2 1.3 constant_dynamic-slice_fusion.5
  43.8 4.9 %fusion.173 = f32[8,512]{1,0:T(8,128)S(1)} fusion(bf16[512,8,16]{0,2,1:T(8,128)(2,1)S(1)} %bitcast.122, bf16[1024,8,16]{0,2,1:T(8,128)(2,1)S(1)} %bitcast.116), kind=kOutput, calls=%fused_computation.127.clone.1 | convolution fusion | flops 146801664 | bytes 409600 | tf_op jit(solution)/shard_map/while/body/eval_jaxpr/sub | solution.py:65
  48.7 5.7 %fusion.174 = bf16[8,16,512]{2,1,0:T(8,128)(2,1)S(1)} fusion(bf16[1024,8,16]{0,2,1:T(8,128)(2,1)S(1)} %bitcast.114, f32[8,512]{1,0:T(8,128)S(1)} %fusion.173, bf16[512,8,16]{0,2,1:T(8,128)(2,1)S(1)} %bitcast.123, bf16[1024,8,16]{0,2,1:T(8,128)(2,1)S(1)} %bitcast.117), kind=kOutput, calls=%fused_computation.19.clone.1 | convolution fusion | flops 285283328 | bytes 802816 | tf_op jit(solution)/shard_map/while/body/eval_jaxpr/hqk,khd->qhd/dot_general | solution.py:66
  54.7 4.9 %fusion.175 = f32[8,512]{1,0:T(8,128)S(1)} fusion(bf16[512,8,16]{0,2,1:T(8,128)(2,1)S(1)} %bitcast.120, bf16[1024,8,16]{0,2,1:T(8,128)(2,1)S(1)} %bitcast.118), kind=kOutput, calls=%fused_computation.128.clone.1 | convolution fusion | flops 146801664 | bytes 409600 | tf_op jit(solution)/shard_map/while/body/eval_jaxpr/sub | solution.py:65
  59.6 5.7 %fusion.176 = bf16[8,16,512]{2,1,0:T(8,128)(2,1)S(1)} fusion(bf16[1024,8,16]{0,2,1:T(8,128)(2,1)S(1)} %bitcast.115, f32[8,512]{1,0:T(8,128)S(1)} %fusion.175, bf16[512,8,16]{0,2,1:T(8,128)(2,1)S(1)} %bitcast.121, bf16[1024,8,16]{0,2,1:T(8,128)(2,1)S(1)} %bitcast.119), kind=kOutput, calls=%fused_computation.20.clone.1 | convolution fusion | flops 285283328 | bytes 802816 | tf_op jit(solution)/shard_map/while/body/eval_jaxpr/hqk,khd->qhd/dot_general | solution.py:66
  65.4 0.7 constant_dynamic-update-slice_fusion.2
  66.2 0.6 dynamic_slice.26
  68.0 1.0 constant_dynamic-slice_fusion.6
  69.3 1.3 constant_dynamic-slice_fusion.5
  70.8 4.9 %fusion.173 = f32[8,512]{1,0:T(8,128)S(1)} fusion(bf16[512,8,16]{0,2,1:T(8,128)(2,1)S(1)} %bitcast.122, bf16[1024,8,16]{0,2,1:T(8,128)(2,1)S(1)} %bitcast.116), kind=kOutput, calls=%fused_computation.127.clone.1 | convolution fusion | flops 146801664 | bytes 409600 | tf_op jit(solution)/shard_map/while/body/eval_jaxpr/sub | solution.py:65
  75.7 5.7 %fusion.174 = bf16[8,16,512]{2,1,0:T(8,128)(2,1)S(1)} fusion(bf16[1024,8,16]{0,2,1:T(8,128)(2,1)S(1)} %bitcast.114, f32[8,512]{1,0:T(8,128)S(1)} %fusion.173, bf16[512,8,16]{0,2,1:T(8,128)(2,1)S(1)} %bitcast.123, bf16[1024,8,16]{0,2,1:T(8,128)(2,1)S(1)} %bitcast.117), kind=kOutput, calls=%fused_computation.19.clone.1 | convolution fusion | flops 285283328 | bytes 802816 | tf_op jit(solution)/shard_map/while/body/eval_jaxpr/hqk,khd->qhd/dot_general | solution.py:66
  81.7 4.9 %fusion.175 = f32[8,512]{1,0:T(8,128)S(1)} fusion(bf16[512,8,16]{0,2,1:T(8,128)(2,1)S(1)} %bitcast.120, bf16[1024,8,16]{0,2,1:T(8,128)(2,1)S(1)} %bitcast.118), kind=kOutput, calls=%fused_computation.128.clone.1 | convolution fusion | flops 146801664 | bytes 409600 | tf_op jit(solution)/shard_map/while/body/eval_jaxpr/sub | solution.py:65
  86.6 5.7 %fusion.176 = bf16[8,16,512]{2,1,0:T(8,128)(2,1)S(1)} fusion(bf16[1024,8,16]{0,2,1:T(8,128)(2,1)S(1)} %bitcast.115, f32[8,512]{1,0:T(8,128)S(1)} %fusion.175, bf16[512,8,16]{0,2,1:T(8,128)(2,1)S(1)} %bitcast.121, bf16[1024,8,16]{0,2,1:T(8,128)(2,1)S(1)} %bitcast.119), kind=kOutput, calls=%fused_computation.20.clone.1 | convolution fusion | flops 285283328 | bytes 802816 | tf_op jit(solution)/shard_map/while/body/eval_jaxpr/hqk,khd->qhd/dot_general | solution.py:66
  92.5 0.7 constant_dynamic-update-slice_fusion.2
  93.2 0.6 dynamic_slice.26
  95.1 1.0 constant_dynamic-slice_fusion.6
  96.3 1.3 constant_dynamic-slice_fusion.5
  97.9 4.9 %fusion.173 = f32[8,512]{1,0:T(8,128)S(1)} fusion(bf16[512,8,16]{0,2,1:T(8,128)(2,1)S(1)} %bitcast.122, bf16[1024,8,16]{0,2,1:T(8,128)(2,1)S(1)} %bitcast.116), kind=kOutput, calls=%fused_computation.127.clone.1 | convolution fusion | flops 146801664 | bytes 409600 | tf_op jit(solution)/shard_map/while/body/eval_jaxpr/sub | solution.py:65
  102.8 5.7 %fusion.174 = bf16[8,16,512]{2,1,0:T(8,128)(2,1)S(1)} fusion(bf16[1024,8,16]{0,2,1:T(8,128)(2,1)S(1)} %bitcast.114, f32[8,512]{1,0:T(8,128)S(1)} %fusion.173, bf16[512,8,16]{0,2,1:T(8,128)(2,1)S(1)} %bitcast.123, bf16[1024,8,16]{0,2,1:T(8,128)(2,1)S(1)} %bitcast.117), kind=kOutput, calls=%fused_computation.19.clone.1 | convolution fusion | flops 285283328 | bytes 802816 | tf_op jit(solution)/shard_map/while/body/eval_jaxpr/hqk,khd->qhd/dot_general | solution.py:66
  108.8 4.9 %fusion.175 = f32[8,512]{1,0:T(8,128)S(1)} fusion(bf16[512,8,16]{0,2,1:T(8,128)(2,1)S(1)} %bitcast.120, bf16[1024,8,16]{0,2,1:T(8,128)(2,1)S(1)} %bitcast.118), kind=kOutput, calls=%fused_computation.128.clone.1 | convolution fusion | flops 146801664 | bytes 409600 | tf_op jit(solution)/shard_map/while/body/eval_jaxpr/sub | solution.py:65
  113.7 5.7 %fusion.176 = bf16[8,16,512]{2,1,0:T(8,128)(2,1)S(1)} fusion(bf16[1024,8,16]{0,2,1:T(8,128)(2,1)S(1)} %bitcast.115, f32[8,512]{1,0:T(8,128)S(1)} %fusion.175, bf16[512,8,16]{0,2,1:T(8,128)(2,1)S(1)} %bitcast.121, bf16[1024,8,16]{0,2,1:T(8,128)(2,1)S(1)} %bitcast.119), kind=kOutput, calls=%fused_computation.20.clone.1 | convolution fusion | flops 285283328 | bytes 802816 | tf_op jit(solution)/shard_map/while/body/eval_jaxpr/hqk,khd->qhd/dot_general | solution.py:66
  119.5 0.7 constant_dynamic-update-slice_fusion.2
  120.2 0.6 dynamic_slice.26
  122.1 1.0 constant_dynamic-slice_fusion.6
  123.3 1.3 constant_dynamic-slice_fusion.5
  124.9 4.9 %fusion.173 = f32[8,512]{1,0:T(8,128)S(1)} fusion(bf16[512,8,16]{0,2,1:T(8,128)(2,1)S(1)} %bitcast.122, bf16[1024,8,16]{0,2,1:T(8,128)(2,1)S(1)} %bitcast.116), kind=kOutput, calls=%fused_computation.127.clone.1 | convolution fusion | flops 146801664 | bytes 409600 | tf_op jit(solution)/shard_map/while/body/eval_jaxpr/sub | solution.py:65
  129.8 5.7 %fusion.174 = bf16[8,16,512]{2,1,0:T(8,128)(2,1)S(1)} fusion(bf16[1024,8,16]{0,2,1:T(8,128)(2,1)S(1)} %bitcast.114, f32[8,512]{1,0:T(8,128)S(1)} %fusion.173, bf16[512,8,16]{0,2,1:T(8,128)(2,1)S(1)} %bitcast.123, bf16[1024,8,16]{0,2,1:T(8,128)(2,1)S(1)} %bitcast.117), kind=kOutput, calls=%fused_computation.19.clone.1 | convolution fusion | flops 285283328 | bytes 802816 | tf_op jit(solution)/shard_map/while/body/eval_jaxpr/hqk,khd->qhd/dot_general | solution.py:66
  135.8 4.9 %fusion.175 = f32[8,512]{1,0:T(8,128)S(1)} fusion(bf16[512,8,16]{0,2,1:T(8,128)(2,1)S(1)} %bitcast.120, bf16[1024,8,16]{0,2,1:T(8,128)(2,1)S(1)} %bitcast.118), kind=kOutput, calls=%fused_computation.128.clone.1 | convolution fusion | flops 146801664 | bytes 409600 | tf_op jit(solution)/shard_map/while/body/eval_jaxpr/sub | solution.py:65
  140.7 5.7 %fusion.176 = bf16[8,16,512]{2,1,0:T(8,128)(2,1)S(1)} fusion(bf16[1024,8,16]{0,2,1:T(8,128)(2,1)S(1)} %bitcast.115, f32[8,512]{1,0:T(8,128)S(1)} %fusion.175, bf16[512,8,16]{0,2,1:T(8,128)(2,1)S(1)} %bitcast.121, bf16[1024,8,16]{0,2,1:T(8,128)(2,1)S(1)} %bitcast.119), kind=kOutput, calls=%fused_computation.20.clone.1 | convolution fusion | flops 285283328 | bytes 802816 | tf_op jit(solution)/shard_map/while/body/eval_jaxpr/hqk,khd->qhd/dot_general | solution.py:66
  146.6 0.7 constant_dynamic-update-slice_fusion.2
  147.7 1.8 convert_reduce_fusion
  149.5 0.3 fusion.66
  149.8 19.7 %fusion.59 = bf16[2048,256]{0,1:T(8,128)(2,1)S(1)} fusion(bf16[1024,256]{1,0:T(8,128)(2,1)S(1)} %copy-done, bf16[256,1024]{1,0:T(8,128)(2,1)S(1)} %copy-done.10, bf16[2048,256]{0,1:T(8,128)(2,1)S(1)} %get-tuple-element.121, f32[2048]{0:T(1024)S(1)} %add_rsqrt_fusion, f32[2048]{0:T(1024)S(1)} %broadcast_multiply_fusion), kind=kOutput, calls=%fused_computation.62 | convolution fusion | flops 2287468544 | bytes 3162112 | tf_op jit(solution)/shard_map/dot_general | solution.py:85
  169.6 0.5 copy.26
  170.1 11.2 %scatter_custom_fusion.1 = bf16[4096,256]{1,0:T(8,128)(2,1)} fusion(s32[2048]{0:T(1024)} %copy-done.9, bf16[2048,256]{1,0:T(8,128)(2,1)S(1)} %copy.26, bf16[]{:T(256)} %constant.135.clone.1), kind=kCustom, calls=%fused_computation.75 | custom fusion | bytes 2097664 | tf_op jit(solution)/shard_map/scatter | solution.py:175
  181.4 6.0 %all-to-all-start.1 = ((bf16[32,128,256]{2,1,0:T(8,128)(2,1)}), bf16[32,128,256]{2,1,0:T(8,128)(2,1)}, u32[]{:S(2)}, u32[]{:S(2)}) async-start(bf16[32,128,256]{2,1,0:T(8,128)(2,1)} %bitcast.113), calls=%async_computation.1 | async-start | bytes 4194304 | tf_op jit(solution)/shard_map/all_to_all | solution.py:178
  187.4 0.7 compare_select_fusion
  188.2 47.5 %all-to-all-done.1 = bf16[32,128,256]{2,1,0:T(8,128)(2,1)} async-done(((bf16[32,128,256]{2,1,0:T(8,128)(2,1)}), bf16[32,128,256]{2,1,0:T(8,128)(2,1)}, u32[]{:S(2)}, u32[]{:S(2)}) %all-to-all-start.1) | async-done | bytes 2097184 | tf_op jit(solution)/shard_map/all_to_all | solution.py:178
  235.7 18.4 %scatter_custom_fusion.2.own_ref = bf16[2048,256]{1,0:T(8,128)(2,1)S(1)} fusion(s32[4096]{0:T(1024)S(1)} %bitcast.132, bf16[4096,256]{1,0:T(8,128)(2,1)} %bitcast.23, bf16[]{:T(256)} %constant.135.clone.1), kind=kCustom, calls=%fused_computation.77 | custom fusion | bytes 1049088 | tf_op jit(solution)/shard_map/scatter | solution.py:198
  254.2 3.7 %collective-permute-start.3 = (bf16[2048,256]{1,0:T(8,128)(2,1)S(1)}, bf16[2048,256]{1,0:T(8,128)(2,1)S(1)}, u32[]{:S(2)}, u32[]{:S(2)}) collective-permute-start(bf16[2048,256]{1,0:T(8,128)(2,1)S(1)} %scatter_custom_fusion.2.own_ref), channel_id=1, source_target_pairs={{1,0},{2,1},{3,2},{4,3},{5,4},{6,5},{7,6},{8,7},{9,8},{10,9},{11,1... | collective-permute-start | bytes 3145736 | tf_op jit(solution)/shard_map/ppermute | solution.py:204
  257.8 1.9 collective-permute-start.2
  260.1 1.0 reshape.180.idx_ref
  261.0 19.1 %collective-permute-done.3.right_ref = bf16[2048,256]{1,0:T(8,128)(2,1)S(1)} collective-permute-done((bf16[2048,256]{1,0:T(8,128)(2,1)S(1)}, bf16[2048,256]{1,0:T(8,128)(2,1)S(1)}, u32[]{:S(2)}, u32[]{:S(2)}) %collective-permute-start.3) | collective-permute-done | bytes 1048608 | tf_op jit(solution)/shard_map/ppermute | solution.py:204
  280.2 24.4 %collective-permute-done.2.left_ref = bf16[2048,256]{1,0:T(8,128)(2,1)} collective-permute-done((bf16[2048,256]{1,0:T(8,128)(2,1)S(1)}, bf16[2048,256]{1,0:T(8,128)(2,1)}, u32[]{:S(2)}, u32[]{:S(2)}) %collective-permute-start.2) | collective-permute-done | bytes 1048608 | tf_op jit(solution)/shard_map/ppermute | solution.py:203
  304.6 57.4 %shard_map.100 = bf16[2048,256]{1,0:T(8,128)(2,1)} custom-call(s32[4,1,13824]{2,1,0:T(1,128)} %reshape.180.idx_ref, bf16[2048,256]{1,0:T(8,128)(2,1)} %collective-permute-done.2.left_ref, bf16[2048,256]{1,0:T(8,128)(2,1)} %copy-done.4, bf16[2048,256]{1,0:T(8,128)(2,1)} %copy-done.5, bf16[6912,256]{1,0:T(8,128)(2,1)} %w_ref.1, bf16[256,256]{1,0:T(8,128)(2,1)} %lin_ref.1), custom_call_target="tpu_custom_call" | custom-call | tf_op jit(solution)/shard_map/pallas_call | solution.py:130
  (73 shorter events, 4.7 us)
Async XLA Ops:
  0.0 149.8 %copy-start = (bf16[1024,256]{1,0:T(8,128)(2,1)S(1)}, bf16[1024,256]{1,0:T(8,128)(2,1)}, u32[]{:S(2)}) copy-start(bf16[1024,256]{1,0:T(8,128)(2,1)} %param.16) | copy-start | bytes 1572868
  0.0 2.1 copy-start.11
  1.6 1.6 copy-start.1
  2.1 7.5 %copy-start.8 = (s32[2048]{0:T(1024)S(1)}, s32[2048]{0:T(1024)}, u32[]{:S(2)}) copy-start(s32[2048]{0:T(1024)} %param.17) | copy-start | bytes 24580
  3.2 1.7 copy-start.3
  4.9 31.9 %collective-permute-start = (bf16[512,512]{1,0:T(8,128)(2,1)S(1)}, bf16[512,512]{1,0:T(8,128)(2,1)S(1)}, u32[]{:S(2)}, u32[]{:S(2)}) collective-permute-start(bf16[512,512]{1,0:T(8,128)(2,1)S(1)} %get-tuple-element.118), channel_id=1, source_target_pairs={{0,1},{1,2},{2,3},{3,4},{4,5},{5,6},{6,7},{7,8},{8,9},{9,10},{10,1... | collective-permute-start | bytes 1572872 | tf_op jit(solution)/shard_map/ppermute | solution.py:26
  7.0 29.8 %collective-permute-start.1 = (bf16[512,512]{1,0:T(8,128)(2,1)S(1)}, bf16[512,512]{1,0:T(8,128)(2,1)S(1)}, u32[]{:S(2)}, u32[]{:S(2)}) collective-permute-start(bf16[512,512]{1,0:T(8,128)(2,1)S(1)} %get-tuple-element.119), channel_id=1, source_target_pairs={{1,0},{2,1},{3,2},{4,3},{5,4},{6,5},{7,6},{8,7},{9,8},{10,9},{11,1... | collective-permute-start | bytes 1572872 | tf_op jit(solution)/shard_map/ppermute | solution.py:28
  19.5 17.6 %copy-start.9 = (s32[2048]{0:T(1024)}, s32[2048]{0:T(1024)S(1)}, u32[]{:S(2)}) copy-start(s32[2048]{0:T(1024)S(1)} %compare_select_fusion.2) | copy-start | bytes 24580
  28.3 153.0 %all-to-all-start = ((s32[32,1,128]{2,1,0:T(1,128)}), s32[32,1,128]{2,1,0:T(1,128)}, u32[]{:S(2)}, u32[]{:S(2)}) async-start(s32[32,1,128]{2,1,0:T(1,128)} %bitcast.18), calls=%async_computation | async-start | bytes 32768 | tf_op jit(solution)/shard_map/all_to_all | solution.py:185
  39.0 108.7 %copy-start.2 = (bf16[2048,256]{0,1:T(8,128)(2,1)S(1)}, bf16[2048,256]{0,1:T(8,128)(2,1)}, u32[]{:S(2)}) copy-start(bf16[2048,256]{0,1:T(8,128)(2,1)} %copy-done.1) | copy-start | bytes 3145732
  39.0 108.7 %copy-start.7 = (bf16[256,256]{1,0:T(8,128)(2,1)S(1)}, bf16[256,256]{1,0:T(8,128)(2,1)}, u32[]{:S(2)}) copy-start(bf16[256,256]{1,0:T(8,128)(2,1)} %param.14) | copy-start | bytes 393220
  147.7 2.2 copy-start.10
  170.1 89.7 %copy-start.6 = (s32[2048,27]{0,1:T(8,128)S(1)}, s32[2048,27]{0,1:T(8,128)}, u32[]{:S(2)}) copy-start(s32[2048,27]{0,1:T(8,128)} %param.19) | copy-start | bytes 663556
  181.4 54.4 %all-to-all-start.1 = ((bf16[32,128,256]{2,1,0:T(8,128)(2,1)}), bf16[32,128,256]{2,1,0:T(8,128)(2,1)}, u32[]{:S(2)}, u32[]{:S(2)}) async-start(bf16[32,128,256]{2,1,0:T(8,128)(2,1)} %bitcast.113), calls=%async_computation.1 | async-start | bytes 4194304 | tf_op jit(solution)/shard_map/all_to_all | solution.py:178
  254.2 50.4 %copy-start.4 = (bf16[2048,256]{1,0:T(8,128)(2,1)}, bf16[2048,256]{1,0:T(8,128)(2,1)S(1)}, u32[]{:S(2)}) copy-start(bf16[2048,256]{1,0:T(8,128)(2,1)S(1)} %scatter_custom_fusion.2.own_ref) | copy-start | bytes 3145732
  254.2 26.0 %collective-permute-start.3 = (bf16[2048,256]{1,0:T(8,128)(2,1)S(1)}, bf16[2048,256]{1,0:T(8,128)(2,1)S(1)}, u32[]{:S(2)}, u32[]{:S(2)}) collective-permute-start(bf16[2048,256]{1,0:T(8,128)(2,1)S(1)} %scatter_custom_fusion.2.own_ref), channel_id=1, source_target_pairs={{1,0},{2,1},{3,2},{4,3},{5,4},{6,5},{7,6},{8,7},{9,8},{10,9},{11,1... | collective-permute-start | bytes 3145736 | tf_op jit(solution)/shard_map/ppermute | solution.py:204
  257.8 46.7 %collective-permute-start.2 = (bf16[2048,256]{1,0:T(8,128)(2,1)S(1)}, bf16[2048,256]{1,0:T(8,128)(2,1)}, u32[]{:S(2)}, u32[]{:S(2)}) collective-permute-start(bf16[2048,256]{1,0:T(8,128)(2,1)S(1)} %scatter_custom_fusion.2.own_ref), channel_id=1, source_target_pairs={{0,1},{1,2},{2,3},{3,4},{4,5},{5,6},{6,7},{7,8},{8,9},{9,10},{10,1... | collective-permute-start | bytes 3145736 | tf_op jit(solution)/shard_map/ppermute | solution.py:203
  280.2 24.4 %copy-start.5 = (bf16[2048,256]{1,0:T(8,128)(2,1)}, bf16[2048,256]{1,0:T(8,128)(2,1)S(1)}, u32[]{:S(2)}) copy-start(bf16[2048,256]{1,0:T(8,128)(2,1)S(1)} %collective-permute-done.3.right_ref) | copy-start | bytes 3145732

commit v2 on v1

v2 whole, which is shorter than its diff:
```python
import functools

import jax
import jax.numpy as jnp
from jax import lax
from jax.experimental import pallas as pl
from jax.experimental.pallas import tpu as pltpu
from jax.sharding import PartitionSpec as P

HEADS = 16
HEAD_DIM = 16
PATCH = 1024
LANES = 128
EPS = 1e-05
LOG2E = 1.4426950408889634
AXES = ("curve", "group")


def layer_norm(values):
    values = values.astype(jnp.float32)
    center = jnp.mean(values, axis=-1, keepdims=True)
    offset = values - center
    spread = jnp.mean(offset * offset, axis=-1, keepdims=True)
    return offset * lax.rsqrt(spread + EPS)


def dot(left, right):
    return jnp.dot(left, right, preferred_element_type=jnp.float32)


def gelu(values):
    return 0.5 * values * (1.0 + lax.erf(values * 0.7071067811865476))


def slots_kernel(devices, capacity, device_ref, position_ref, index_ref, place_ref):
    rows = device_ref.shape[1]
    chunk = min(256, rows)
    row_id = lax.broadcasted_iota(jnp.int32, (chunk, chunk), 0)
    col_id = lax.broadcasted_iota(jnp.int32, (chunk, chunk), 1)
    before = (row_id <= col_id).astype(jnp.float32).astype(jnp.bfloat16)
    device_id = lax.broadcasted_iota(jnp.int32, (devices, chunk), 0)
    slot_id = lax.broadcasted_iota(jnp.int32, (capacity, chunk), 0)
    carry = jnp.zeros((devices, 1), jnp.float32)
    place = jnp.zeros((2 * devices, capacity), jnp.float32)
    for part in range(rows // chunk):
        span = slice(part * chunk, (part + 1) * chunk)
        target = device_ref[:, span]
        mine = (device_id == target).astype(jnp.float32)
        running = dot(mine.astype(jnp.bfloat16), before) + carry
        carry = running[:, chunk - 1 : chunk]
        slot = (jnp.sum(mine * running, axis=0, keepdims=True) - 1.0).astype(jnp.int32)
        index_ref[:, span] = 2 * (target * capacity + slot)
        code = position_ref[:, span] + 1
        high = mine * (code // LANES).astype(jnp.float32)
        low = mine * (code % LANES).astype(jnp.float32)
        here = (slot_id == slot).astype(jnp.float32).astype(jnp.bfloat16)
        place += lax.dot_general(
            jnp.concatenate([high, low], axis=0).astype(jnp.bfloat16),
            here,
            (((1,), (1,)), ((), ())),
            preferred_element_type=jnp.float32,
        )
    place_ref[...] = 2 * (place[:devices] * float(LANES) + place[devices:]).astype(jnp.int32)


def find_slots(device, position, devices, capacity):
    rows = device.shape[0]
    return pl.pallas_call(
        functools.partial(slots_kernel, devices, capacity),
        out_shape=(
            jax.ShapeDtypeStruct((1, rows), jnp.int32),
            jax.ShapeDtypeStruct((devices, capacity), jnp.int32),
        ),
        name="find_slots",
    )(device.reshape(1, rows), position.reshape(1, rows))


def block_kernel(
    index_ref,
    left_ref,
    own_ref,
    right_ref,
    qkv_ref,
    proj_ref,
    up_ref,
    down_ref,
    send_ref,
    query,
    key,
    value,
    pairs,
    table,
):
    step = pl.program_id(0)
    rows, channels = own_ref.shape
    half = PATCH // 2

    @pl.when(step == 0)
    def _():
        count = rows // half
        for part in range(count + 2):
            if part == 0:
                source = left_ref[...]
            elif part == count + 1:
                source = right_ref[...]
            else:
                source = own_ref[(part - 1) * half : part * half, :]
            normed = layer_norm(source).astype(jnp.bfloat16)
            span = slice(part * half, (part + 1) * half)
            key[:, span] = lax.dot_general(
                qkv_ref[:, channels : 2 * channels],
                normed,
                (((0,), (1,)), ((), ())),
                preferred_element_type=jnp.float32,
            ).astype(jnp.bfloat16)
            value[span, :] = dot(normed, qkv_ref[:, 2 * channels :]).astype(jnp.bfloat16)
            if 0 < part <= count:
                query[(part - 1) * half : part * half, :] = dot(normed, qkv_ref[:, :channels]).astype(jnp.bfloat16)

    first = pl.multiple_of(step * half, half)
    start = pl.multiple_of(PATCH * ((step + 1) // 2), PATCH)
    per_group = LANES // HEAD_DIM
    head_of = lax.broadcasted_iota(jnp.int32, (1, LANES), 1) // HEAD_DIM
    scale = HEAD_DIM ** (-0.5) * LOG2E
    pieces = []
    for group in range(channels // LANES):
        lanes = slice(group * LANES, (group + 1) * LANES)
        queries = query[pl.ds(first, half), lanes]
        keys = key[lanes, pl.ds(start, PATCH)]
        values = value[pl.ds(start, PATCH), lanes]
        total = None
        for head in range(per_group):
            mine = head_of == head
            scores = dot(jnp.where(mine, queries, jnp.zeros_like(queries)), keys)
            peak = jnp.max(scores, axis=1, keepdims=True)
            weights = jnp.exp2((scores - peak) * scale).astype(jnp.bfloat16)
            ones = jnp.broadcast_to(mine.astype(jnp.float32).astype(jnp.bfloat16), values.shape)
            both = jnp.concatenate([jnp.where(mine, values, jnp.zeros_like(values)), ones], axis=1)
            result = dot(weights, both)
            total = result if total is None else total + result
        pieces.append((total[:, :LANES] / total[:, LANES:]).astype(jnp.bfloat16))
    mixed = jnp.concatenate(pieces, axis=1)
    after = (own_ref[pl.ds(first, half), :].astype(jnp.float32) + dot(mixed, proj_ref[...])).astype(jnp.bfloat16)
    normed = layer_norm(after).astype(jnp.bfloat16)
    hidden = gelu(dot(normed, up_ref[...])).astype(jnp.bfloat16)
    out = (after.astype(jnp.float32) + dot(hidden, down_ref[...])).astype(jnp.bfloat16).astype(jnp.float32)
    pairs[pl.ds(0, half, stride=2), :] = out[:, :LANES]
    pairs[pl.ds(1, half, stride=2), :] = out[:, LANES:]
    for row in range(half):
        slot = pl.multiple_of(index_ref[0, first + row], 2)
        table[pl.ds(slot, 2), :] = pairs[2 * row : 2 * row + 2, :]

    @pl.when(step == pl.num_programs(0) - 1)
    def _():
        slots = send_ref.shape[0]
        for side in range(2):
            send_ref[:, side * LANES : (side + 1) * LANES] = table[pl.ds(side, slots, stride=2), :].astype(jnp.bfloat16)


def block_one(index, left, own, right, qkv, proj, up, down, slots):
    rows, channels = own.shape
    half = PATCH // 2
    vmem = pl.BlockSpec(memory_space=pltpu.VMEM)
    return pl.pallas_call(
        block_kernel,
        out_shape=jax.ShapeDtypeStruct((slots, channels), jnp.bfloat16),
        grid=(rows // half,),
        in_specs=[pl.BlockSpec(memory_space=pltpu.SMEM)] + [vmem] * 7,
        out_specs=vmem,
        scratch_shapes=[
            pltpu.VMEM((rows, channels), jnp.bfloat16),
            pltpu.VMEM((channels, rows + PATCH), jnp.bfloat16),
            pltpu.VMEM((rows + PATCH, channels), jnp.bfloat16),
            pltpu.VMEM((2 * half, LANES), jnp.float32),
            pltpu.VMEM((2 * slots, LANES), jnp.float32),
        ],
        compiler_params=pltpu.CompilerParams(vmem_limit_bytes=56 << 20),
        name="block_one",
    )(index, left, own, right, qkv, proj, up, down)


def settle_kernel(place_ref, got_ref, serial_ref, pairs, table):
    slots = got_ref.shape[0]
    rows = serial_ref.shape[0]
    capacity = place_ref.shape[1]
    for side in range(2):
        pairs[pl.ds(side, slots, stride=2), :] = got_ref[:, side * LANES : (side + 1) * LANES].astype(jnp.float32)

    def body(source, carry):
        base = pl.multiple_of(source * (2 * capacity), 2 * capacity)
        for slot in range(capacity):
            target = pl.multiple_of(place_ref[source, slot] + 6, 2)
            table[pl.ds(target, 2), :] = pairs[pl.ds(base + 2 * slot, 2), :]
        return carry

    lax.fori_loop(0, place_ref.shape[0], body, 0)
    for side in range(2):
        serial_ref[:, side * LANES : (side + 1) * LANES] = table[pl.ds(8 + side, rows, stride=2), :].astype(
            jnp.bfloat16
        )


def settle(place, got, rows):
    slots, channels = got.shape
    vmem = pl.BlockSpec(memory_space=pltpu.VMEM)
    return pl.pallas_call(
        settle_kernel,
        out_shape=jax.ShapeDtypeStruct((rows, channels), jnp.bfloat16),
        in_specs=[pl.BlockSpec(memory_space=pltpu.SMEM), vmem],
        out_specs=vmem,
        scratch_shapes=[pltpu.VMEM((2 * slots, LANES), jnp.float32), pltpu.VMEM((2 * rows + 8, LANES), jnp.float32)],
        compiler_params=pltpu.CompilerParams(vmem_limit_bytes=56 << 20),
        name="settle",
    )(place, got)


def conv_kernel(block, offs, rows, idx_ref, left_ref, own_ref, right_ref, w_ref, lin_ref, out_ref, tab, buf, lhs):
    step = pl.program_id(0)
    lanes = LANES

    @pl.when(step == 0)
    def _():
        for part, ref in enumerate((left_ref, own_ref, right_ref)):
            for half in range(2):
                tab[pl.ds(2 * part * rows + half, rows, stride=2), :] = ref[:, half * lanes:(half + 1) * lanes].astype(jnp.float32)
        tab[pl.ds(6 * rows, 8), :] = jnp.zeros((8, lanes), jnp.float32)

    start = pl.multiple_of(step * block, block)
    width = 2 * lanes
    mid = offs // 2
    for k, ref in ((0, left_ref), (mid, own_ref), (offs - 1, right_ref)):
        lhs[:, k * width:(k + 1) * width] = ref[pl.ds(start, block), :]

    def one(o):
        base = o * block
        for j in range(block):
            buf[2 * j:2 * j + 2, :] = tab[pl.ds(pl.multiple_of(idx_ref[0, 0, base + j], 2), 2), :]
        for half in range(2):
            lhs[:, pl.ds(pl.multiple_of(o * width + half * lanes, lanes), lanes)] = buf[pl.ds(half, block, stride=2), :].astype(jnp.bfloat16)

    def body(o, carry):
        one(o)
        return carry
    lax.fori_loop(1, mid, body, 0)
    lax.fori_loop(mid + 1, offs - 1, body, 0)
    conv = jnp.dot(lhs[...], w_ref[...], preferred_element_type=jnp.float32).astype(jnp.bfloat16)
    linear = jnp.dot(conv, lin_ref[...], preferred_element_type=jnp.float32)
    out_ref[...] = (own_ref[pl.ds(start, block), :].astype(jnp.float32) + layer_norm(linear)).astype(jnp.bfloat16)

def position_conv(idx, left, own, right, w, lin, block):
    rows, ch = own.shape
    offs = w.shape[0] // ch
    vm = pl.BlockSpec(memory_space=pltpu.VMEM)
    return pl.pallas_call(
        functools.partial(conv_kernel, block, offs, rows),
        out_shape=jax.ShapeDtypeStruct((rows, ch), jnp.bfloat16),
        grid=(rows // block,),
        in_specs=[pl.BlockSpec((1, 1, offs * block), lambda i: (i, 0, 0), memory_space=pltpu.SMEM), vm, vm, vm, vm, vm],
        out_specs=pl.BlockSpec((block, ch), lambda i: (i, 0)),
        scratch_shapes=[pltpu.VMEM((6 * rows + 8, LANES), jnp.float32), pltpu.VMEM((2 * block, LANES), jnp.float32), pltpu.VMEM((block, offs * ch), jnp.bfloat16)],
        compiler_params=pltpu.CompilerParams(vmem_limit_bytes=56 << 20),
    )(idx, left, own, right, w, lin)

def gather_rows(near, block):
    rows, offs = near.shape
    h = jnp.arange(rows, dtype=jnp.int32)[:, None]
    idx = 2 * jnp.where(near < 0, 3 * rows, near + h)
    return idx.reshape(rows // block, block, offs).transpose(0, 2, 1).reshape(rows // block, 1, offs * block)


def on_device(
    points,
    qkv_one,
    proj_one,
    up_one,
    down_one,
    hilbert_device,
    hilbert_position,
    neighbors,
    conv_two,
    linear_two,
):
    row_count, channels = points.shape
    half = PATCH // 2
    devices = lax.axis_size(AXES)
    capacity = 2 * row_count // devices
    ring_up = [(i, (i + 1) % devices) for i in range(devices)]
    ring_down = [((i + 1) % devices, i) for i in range(devices)]
    before = lax.ppermute(points[row_count - half :], AXES, ring_up)
    behind = lax.ppermute(points[:half], AXES, ring_down)
    index, place = find_slots(hilbert_device, hilbert_position, devices, capacity)
    got_place = lax.all_to_all(place, AXES, split_axis=0, concat_axis=0, tiled=True)
    send = block_one(index, before, points, behind, qkv_one, proj_one, up_one, down_one, devices * capacity)
    got = lax.all_to_all(
        send.reshape(devices, capacity, channels), AXES, split_axis=0, concat_axis=0, tiled=True
    )
    serial = settle(got_place, got.reshape(devices * capacity, channels), row_count)
    left = lax.ppermute(serial, AXES, ring_up[:-1])
    right = lax.ppermute(serial, AXES, ring_down[:-1])
    block = min(512, row_count)
    return position_conv(gather_rows(neighbors, block), left, serial, right, conv_two, linear_two, block)


def solution(mesh):
    split = P(AXES)
    rows = P(AXES, None)
    return jax.shard_map(
        on_device,
        mesh=mesh,
        in_specs=(rows, P(), P(), P(), P(), split, split, rows, P(), P()),
        out_specs=rows,
        check_vma=False,
    )
```

time: 367 us -> 242 us (0.66); the launches traced: 362 us -> 242 us
  matrix products: 107 us -> 0 us
  local copies, waits for them, and re-layouts: 67.9 us -> 3.9 us
  Pallas kernels: 57.4 us -> 120 us
  blocking collectives: 0 us -> 55.3 us
  waiting for transfers between devices: 91.1 us -> 45.8 us
  other arithmetic: 11.5 us -> 0.04 us
  loops' own time: 5.86 us -> 0 us
  starting transfers between devices: 20.8 us -> 16.5 us
    dot_general x11 -> x0, matrix products: 68 us -> none  [the longest x8 45.5 us: one_block(): jnp.einsum('hqk,khd->qhd', weights, value_group, preferred_element_type=j...]
    pallas_call x0 -> x3, Pallas kernels: none -> 62.5 us  [the longest x1 53.8 us: block_one(): pl.pallas_call(block_kernel, out_shape=jax.ShapeDtypeStruct((slots, chann...]
    all_to_all x0 -> x1, blocking collectives: none -> 55.3 us  [on_device(): lax.all_to_all(send.reshape(devices, capacity, channels), AXES, split_axi...]
    all_to_all x2 -> x1, waiting for transfers between devices: 47.6 us -> 0.01 us  [on_device(): lax.all_to_all(place, AXES, split_axis=0, concat_axis=0, tiled=True)]
    sub x8 -> x0, matrix products: 39.1 us -> none  [one_block(): weights = jax.nn.softmax(scores, axis=-1).astype(jnp.bfloat16)]
    scatter x3 -> x0, local copies, waits for them, and re-layouts: 38.5 us -> none  [the longest x1 18.4 us: on_device(): serial = jnp.zeros((row_count, channels), jnp.bfloat16).at[target].set(go...]
    slice x13 -> x1, local copies, waits for them, and re-layouts: 15.1 us -> 1.06 us  [on_device(): behind = lax.ppermute(points[:half], AXES, ring_down)]
    another operation x3 -> x0, other arithmetic: 9.41 us -> none
  transfers between devices with their start and end apart: 6 -> 5, of which waited for: 3 -> 4; matrix products, arithmetic and copies ran while one was open for 45% -> 0% of each run, Pallas kernels for 0% -> 23%
where the time goes in v2:
time: 242 us
  Pallas kernels  120 us (50%)
  blocking collectives  55.3 us (23%)
  waiting for transfers between devices  45.8 us (19%)
  starting transfers between devices  16.5 us (7%)
  local copies, waits for them, and re-layouts  3.9 us (2%)
    pallas_call x1, Pallas kernels, position_conv(): pl.pallas_call(functools.partial(conv_kernel, block, offs, rows), out_sha...  57.4 us
    all_to_all x1, blocking collectives, on_device(): lax.all_to_all(send.reshape(devices, capacity, channels), AXES, split_axi...  55.3 us
    pallas_call x1, Pallas kernels, block_one(): pl.pallas_call(block_kernel, out_shape=jax.ShapeDtypeStruct((slots, chann...  53.8 us
    ppermute x1, waiting for transfers between devices, on_device(): right = lax.ppermute(serial, AXES, ring_down[:-1])  21.8 us
    ppermute x1, waiting for transfers between devices, on_device(): left = lax.ppermute(serial, AXES, ring_up[:-1])  20.8 us
    pallas_call x1, Pallas kernels, settle(): pl.pallas_call(settle_kernel, out_shape=jax.ShapeDtypeStruct((rows, chann...  6.52 us
    ppermute x1, starting transfers between devices, on_device(): right = lax.ppermute(serial, AXES, ring_down[:-1])  5.44 us
  transfers between devices with their start and end apart: 5, of which 4 were waited for; matrix products, arithmetic and copies ran while one was open for 0% of the time, Pallas kernels for 23%

profile of v2, /device:TPU:1, one launch (start us, length us, event | category | flops | bytes accessed | tf_op | source)
XLA Modules:
  0.0 241.6 jit_solution(10996618677274150276)
XLA Ops:
  0.0 1.1 fusion
  1.1 2.2 collective-permute-start
  3.3 2.7 %collective-permute-start.1 = (bf16[512,256]{1,0:T(8,128)(2,1)S(1)}, bf16[512,256]{1,0:T(8,128)(2,1)S(1)}, u32[]{:S(2)}, u32[]{:S(2)}) collective-permute-start(bf16[512,256]{1,0:T(8,128)(2,1)S(1)} %get-tuple-element.9), channel_id=1, source_target_pairs={{1,0},{2,1},{3,2},{4,3},{5,4},{6,5},{7,6},{8,7},{9,8},{10,9},{11,1... | collective-permute-start | bytes 786440 | tf_op jit(solution)/shard_map/ppermute | solution.py:290
  5.9 2.2 find_slots.1
  8.1 4.3 %all-to-all-start = ((s32[32,1,128]{2,1,0:T(1,128)}), s32[32,1,128]{2,1,0:T(1,128)S(1)}, u32[]{:S(2)}, u32[]{:S(2)}) async-start(s32[32,1,128]{2,1,0:T(1,128)} %bitcast.17), calls=%async_computation | async-start | bytes 32768 | tf_op jit(solution)/shard_map/all_to_all | solution.py:292
  12.4 0.1 collective-permute-done.left_ref
  12.5 0.0 copy-start.2
  12.5 3.2 %collective-permute-done.1.right_ref = bf16[512,256]{1,0:T(8,128)(2,1)S(1)} collective-permute-done((bf16[512,256]{1,0:T(8,128)(2,1)S(1)}, bf16[512,256]{1,0:T(8,128)(2,1)S(1)}, u32[]{:S(2)}, u32[]{:S(2)}) %collective-permute-start.1) | collective-permute-done | bytes 262176 | tf_op jit(solution)/shard_map/ppermute | solution.py:290
  15.7 0.0 copy-start.3
  15.7 0.0 copy-done.2
  15.7 0.7 copy-done.3
  16.4 53.8 %block_one.1 = bf16[4096,256]{1,0:T(8,128)(2,1)} custom-call(s32[1,2048]{1,0:T(1,128)} %get-tuple-element.8.index_ref, bf16[512,256]{1,0:T(8,128)(2,1)} %copy-done.2, bf16[2048,256]{1,0:T(8,128)(2,1)} %own_ref.1, bf16[512,256]{1,0:T(8,128)(2,1)} %copy-done.3, bf16[256,768]{1,0:T(8,128)(2,1)} %qkv_ref.1, bf16[256,256]{1,0:T(8,128)(2,1)} %proj_ref.1, ...), custom_call_target="tpu_custom_call" | custom-call | tf_op jit(solution)/shard_map/block_one/pallas_call | solution.py:164
  70.2 0.0 all-to-all-done
  70.2 0.0 copy-start.5
  70.2 55.3 %all_to_all.16 = bf16[32,128,256]{2,1,0:T(8,128)(2,1)} all-to-all(bf16[32,128,256]{2,1,0:T(8,128)(2,1)} %bitcast.13), channel_id=1, replica_groups=mesh['curve'=8,'group'=4] {'curve','group'}, dimensions={0} | all-to-all | bytes 4194304 | tf_op jit(solution)/shard_map/all_to_all | solution.py:294
  125.5 0.0 copy-done.5
  125.5 0.0 copy-start.4
  125.5 6.5 %settle.1.own_ref = bf16[2048,256]{1,0:T(8,128)(2,1)} custom-call(s32[32,128]{1,0:T(8,128)} %bitcast.16, bf16[4096,256]{1,0:T(8,128)(2,1)} %bitcast.14), custom_call_target="tpu_custom_call" | custom-call | tf_op jit(solution)/shard_map/settle/pallas_call | solution.py:206
  132.0 1.9 collective-permute-start.2
  134.0 5.4 %collective-permute-start.3 = (bf16[2048,256]{1,0:T(8,128)(2,1)}, bf16[2048,256]{1,0:T(8,128)(2,1)S(1)}, u32[]{:S(2)}, u32[]{:S(2)}) collective-permute-start(bf16[2048,256]{1,0:T(8,128)(2,1)} %settle.1.own_ref), channel_id=1, source_target_pairs={{1,0},{2,1},{3,2},{4,3},{5,4},{6,5},{7,6},{8,7},{9,8},{10,9},{11,1... | collective-permute-start | bytes 3145736 | tf_op jit(solution)/shard_map/ppermute | solution.py:299
  139.4 0.0 copy-done.4
  139.5 0.1 reshape.20
  139.6 0.1 copy.18
  139.7 0.9 reshape.26.idx_ref
  140.6 20.8 %collective-permute-done.2.left_ref = bf16[2048,256]{1,0:T(8,128)(2,1)S(1)} collective-permute-done((bf16[2048,256]{1,0:T(8,128)(2,1)}, bf16[2048,256]{1,0:T(8,128)(2,1)S(1)}, u32[]{:S(2)}, u32[]{:S(2)}) %collective-permute-start.2) | collective-permute-done | bytes 1048608 | tf_op jit(solution)/shard_map/ppermute | solution.py:298
  161.4 0.0 copy-start
  161.4 21.8 %collective-permute-done.3.right_ref = bf16[2048,256]{1,0:T(8,128)(2,1)S(1)} collective-permute-done((bf16[2048,256]{1,0:T(8,128)(2,1)}, bf16[2048,256]{1,0:T(8,128)(2,1)S(1)}, u32[]{:S(2)}, u32[]{:S(2)}) %collective-permute-start.3) | collective-permute-done | bytes 1048608 | tf_op jit(solution)/shard_map/ppermute | solution.py:299
  183.2 0.0 copy-done
  183.2 0.0 copy-start.1
  183.2 1.0 copy-done.1
  184.1 57.4 %shard_map.100 = bf16[2048,256]{1,0:T(8,128)(2,1)} custom-call(s32[4,1,13824]{2,1,0:T(1,128)} %reshape.26.idx_ref, bf16[2048,256]{1,0:T(8,128)(2,1)} %copy-done, bf16[2048,256]{1,0:T(8,128)(2,1)} %settle.1.own_ref, bf16[2048,256]{1,0:T(8,128)(2,1)} %copy-done.1, bf16[6912,256]{1,0:T(8,128)(2,1)} %w_ref.1, bf16[256,256]{1,0:T(8,128)(2,1)} %lin_ref.1), custom_call_target="tpu_custom_call" | custom-call | tf_op jit(solution)/shard_map/pallas_call | solution.py:254
  (1 shorter events, 0.0 us)
Async XLA Ops:
  1.1 11.5 %collective-permute-start = (bf16[512,256]{1,0:T(8,128)(2,1)S(1)}, bf16[512,256]{1,0:T(8,128)(2,1)S(1)}, u32[]{:S(2)}, u32[]{:S(2)}) collective-permute-start(bf16[512,256]{1,0:T(8,128)(2,1)S(1)} %get-tuple-element.10), channel_id=1, source_target_pairs={{0,1},{1,2},{2,3},{3,4},{4,5},{5,6},{6,7},{7,8},{8,9},{9,10},{10,1... | collective-permute-start | bytes 786440 | tf_op jit(solution)/shard_map/ppermute | solution.py:289
  3.3 12.5 %collective-permute-start.1 = (bf16[512,256]{1,0:T(8,128)(2,1)S(1)}, bf16[512,256]{1,0:T(8,128)(2,1)S(1)}, u32[]{:S(2)}, u32[]{:S(2)}) collective-permute-start(bf16[512,256]{1,0:T(8,128)(2,1)S(1)} %get-tuple-element.9), channel_id=1, source_target_pairs={{1,0},{2,1},{3,2},{4,3},{5,4},{6,5},{7,6},{8,7},{9,8},{10,9},{11,1... | collective-permute-start | bytes 786440 | tf_op jit(solution)/shard_map/ppermute | solution.py:290
  8.1 62.1 %all-to-all-start = ((s32[32,1,128]{2,1,0:T(1,128)}), s32[32,1,128]{2,1,0:T(1,128)S(1)}, u32[]{:S(2)}, u32[]{:S(2)}) async-start(s32[32,1,128]{2,1,0:T(1,128)} %bitcast.17), calls=%async_computation | async-start | bytes 32768 | tf_op jit(solution)/shard_map/all_to_all | solution.py:292
  12.5 3.2 %copy-start.2 = (bf16[512,256]{1,0:T(8,128)(2,1)}, bf16[512,256]{1,0:T(8,128)(2,1)S(1)}, u32[]{:S(2)}) copy-start(bf16[512,256]{1,0:T(8,128)(2,1)S(1)} %collective-permute-done.left_ref) | copy-start | bytes 786436
  15.7 0.7 copy-start.3
  70.2 55.3 %copy-start.5 = (s32[32,1,128]{2,1,0:T(1,128)}, s32[32,1,128]{2,1,0:T(1,128)S(1)}, u32[]{:S(2)}) copy-start(s32[32,1,128]{2,1,0:T(1,128)S(1)} %all-to-all-done) | copy-start | bytes 49156
  125.5 13.9 %copy-start.4 = (s32[2048,27]{0,1:T(8,128)S(1)}, s32[2048,27]{0,1:T(8,128)}, u32[]{:S(2)}) copy-start(s32[2048,27]{0,1:T(8,128)} %param.17) | copy-start | bytes 663556
  132.0 29.4 %collective-permute-start.2 = (bf16[2048,256]{1,0:T(8,128)(2,1)}, bf16[2048,256]{1,0:T(8,128)(2,1)S(1)}, u32[]{:S(2)}, u32[]{:S(2)}) collective-permute-start(bf16[2048,256]{1,0:T(8,128)(2,1)} %settle.1.own_ref), channel_id=1, source_target_pairs={{0,1},{1,2},{2,3},{3,4},{4,5},{5,6},{6,7},{7,8},{8,9},{9,10},{10,1... | collective-permute-start | bytes 3145736 | tf_op jit(solution)/shard_map/ppermute | solution.py:298
  134.0 49.2 %collective-permute-start.3 = (bf16[2048,256]{1,0:T(8,128)(2,1)}, bf16[2048,256]{1,0:T(8,128)(2,1)S(1)}, u32[]{:S(2)}, u32[]{:S(2)}) collective-permute-start(bf16[2048,256]{1,0:T(8,128)(2,1)} %settle.1.own_ref), channel_id=1, source_target_pairs={{1,0},{2,1},{3,2},{4,3},{5,4},{6,5},{7,6},{8,7},{9,8},{10,9},{11,1... | collective-permute-start | bytes 3145736 | tf_op jit(solution)/shard_map/ppermute | solution.py:299
  161.4 21.8 %copy-start = (bf16[2048,256]{1,0:T(8,128)(2,1)}, bf16[2048,256]{1,0:T(8,128)(2,1)S(1)}, u32[]{:S(2)}) copy-start(bf16[2048,256]{1,0:T(8,128)(2,1)S(1)} %collective-permute-done.2.left_ref) | copy-start | bytes 3145732
  183.2 1.0 copy-start.1

commit v3 on v2

--- a/solution.py
+++ b/solution.py
@@ -214,58 +214,105 @@
     )(place, got)
 
 
-def conv_kernel(block, offs, rows, idx_ref, left_ref, own_ref, right_ref, w_ref, lin_ref, out_ref, tab, buf, lhs):
+CHUNK = 32
+
+
+def pick(step, values):
+    return sum(jnp.where(step == place, value, 0) for place, value in enumerate(values) if value)
+
+
+def conv_kernel(segment, starts, stores, sources, kept, rows, index_ref, *refs):
+    parts, refs = refs[: len(sources)], refs[len(sources) :]
+    olds, refs = refs[: len(kept)], refs[len(kept) :]
+    weight_ref, linear_ref, out_ref, table, ping, pong, operand = refs
     step = pl.program_id(0)
-    lanes = LANES
+    width = out_ref.shape[1]
+    offsets = weight_ref.shape[0] // width
+    middle = offsets // 2
+    moved = offsets - 3
+    block = 2 * segment
+    sides = width // LANES
 
     @pl.when(step == 0)
     def _():
-        for part, ref in enumerate((left_ref, own_ref, right_ref)):
-            for half in range(2):
-                tab[pl.ds(2 * part * rows + half, rows, stride=2), :] = ref[:, half * lanes:(half + 1) * lanes].astype(jnp.float32)
-        tab[pl.ds(6 * rows, 8), :] = jnp.zeros((8, lanes), jnp.float32)
-
-    start = pl.multiple_of(step * block, block)
-    width = 2 * lanes
-    mid = offs // 2
-    for k, ref in ((0, left_ref), (mid, own_ref), (offs - 1, right_ref)):
-        lhs[:, k * width:(k + 1) * width] = ref[pl.ds(start, block), :]
-
-    def one(o):
-        base = o * block
-        for j in range(block):
-            buf[2 * j:2 * j + 2, :] = tab[pl.ds(pl.multiple_of(idx_ref[0, 0, base + j], 2), 2), :]
-        for half in range(2):
-            lhs[:, pl.ds(pl.multiple_of(o * width + half * lanes, lanes), lanes)] = buf[pl.ds(half, block, stride=2), :].astype(jnp.bfloat16)
-
-    def body(o, carry):
-        one(o)
+        for (first, count), ref in zip(sources, parts):
+            for side in range(sides):
+                table[pl.ds(2 * first + side, count, stride=2), :] = ref[:, side * LANES : (side + 1) * LANES].astype(
+                    jnp.float32
+                )
+        table[pl.ds(6 * rows, 8), :] = jnp.zeros((8, LANES), jnp.float32)
+        for first, ref in zip(kept, olds):
+            out_ref[first : first + ref.shape[0], :] = ref[...]
+
+    begins = [pl.multiple_of(pick(step, [pair[piece] for pair in starts]), segment) for piece in range(2)]
+    ends = [pl.multiple_of(pick(step, [pair[piece] for pair in stores]), segment) for piece in range(2)]
+    for span, offset in enumerate((0, middle, offsets - 1)):
+        for piece, begin in enumerate(begins):
+            for side in range(sides):
+                operand[
+                    piece * segment : (piece + 1) * segment,
+                    offset * width + side * LANES : offset * width + (side + 1) * LANES,
+                ] = table[pl.ds(2 * (span * rows + begin) + side, segment, stride=2), :].astype(jnp.bfloat16)
+
+    def fetch(order, buffer, row):
+        for other in range(row, row + CHUNK):
+            source = pl.multiple_of(index_ref[0, 0, order * block + other], 2)
+            buffer[2 * other : 2 * other + 2, :] = table[pl.ds(source, 2), :]
+
+    def settle_columns(order, buffer, row):
+        offset = order + jnp.where(order < middle - 1, 1, 2)
+        column = pl.multiple_of(offset * width, width)
+        halves = [buffer[pl.ds(2 * row + side, CHUNK, stride=2), :].astype(jnp.bfloat16) for side in range(sides)]
+        operand[row : row + CHUNK, pl.ds(column, width)] = jnp.concatenate(halves, axis=1)
+
+    def body(pair, carry):
+        for turn, (filled, other) in enumerate(((ping, pong), (pong, ping))):
+            order = 2 * pair + turn
+            for row in range(0, block, CHUNK):
+                fetch(order, filled, row)
+                settle_columns(jnp.maximum(order - 1, 0), other, row)
         return carry
-    lax.fori_loop(1, mid, body, 0)
-    lax.fori_loop(mid + 1, offs - 1, body, 0)
-    conv = jnp.dot(lhs[...], w_ref[...], preferred_element_type=jnp.float32).astype(jnp.bfloat16)
-    linear = jnp.dot(conv, lin_ref[...], preferred_element_type=jnp.float32)
-    out_ref[...] = (own_ref[pl.ds(start, block), :].astype(jnp.float32) + layer_norm(linear)).astype(jnp.bfloat16)
-
-def position_conv(idx, left, own, right, w, lin, block):
-    rows, ch = own.shape
-    offs = w.shape[0] // ch
-    vm = pl.BlockSpec(memory_space=pltpu.VMEM)
+
+    lax.fori_loop(0, moved // 2, body, 0)
+    for row in range(0, block, CHUNK):
+        settle_columns(jnp.int32(moved - 1), pong, row)
+    conv = dot(operand[...], weight_ref[...]).astype(jnp.bfloat16)
+    normed = layer_norm(dot(conv, linear_ref[...]))
+    for piece in range(2):
+        begin = 2 * (rows + begins[piece])
+        own = [table[pl.ds(begin + side, segment, stride=2), :] for side in range(sides)]
+        result = jnp.concatenate(own, axis=1) + normed[piece * segment : (piece + 1) * segment]
+        out_ref[pl.ds(ends[piece], segment), :] = result.astype(jnp.bfloat16)
+
+
+def position_conv(near, starts, stores, count, sources, parts, kept, olds, weight, linear):
+    rows, offsets = near.shape
+    channels = linear.shape[0]
+    segment = rows // 8
+    middle = offsets // 2
+    steps = len(starts)
+    row_id = jnp.arange(rows, dtype=jnp.int32)[:, None]
+    index = 2 * jnp.where(near < 0, 3 * rows, near + row_id)
+    index = jnp.concatenate([index[:, 1:middle], index[:, middle + 1 : offsets - 1]], axis=1)
+    index = jnp.concatenate([index[begin : begin + segment] for pair in starts for begin in pair], axis=0)
+    index = index.reshape(steps, 2 * segment, offsets - 3).transpose(0, 2, 1).reshape(steps, 1, -1)
+    vmem = pl.BlockSpec(memory_space=pltpu.VMEM)
     return pl.pallas_call(
-        functools.partial(conv_kernel, block, offs, rows),
-        out_shape=jax.ShapeDtypeStruct((rows, ch), jnp.bfloat16),
-        grid=(rows // block,),
-        in_specs=[pl.BlockSpec((1, 1, offs * block), lambda i: (i, 0, 0), memory_space=pltpu.SMEM), vm, vm, vm, vm, vm],
-        out_specs=pl.BlockSpec((block, ch), lambda i: (i, 0)),
-        scratch_shapes=[pltpu.VMEM((6 * rows + 8, LANES), jnp.float32), pltpu.VMEM((2 * block, LANES), jnp.float32), pltpu.VMEM((block, offs * ch), jnp.bfloat16)],
+        functools.partial(conv_kernel, segment, starts, stores, sources, kept, rows),
+        out_shape=jax.ShapeDtypeStruct((count, channels), jnp.bfloat16),
+        grid=(steps,),
+        in_specs=[pl.BlockSpec((1, 1, index.shape[2]), lambda step: (step, 0, 0), memory_space=pltpu.SMEM)]
+        + [vmem] * (len(parts) + len(olds) + 2),
+        out_specs=vmem,
+        scratch_shapes=[
+            pltpu.VMEM((6 * rows + 8, LANES), jnp.float32),
+            pltpu.VMEM((4 * segment, LANES), jnp.float32),
+            pltpu.VMEM((4 * segment, LANES), jnp.float32),
+            pltpu.VMEM((2 * segment, offsets * channels), jnp.bfloat16),
+        ],
         compiler_params=pltpu.CompilerParams(vmem_limit_bytes=56 << 20),
-    )(idx, left, own, right, w, lin)
-
-def gather_rows(near, block):
-    rows, offs = near.shape
-    h = jnp.arange(rows, dtype=jnp.int32)[:, None]
-    idx = 2 * jnp.where(near < 0, 3 * rows, near + h)
-    return idx.reshape(rows // block, block, offs).transpose(0, 2, 1).reshape(rows // block, 1, offs * block)
+        name="position_conv",
+    )(index, *parts, *olds, weight, linear)
 
 
 def on_device(
@@ -295,10 +342,24 @@
         send.reshape(devices, capacity, channels), AXES, split_axis=0, concat_axis=0, tiled=True
     )
     serial = settle(got_place, got.reshape(devices * capacity, channels), row_count)
-    left = lax.ppermute(serial, AXES, ring_up[:-1])
-    right = lax.ppermute(serial, AXES, ring_down[:-1])
-    block = min(512, row_count)
-    return position_conv(gather_rows(neighbors, block), left, serial, right, conv_two, linear_two, block)
+    segment = row_count // 8
+    low, high = 3 * segment, 5 * segment
+    left_near = lax.ppermute(serial[low:], AXES, ring_up[:-1])
+    right_near = lax.ppermute(serial[:high], AXES, ring_down[:-1])
+    left_far = lax.ppermute(serial[:low], AXES, ring_up[:-1])
+    right_far = lax.ppermute(serial[high:], AXES, ring_down[:-1])
+    parts = [left_near, serial, right_near]
+    sources = [(low, row_count - low), (row_count, row_count), (2 * row_count, high)]
+    inner = [(low, low + segment)]
+    outer = [(0, segment), (2 * segment, high), (6 * segment, 7 * segment)]
+    center = position_conv(
+        neighbors, inner, [(0, segment)], 2 * segment, sources, parts, [], [], conv_two, linear_two
+    )
+    parts += [left_far, right_far]
+    sources += [(0, low), (2 * row_count + high, row_count - high)]
+    return position_conv(
+        neighbors, outer, outer, row_count, sources, parts, [low], [center], conv_two, linear_two
+    )
 
 
 def solution(mesh):

time: 242 us -> 231 us (0.955)
  blocking collectives: 55.3 us -> 0 us
  waiting for transfers between devices: 45.8 us -> 69.5 us
  starting transfers between devices: 16.5 us -> 29.4 us
  local copies, waits for them, and re-layouts: 3.9 us -> 11 us
    all_to_all x1 -> x0, blocking collectives: 55.3 us -> none  [on_device(): lax.all_to_all(send.reshape(devices, capacity, channels), AXES, split_axi...]
    all_to_all x0 -> x1, waiting for transfers between devices: none -> 48.2 us  [on_device(): lax.all_to_all(send.reshape(devices, capacity, channels), AXES, split_axi...]
    ppermute x2 -> x4, waiting for transfers between devices: 42.5 us -> 18.6 us  [the longest x1 16.4 us: on_device(): left_near = lax.ppermute(serial[low:], AXES, ring_up[:-1])]
    ppermute x2 -> x4, starting transfers between devices: 7.35 us -> 12.9 us  [the longest x1 5.43 us: on_device(): right_far = lax.ppermute(serial[high:], AXES, ring_down[:-1])]
    all_to_all x0 -> x1, starting transfers between devices: none -> 4.54 us  [on_device(): lax.all_to_all(send.reshape(devices, capacity, channels), AXES, split_axi...]
    unnamed x12 -> x20, local copies, waits for them, and re-layouts: 1.68 us -> 4.99 us
    slice x0 -> x3, local copies, waits for them, and re-layouts: none -> 3.25 us  [the longest x1 2.29 us: on_device(): right_near = lax.ppermute(serial[:high], AXES, ring_down[:-1])]
    ppermute x1, waiting for transfers between devices: 3.2 us -> 0.01 us  [on_device(): behind = lax.ppermute(points[:half], AXES, ring_down)]
  transfers between devices with their start and end apart: 5 -> 8, of which waited for: 4 -> 4; matrix products, arithmetic and copies ran while one was open for 0% -> 1% of each run, Pallas kernels for 23% -> 31%
where the time goes in v3:
time: 231 us; the launch traced here: 230 us
  Pallas kernels  120 us (52%)
  waiting for transfers between devices  69.5 us (30%)
  starting transfers between devices  29.4 us (13%)
  local copies, waits for them, and re-layouts  11 us (5%)
    pallas_call x2, Pallas kernels, position_conv(): pl.pallas_call(functools.partial(conv_kernel, segment, starts, stores, so...  57.8 us
    pallas_call x1, Pallas kernels, block_one(): pl.pallas_call(block_kernel, out_shape=jax.ShapeDtypeStruct((slots, chann...  53.8 us
    all_to_all x1, waiting for transfers between devices, on_device(): lax.all_to_all(send.reshape(devices, capacity, channels), AXES, split_axi...  48.2 us
    ppermute x1, waiting for transfers between devices, on_device(): left_near = lax.ppermute(serial[low:], AXES, ring_up[:-1])  16.4 us
    all_to_all x1, starting transfers between devices, on_device(): lax.all_to_all(place, AXES, split_axis=0, concat_axis=0, tiled=True)  7.16 us
    pallas_call x1, Pallas kernels, settle(): pl.pallas_call(settle_kernel, out_shape=jax.ShapeDtypeStruct((rows, chann...  6.5 us
    ppermute x1, starting transfers between devices, on_device(): right_far = lax.ppermute(serial[high:], AXES, ring_down[:-1])  5.43 us
    unnamed x20, local copies, waits for them, and re-layouts  4.99 us
  transfers between devices with their start and end apart: 8, of which 4 were waited for; matrix products, arithmetic and copies ran while one was open for 1% of the time, Pallas kernels for 31%

profile of v3, /device:TPU:1, one launch (start us, length us, event | category | flops | bytes accessed | tf_op | source)
XLA Modules:
  0.0 230.3 jit_solution(3752854604637790453)
XLA Ops:
  0.0 1.1 fusion.5
  1.1 4.8 %collective-permute-start.1 = (bf16[512,256]{1,0:T(8,128)(2,1)S(1)}, bf16[512,256]{1,0:T(8,128)(2,1)S(1)}, u32[]{:S(2)}, u32[]{:S(2)}) collective-permute-start(bf16[512,256]{1,0:T(8,128)(2,1)S(1)} %get-tuple-element.13), channel_id=1, source_target_pairs={{1,0},{2,1},{3,2},{4,3},{5,4},{6,5},{7,6},{8,7},{9,8},{10,9},{11,1... | collective-permute-start | bytes 786440 | tf_op jit(solution)/shard_map/ppermute | solution.py:337
  5.8 0.0 collective-permute-start
  5.8 2.2 find_slots.1
  8.0 7.2 %all-to-all-start = ((s32[32,1,128]{2,1,0:T(1,128)}), s32[32,1,128]{2,1,0:T(1,128)S(1)}, u32[]{:S(2)}, u32[]{:S(2)}) async-start(s32[32,1,128]{2,1,0:T(1,128)} %bitcast.19), calls=%async_computation | async-start | bytes 32768 | tf_op jit(solution)/shard_map/all_to_all | solution.py:339
  15.2 0.0 collective-permute-done.1.right_ref
  15.2 0.0 copy-start.6
  15.2 2.7 %collective-permute-done.left_ref = bf16[512,256]{1,0:T(8,128)(2,1)S(1)} collective-permute-done((bf16[512,256]{1,0:T(8,128)(2,1)S(1)}, bf16[512,256]{1,0:T(8,128)(2,1)S(1)}, u32[]{:S(2)}, u32[]{:S(2)}) %collective-permute-start) | collective-permute-done | bytes 262176 | tf_op jit(solution)/shard_map/ppermute | solution.py:336
  17.9 0.0 copy-start.7
  17.9 0.0 copy-done.6
  17.9 0.7 copy-done.7
  18.6 53.8 %block_one.1 = bf16[4096,256]{1,0:T(8,128)(2,1)} custom-call(s32[1,2048]{1,0:T(1,128)} %get-tuple-element.8.index_ref, bf16[512,256]{1,0:T(8,128)(2,1)} %copy-done.7, bf16[2048,256]{1,0:T(8,128)(2,1)} %own_ref.1, bf16[512,256]{1,0:T(8,128)(2,1)} %copy-done.6, bf16[256,768]{1,0:T(8,128)(2,1)} %qkv_ref.1, bf16[256,256]{1,0:T(8,128)(2,1)} %proj_ref.1, ...), custom_call_target="tpu_custom_call" | custom-call | tf_op jit(solution)/shard_map/block_one/pallas_call | solution.py:164
  72.4 0.0 all-to-all-done
  72.4 0.0 copy-start.9
  72.4 0.0 copy-start.8
  72.4 0.6 copy-done.9
  73.0 4.5 %all-to-all-start.1 = ((bf16[32,128,256]{2,1,0:T(8,128)(2,1)}), bf16[32,128,256]{2,1,0:T(8,128)(2,1)S(1)}, u32[]{:S(2)}, u32[]{:S(2)}) async-start(bf16[32,128,256]{2,1,0:T(8,128)(2,1)} %bitcast.15), calls=%async_computation.1 | async-start | bytes 4194304 | tf_op jit(solution)/shard_map/all_to_all | solution.py:341
  77.6 0.0 copy-done.8
  77.6 48.2 %all-to-all-done.1 = bf16[32,128,256]{2,1,0:T(8,128)(2,1)S(1)} async-done(((bf16[32,128,256]{2,1,0:T(8,128)(2,1)}), bf16[32,128,256]{2,1,0:T(8,128)(2,1)S(1)}, u32[]{:S(2)}, u32[]{:S(2)}) %all-to-all-start.1) | async-done | bytes 2097184 | tf_op jit(solution)/shard_map/all_to_all | solution.py:341
  125.8 0.0 copy-start.1
  125.8 1.3 copy-done.1
  127.1 6.5 %settle.1.refs_1_ = bf16[2048,256]{1,0:T(8,128)(2,1)} custom-call(s32[32,128]{1,0:T(8,128)} %bitcast.18, bf16[4096,256]{1,0:T(8,128)(2,1)} %bitcast.16), custom_call_target="tpu_custom_call" | custom-call | tf_op jit(solution)/shard_map/settle/pallas_call | solution.py:206
  133.6 0.0 copy-start
  133.6 2.3 fusion.4
  135.9 3.6 %collective-permute-start.3 = (bf16[1280,256]{1,0:T(8,128)(2,1)}, bf16[1280,256]{1,0:T(8,128)(2,1)S(1)}, u32[]{:S(2)}, u32[]{:S(2)}) collective-permute-start(bf16[1280,256]{1,0:T(8,128)(2,1)} %get-tuple-element.11), channel_id=1, source_target_pairs={{1,0},{2,1},{3,2},{4,3},{5,4},{6,5},{7,6},{8,7},{9,8},{10,9},{11,1... | collective-permute-start | bytes 1966088 | tf_op jit(solution)/shard_map/ppermute | solution.py:348
  139.6 1.9 collective-permute-start.2
  141.5 0.0 copy-done
  141.5 0.9 fusion.3
  142.5 5.4 %collective-permute-start.5 = (bf16[768,256]{1,0:T(8,128)(2,1)}, bf16[768,256]{1,0:T(8,128)(2,1)S(1)}, u32[]{:S(2)}, u32[]{:S(2)}) collective-permute-start(bf16[768,256]{1,0:T(8,128)(2,1)} %get-tuple-element.9), channel_id=1, source_target_pairs={{1,0},{2,1},{3,2},{4,3},{5,4},{6,5},{7,6},{8,7},{9,8},{10,9},{11,1... | collective-permute-start | bytes 1179656 | tf_op jit(solution)/shard_map/ppermute | solution.py:350
  147.9 1.9 collective-permute-start.4
  149.8 0.7 reshape.33.index_ref
  150.6 0.1 reshape.26
  150.7 0.1 copy.13
  150.7 0.8 reshape.27.index_ref
  151.6 2.1 collective-permute-done.3.refs_2_
  153.7 0.0 copy-start.2
  153.7 16.4 %collective-permute-done.2.refs_0_ = bf16[1280,256]{1,0:T(8,128)(2,1)S(1)} collective-permute-done((bf16[1280,256]{1,0:T(8,128)(2,1)S(1)}, bf16[1280,256]{1,0:T(8,128)(2,1)S(1)}, u32[]{:S(2)}, u32[]{:S(2)}) %collective-permute-start.2) | collective-permute-done | bytes 655392 | tf_op jit(solution)/shard_map/ppermute | solution.py:347
  170.1 0.0 copy-done.2
  170.1 0.0 copy-start.3
  170.1 0.9 copy-done.3
  171.0 16.1 %position_conv.2.refs_5_ = bf16[512,256]{1,0:T(8,128)(2,1)} custom-call(s32[1,1,12288]{2,1,0:T(1,128)} %reshape.33.index_ref, bf16[1280,256]{1,0:T(8,128)(2,1)} %copy-done.3, bf16[2048,256]{1,0:T(8,128)(2,1)} %settle.1.refs_1_, bf16[1280,256]{1,0:T(8,128)(2,1)} %copy-done.2, bf16[6912,256]{1,0:T(8,128)(2,1)} %refs_6_.1, bf16[256,256]{1,0:T(8,128)(2,1)} %refs_7_.1), custom_call_target="tpu_custom_call" | custom-call | tf_op jit(solution)/shard_map/position_conv/pallas_call | solution.py:300
  187.1 0.0 collective-permute-done.5.refs_4_
  187.1 0.0 copy-start.4
  187.1 0.0 collective-permute-done.4.refs_3_
  187.1 0.7 copy-done.4
  187.8 0.0 copy-start.5
  187.8 0.7 copy-done.5
  188.6 41.7 %position_conv.3 = bf16[2048,256]{1,0:T(8,128)(2,1)} custom-call(s32[3,1,12288]{2,1,0:T(1,128)} %reshape.27.index_ref, bf16[1280,256]{1,0:T(8,128)(2,1)} %copy-done.3, bf16[2048,256]{1,0:T(8,128)(2,1)} %settle.1.refs_1_, bf16[1280,256]{1,0:T(8,128)(2,1)} %copy-done.2, bf16[768,256]{1,0:T(8,128)(2,1)} %copy-done.5, bf16[768,256]{1,0:T(8,128)(2,1)} %copy-done.4, ...), custom_call_target="tpu_custom_call" | custom-call | tf_op jit(solution)/shard_map/position_conv/pallas_call | solution.py:300
  (5 shorter events, 0.1 us)
Async XLA Ops:
  1.1 14.1 %collective-permute-start.1 = (bf16[512,256]{1,0:T(8,128)(2,1)S(1)}, bf16[512,256]{1,0:T(8,128)(2,1)S(1)}, u32[]{:S(2)}, u32[]{:S(2)}) collective-permute-start(bf16[512,256]{1,0:T(8,128)(2,1)S(1)} %get-tuple-element.13), channel_id=1, source_target_pairs={{1,0},{2,1},{3,2},{4,3},{5,4},{6,5},{7,6},{8,7},{9,8},{10,9},{11,1... | collective-permute-start | bytes 786440 | tf_op jit(solution)/shard_map/ppermute | solution.py:337
  5.8 12.1 %collective-permute-start = (bf16[512,256]{1,0:T(8,128)(2,1)S(1)}, bf16[512,256]{1,0:T(8,128)(2,1)S(1)}, u32[]{:S(2)}, u32[]{:S(2)}) collective-permute-start(bf16[512,256]{1,0:T(8,128)(2,1)S(1)} %get-tuple-element.14), channel_id=1, source_target_pairs={{0,1},{1,2},{2,3},{3,4},{4,5},{5,6},{6,7},{7,8},{8,9},{9,10},{10,1... | collective-permute-start | bytes 786440 | tf_op jit(solution)/shard_map/ppermute | solution.py:336
  8.0 64.4 %all-to-all-start = ((s32[32,1,128]{2,1,0:T(1,128)}), s32[32,1,128]{2,1,0:T(1,128)S(1)}, u32[]{:S(2)}, u32[]{:S(2)}) async-start(s32[32,1,128]{2,1,0:T(1,128)} %bitcast.19), calls=%async_computation | async-start | bytes 32768 | tf_op jit(solution)/shard_map/all_to_all | solution.py:339
  15.2 2.8 %copy-start.6 = (bf16[512,256]{1,0:T(8,128)(2,1)}, bf16[512,256]{1,0:T(8,128)(2,1)S(1)}, u32[]{:S(2)}) copy-start(bf16[512,256]{1,0:T(8,128)(2,1)S(1)} %collective-permute-done.1.right_ref) | copy-start | bytes 786436
  17.9 0.7 copy-start.7
  72.4 0.6 copy-start.9
  72.4 5.2 %copy-start.8 = (s32[2048,27]{0,1:T(8,128)S(1)}, s32[2048,27]{0,1:T(8,128)}, u32[]{:S(2)}) copy-start(s32[2048,27]{0,1:T(8,128)} %param.17) | copy-start | bytes 663556
  73.0 52.8 %all-to-all-start.1 = ((bf16[32,128,256]{2,1,0:T(8,128)(2,1)}), bf16[32,128,256]{2,1,0:T(8,128)(2,1)S(1)}, u32[]{:S(2)}, u32[]{:S(2)}) async-start(bf16[32,128,256]{2,1,0:T(8,128)(2,1)} %bitcast.15), calls=%async_computation.1 | async-start | bytes 4194304 | tf_op jit(solution)/shard_map/all_to_all | solution.py:341
  125.8 1.3 copy-start.1
  133.6 7.9 %copy-start = (bf16[2048,256]{1,0:T(8,128)(2,1)S(1)}, bf16[2048,256]{1,0:T(8,128)(2,1)}, u32[]{:S(2)}) copy-start(bf16[2048,256]{1,0:T(8,128)(2,1)} %settle.1.refs_1_) | copy-start | bytes 3145732
  135.9 17.7 %collective-permute-start.3 = (bf16[1280,256]{1,0:T(8,128)(2,1)}, bf16[1280,256]{1,0:T(8,128)(2,1)S(1)}, u32[]{:S(2)}, u32[]{:S(2)}) collective-permute-start(bf16[1280,256]{1,0:T(8,128)(2,1)} %get-tuple-element.11), channel_id=1, source_target_pairs={{1,0},{2,1},{3,2},{4,3},{5,4},{6,5},{7,6},{8,7},{9,8},{10,9},{11,1... | collective-permute-start | bytes 1966088 | tf_op jit(solution)/shard_map/ppermute | solution.py:348
  139.6 30.5 %collective-permute-start.2 = (bf16[1280,256]{1,0:T(8,128)(2,1)S(1)}, bf16[1280,256]{1,0:T(8,128)(2,1)S(1)}, u32[]{:S(2)}, u32[]{:S(2)}) collective-permute-start(bf16[1280,256]{1,0:T(8,128)(2,1)S(1)} %get-tuple-element.12), channel_id=1, source_target_pairs={{0,1},{1,2},{2,3},{3,4},{4,5},{5,6},{6,7},{7,8},{8,9},{9,10},{10,1... | collective-permute-start | bytes 1966088 | tf_op jit(solution)/shard_map/ppermute | solution.py:347
  142.5 44.6 %collective-permute-start.5 = (bf16[768,256]{1,0:T(8,128)(2,1)}, bf16[768,256]{1,0:T(8,128)(2,1)S(1)}, u32[]{:S(2)}, u32[]{:S(2)}) collective-permute-start(bf16[768,256]{1,0:T(8,128)(2,1)} %get-tuple-element.9), channel_id=1, source_target_pairs={{1,0},{2,1},{3,2},{4,3},{5,4},{6,5},{7,6},{8,7},{9,8},{10,9},{11,1... | collective-permute-start | bytes 1179656 | tf_op jit(solution)/shard_map/ppermute | solution.py:350
  147.9 39.2 %collective-permute-start.4 = (bf16[768,256]{1,0:T(8,128)(2,1)}, bf16[768,256]{1,0:T(8,128)(2,1)S(1)}, u32[]{:S(2)}, u32[]{:S(2)}) collective-permute-start(bf16[768,256]{1,0:T(8,128)(2,1)} %get-tuple-element.10), channel_id=1, source_target_pairs={{0,1},{1,2},{2,3},{3,4},{4,5},{5,6},{6,7},{7,8},{8,9},{9,10},{10,1... | collective-permute-start | bytes 1179656 | tf_op jit(solution)/shard_map/ppermute | solution.py:349
  153.7 16.4 %copy-start.2 = (bf16[1280,256]{1,0:T(8,128)(2,1)}, bf16[1280,256]{1,0:T(8,128)(2,1)S(1)}, u32[]{:S(2)}) copy-start(bf16[1280,256]{1,0:T(8,128)(2,1)S(1)} %collective-permute-done.3.refs_2_) | copy-start | bytes 1966084
  170.1 0.9 copy-start.3
  187.1 0.8 copy-start.4
  187.8 0.7 copy-start.5

commit v4 on v3

--- a/solution.py
+++ b/solution.py
@@ -75,50 +75,22 @@
     )(device.reshape(1, rows), position.reshape(1, rows))
 
 
-def block_kernel(
-    index_ref,
-    left_ref,
-    own_ref,
-    right_ref,
-    qkv_ref,
-    proj_ref,
-    up_ref,
-    down_ref,
-    send_ref,
-    query,
-    key,
-    value,
-    pairs,
-    table,
-):
-    step = pl.program_id(0)
-    rows, channels = own_ref.shape
-    half = PATCH // 2
-
-    @pl.when(step == 0)
-    def _():
-        count = rows // half
-        for part in range(count + 2):
-            if part == 0:
-                source = left_ref[...]
-            elif part == count + 1:
-                source = right_ref[...]
-            else:
-                source = own_ref[(part - 1) * half : part * half, :]
-            normed = layer_norm(source).astype(jnp.bfloat16)
-            span = slice(part * half, (part + 1) * half)
-            key[:, span] = lax.dot_general(
-                qkv_ref[:, channels : 2 * channels],
-                normed,
-                (((0,), (1,)), ((), ())),
-                preferred_element_type=jnp.float32,
-            ).astype(jnp.bfloat16)
-            value[span, :] = dot(normed, qkv_ref[:, 2 * channels :]).astype(jnp.bfloat16)
-            if 0 < part <= count:
-                query[(part - 1) * half : part * half, :] = dot(normed, qkv_ref[:, :channels]).astype(jnp.bfloat16)
-
-    first = pl.multiple_of(step * half, half)
-    start = pl.multiple_of(PATCH * ((step + 1) // 2), PATCH)
+def project(source, key, value, weight_ref, key_ref, value_ref, query_ref=None, query=0):
+    count, channels = source.shape
+    normed = layer_norm(source).astype(jnp.bfloat16)
+    key_ref[:, key : key + count] = lax.dot_general(
+        weight_ref[:, channels : 2 * channels],
+        normed,
+        (((0,), (1,)), ((), ())),
+        preferred_element_type=jnp.float32,
+    ).astype(jnp.bfloat16)
+    value_ref[value : value + count, :] = dot(normed, weight_ref[:, 2 * channels :]).astype(jnp.bfloat16)
+    if query_ref is not None:
+        query_ref[query : query + count, :] = dot(normed, weight_ref[:, :channels]).astype(jnp.bfloat16)
+
+
+def transform(residual, first, start, query, key, value, proj_ref, up_ref, down_ref):
+    half, channels = residual.shape
     per_group = LANES // HEAD_DIM
     head_of = lax.broadcasted_iota(jnp.int32, (1, LANES), 1) // HEAD_DIM
     scale = HEAD_DIM ** (-0.5) * LOG2E
@@ -140,15 +112,82 @@
             total = result if total is None else total + result
         pieces.append((total[:, :LANES] / total[:, LANES:]).astype(jnp.bfloat16))
     mixed = jnp.concatenate(pieces, axis=1)
-    after = (own_ref[pl.ds(first, half), :].astype(jnp.float32) + dot(mixed, proj_ref[...])).astype(jnp.bfloat16)
+    after = (residual.astype(jnp.float32) + dot(mixed, proj_ref[...])).astype(jnp.bfloat16)
     normed = layer_norm(after).astype(jnp.bfloat16)
     hidden = gelu(dot(normed, up_ref[...])).astype(jnp.bfloat16)
-    out = (after.astype(jnp.float32) + dot(hidden, down_ref[...])).astype(jnp.bfloat16).astype(jnp.float32)
-    pairs[pl.ds(0, half, stride=2), :] = out[:, :LANES]
-    pairs[pl.ds(1, half, stride=2), :] = out[:, LANES:]
-    for row in range(half):
-        slot = pl.multiple_of(index_ref[0, first + row], 2)
-        table[pl.ds(slot, 2), :] = pairs[2 * row : 2 * row + 2, :]
+    return (after.astype(jnp.float32) + dot(hidden, down_ref[...])).astype(jnp.bfloat16)
+
+
+def inner_kernel(own_ref, qkv_ref, proj_ref, up_ref, down_ref, out_ref, query, key, value):
+    step = pl.program_id(0)
+    half = PATCH // 2
+    steps = out_ref.shape[0] // half
+
+    @pl.when(step == 0)
+    def _():
+        for part in range(steps):
+            at = part * half
+            project(own_ref[at + half : at + 2 * half, :], at, at, qkv_ref, key, value, query, at)
+
+    first = pl.multiple_of(step * half, half)
+    start = pl.multiple_of(PATCH * (step // 2), PATCH)
+    residual = own_ref[pl.ds(first + half, half), :]
+    out_ref[pl.ds(first, half), :] = transform(residual, first, start, query, key, value, proj_ref, up_ref, down_ref)
+
+
+def outer_kernel(
+    index_ref,
+    left_ref,
+    own_ref,
+    right_ref,
+    inner_ref,
+    qkv_ref,
+    proj_ref,
+    up_ref,
+    down_ref,
+    send_ref,
+    query,
+    key,
+    value,
+    pairs,
+    table,
+):
+    step = pl.program_id(0)
+    rows = own_ref.shape[0]
+    half = PATCH // 2
+
+    def deliver(values, row):
+        for side in range(2):
+            pairs[pl.ds(side, half, stride=2), :] = values[:, side * LANES : (side + 1) * LANES].astype(jnp.float32)
+
+        def body(part, carry):
+            base = pl.multiple_of(part * LANES, LANES)
+            for other in range(LANES):
+                slot = pl.multiple_of(index_ref[0, row + base + other], 2)
+                table[pl.ds(slot, 2), :] = pairs[pl.ds(2 * base + 2 * other, 2), :]
+            return carry
+
+        lax.fori_loop(0, half // LANES, body, 0)
+
+    @pl.when(step == 0)
+    def _():
+        project(left_ref[...], 0, 0, qkv_ref, key, value)
+        project(own_ref[:half, :], half, half, qkv_ref, key, value, query, 0)
+        project(own_ref[rows - half :, :], 2 * half, 2 * half, qkv_ref, key, value, query, half)
+        project(right_ref[...], 3 * half, 3 * half, qkv_ref, key, value)
+
+        def body(part, carry):
+            at = pl.multiple_of(part * half, half)
+            deliver(inner_ref[pl.ds(at, half), :], at + half)
+            return carry
+
+        lax.fori_loop(0, inner_ref.shape[0] // half, body, 0)
+
+    row = pl.multiple_of(step * (rows - half), half)
+    first = pl.multiple_of(step * half, half)
+    start = pl.multiple_of(step * PATCH, PATCH)
+    residual = own_ref[pl.ds(row, half), :]
+    deliver(transform(residual, first, start, query, key, value, proj_ref, up_ref, down_ref), row)
 
     @pl.when(step == pl.num_programs(0) - 1)
     def _():
@@ -157,31 +196,52 @@
             send_ref[:, side * LANES : (side + 1) * LANES] = table[pl.ds(side, slots, stride=2), :].astype(jnp.bfloat16)
 
 
-def block_one(index, left, own, right, qkv, proj, up, down, slots):
+def inner_block(own, qkv, proj, up, down):
     rows, channels = own.shape
+    half = PATCH // 2
+    count = rows - 2 * half
+    vmem = pl.BlockSpec(memory_space=pltpu.VMEM)
+    return pl.pallas_call(
+        inner_kernel,
+        out_shape=jax.ShapeDtypeStruct((count, channels), jnp.bfloat16),
+        grid=(count // half,),
+        in_specs=[vmem] * 5,
+        out_specs=vmem,
+        scratch_shapes=[
+            pltpu.VMEM((count, channels), jnp.bfloat16),
+            pltpu.VMEM((channels, count), jnp.bfloat16),
+            pltpu.VMEM((count, channels), jnp.bfloat16),
+        ],
+        compiler_params=pltpu.CompilerParams(vmem_limit_bytes=56 << 20),
+        name="inner_block",
+    )(own, qkv, proj, up, down)
+
+
+def outer_block(index, left, own, right, inner, qkv, proj, up, down, slots):
+    channels = own.shape[1]
     half = PATCH // 2
     vmem = pl.BlockSpec(memory_space=pltpu.VMEM)
     return pl.pallas_call(
-        block_kernel,
+        outer_kernel,
         out_shape=jax.ShapeDtypeStruct((slots, channels), jnp.bfloat16),
-        grid=(rows // half,),
-        in_specs=[pl.BlockSpec(memory_space=pltpu.SMEM)] + [vmem] * 7,
+        grid=(2,),
+        in_specs=[pl.BlockSpec(memory_space=pltpu.SMEM)] + [vmem] * 8,
         out_specs=vmem,
         scratch_shapes=[
-            pltpu.VMEM((rows, channels), jnp.bfloat16),
-            pltpu.VMEM((channels, rows + PATCH), jnp.bfloat16),
-            pltpu.VMEM((rows + PATCH, channels), jnp.bfloat16),
+            pltpu.VMEM((2 * half, channels), jnp.bfloat16),
+            pltpu.VMEM((channels, 2 * PATCH), jnp.bfloat16),
+            pltpu.VMEM((2 * PATCH, channels), jnp.bfloat16),
             pltpu.VMEM((2 * half, LANES), jnp.float32),
             pltpu.VMEM((2 * slots, LANES), jnp.float32),
         ],
         compiler_params=pltpu.CompilerParams(vmem_limit_bytes=56 << 20),
-        name="block_one",
-    )(index, left, own, right, qkv, proj, up, down)
-
-
-def settle_kernel(place_ref, got_ref, serial_ref, pairs, table):
+        name="outer_block",
+    )(index, left, own, right, inner, qkv, proj, up, down)
+
+
+def settle_kernel(spans, place_ref, got_ref, *refs):
+    outs, (pairs, table) = refs[: len(spans)], refs[len(spans) :]
     slots = got_ref.shape[0]
-    rows = serial_ref.shape[0]
     capacity = place_ref.shape[1]
     for side in range(2):
         pairs[pl.ds(side, slots, stride=2), :] = got_ref[:, side * LANES : (side + 1) * LANES].astype(jnp.float32)
@@ -194,20 +254,21 @@
         return carry
 
     lax.fori_loop(0, place_ref.shape[0], body, 0)
-    for side in range(2):
-        serial_ref[:, side * LANES : (side + 1) * LANES] = table[pl.ds(8 + side, rows, stride=2), :].astype(
-            jnp.bfloat16
-        )
-
-
-def settle(place, got, rows):
+    for (first, count), out_ref in zip(spans, outs):
+        for side in range(2):
+            out_ref[:, side * LANES : (side + 1) * LANES] = table[
+                pl.ds(8 + 2 * first + side, count, stride=2), :
+            ].astype(jnp.bfloat16)
+
+
+def settle(place, got, rows, spans):
     slots, channels = got.shape
     vmem = pl.BlockSpec(memory_space=pltpu.VMEM)
     return pl.pallas_call(
-        settle_kernel,
-        out_shape=jax.ShapeDtypeStruct((rows, channels), jnp.bfloat16),
+        functools.partial(settle_kernel, spans),
+        out_shape=tuple(jax.ShapeDtypeStruct((count, channels), jnp.bfloat16) for _, count in spans),
         in_specs=[pl.BlockSpec(memory_space=pltpu.SMEM), vmem],
-        out_specs=vmem,
+        out_specs=(vmem,) * len(spans),
         scratch_shapes=[pltpu.VMEM((2 * slots, LANES), jnp.float32), pltpu.VMEM((2 * rows + 8, LANES), jnp.float32)],
         compiler_params=pltpu.CompilerParams(vmem_limit_bytes=56 << 20),
         name="settle",
@@ -335,19 +396,26 @@
     ring_down = [((i + 1) % devices, i) for i in range(devices)]
     before = lax.ppermute(points[row_count - half :], AXES, ring_up)
     behind = lax.ppermute(points[:half], AXES, ring_down)
+    inner = inner_block(points, qkv_one, proj_one, up_one, down_one)
+    inner, hilbert_device = lax.optimization_barrier((inner, hilbert_device))
     index, place = find_slots(hilbert_device, hilbert_position, devices, capacity)
     got_place = lax.all_to_all(place, AXES, split_axis=0, concat_axis=0, tiled=True)
-    send = block_one(index, before, points, behind, qkv_one, proj_one, up_one, down_one, devices * capacity)
+    send = outer_block(
+        index, before, points, behind, inner, qkv_one, proj_one, up_one, down_one, devices * capacity
+    )
     got = lax.all_to_all(
         send.reshape(devices, capacity, channels), AXES, split_axis=0, concat_axis=0, tiled=True
     )
-    serial = settle(got_place, got.reshape(devices * capacity, channels), row_count)
     segment = row_count // 8
     low, high = 3 * segment, 5 * segment
-    left_near = lax.ppermute(serial[low:], AXES, ring_up[:-1])
-    right_near = lax.ppermute(serial[:high], AXES, ring_down[:-1])
-    left_far = lax.ppermute(serial[:low], AXES, ring_up[:-1])
-    right_far = lax.ppermute(serial[high:], AXES, ring_down[:-1])
+    spans = ((0, row_count), (low, row_count - low), (0, high), (0, low), (high, row_count - high))
+    serial, upper_near, lower_near, lower_far, upper_far = settle(
+        got_place, got.reshape(devices * capacity, channels), row_count, spans
+    )
+    left_near = lax.ppermute(upper_near, AXES, ring_up[:-1])
+    right_near = lax.ppermute(lower_near, AXES, ring_down[:-1])
+    left_far = lax.ppermute(lower_far, AXES, ring_up[:-1])
+    right_far = lax.ppermute(upper_far, AXES, ring_down[:-1])
     parts = [left_near, serial, right_near]
     sources = [(low, row_count - low), (row_count, row_count), (2 * row_count, high)]
     inner = [(low, low + segment)]

time: 231 us -> 230 us (level)
  Pallas kernels: 120 us -> 125 us
  local copies, waits for them, and re-layouts: 11 us -> 7.77 us
  waiting for transfers between devices: 69.5 us -> 66.6 us
    pallas_call x2 -> x3, Pallas kernels: 60.3 us -> 64.7 us  [the longest x1 30.5 us: outer_block(): pl.pallas_call(outer_kernel, out_shape=jax.ShapeDtypeStruct((slots, chann...]
    slice x2 -> x0, local copies, waits for them, and re-layouts: 3.23 us -> none  [the longest x1 2.29 us: on_device(): right_near = lax.ppermute(serial[:high], AXES, ring_down[:-1])]
    all_to_all x1, starting transfers between devices: 7.16 us -> 4.34 us  [on_device(): lax.all_to_all(place, AXES, split_axis=0, concat_axis=0, tiled=True)]
    ppermute x1, waiting for transfers between devices: 2.74 us -> 0.01 us  [on_device(): before = lax.ppermute(points[row_count - half:], AXES, ring_up)]
    unnamed x20 -> x18, local copies, waits for them, and re-layouts: 4.99 us -> 5.02 us
  transfers between devices with their start and end apart: 8 -> 8, of which waited for: 4 -> 3; matrix products, arithmetic and copies ran while one was open for 1% -> 1% of each run, Pallas kernels for 31% -> 33%
where the time goes in v4:
time: 230 us; the launch traced here: 229 us
  Pallas kernels  125 us (54%)
  waiting for transfers between devices  66.6 us (29%)
  starting transfers between devices  29.7 us (13%)
  local copies, waits for them, and re-layouts  7.77 us (3%)
    pallas_call x2, Pallas kernels, position_conv(): pl.pallas_call(functools.partial(conv_kernel, segment, starts, stores, so...  57.8 us
    all_to_all x1, waiting for transfers between devices, on_device(): lax.all_to_all(send.reshape(devices, capacity, channels), AXES, split_axi...  48.2 us
    pallas_call x1, Pallas kernels, outer_block(): pl.pallas_call(outer_kernel, out_shape=jax.ShapeDtypeStruct((slots, chann...  30.5 us
    pallas_call x1, Pallas kernels, inner_block(): pl.pallas_call(inner_kernel, out_shape=jax.ShapeDtypeStruct((count, chann...  26.7 us
    ppermute x1, waiting for transfers between devices, on_device(): right_near = lax.ppermute(lower_near, AXES, ring_down[:-1])  14 us
    pallas_call x1, Pallas kernels, settle(): pl.pallas_call(functools.partial(settle_kernel, spans), out_shape=tuple((...  7.53 us
    all_to_all x1, starting transfers between devices, on_device(): lax.all_to_all(send.reshape(devices, capacity, channels), AXES, split_axi...  5.83 us
    ppermute x1, starting transfers between devices, on_device(): right_far = lax.ppermute(upper_far, AXES, ring_down[:-1])  5.44 us
  transfers between devices with their start and end apart: 8, of which 3 were waited for; matrix products, arithmetic and copies ran while one was open for 1% of the time, Pallas kernels for 33%

profile of v4, /device:TPU:1, one launch (start us, length us, event | category | flops | bytes accessed | tf_op | source)
XLA Modules:
  0.0 229.0 jit_solution(14305640862257127034)
XLA Ops:
  0.0 1.1 fusion.3
  1.1 2.2 collective-permute-start
  3.3 2.7 %collective-permute-start.1 = (bf16[512,256]{1,0:T(8,128)(2,1)S(1)}, bf16[512,256]{1,0:T(8,128)(2,1)S(1)}, u32[]{:S(2)}, u32[]{:S(2)}) collective-permute-start(bf16[512,256]{1,0:T(8,128)(2,1)S(1)} %get-tuple-element.23), channel_id=1, source_target_pairs={{1,0},{2,1},{3,2},{4,3},{5,4},{6,5},{7,6},{8,7},{9,8},{10,9},{11,1... | collective-permute-start | bytes 786440 | tf_op jit(solution)/shard_map/ppermute | solution.py:398
  5.9 26.7 %inner_block.1.inner_ref = bf16[1024,256]{1,0:T(8,128)(2,1)} custom-call(bf16[2048,256]{1,0:T(8,128)(2,1)} %own_ref.3, bf16[256,768]{1,0:T(8,128)(2,1)} %qkv_ref.3, bf16[256,256]{1,0:T(8,128)(2,1)} %proj_ref.3, bf16[256,1024]{1,0:T(8,128)(2,1)} %up_ref.3, bf16[1024,256]{1,0:T(8,128)(2,1)} %down_ref.3), custom_call_target="tpu_custom_call" | custom-call | tf_op jit(solution)/shard_map/inner_block/pallas_call | solution.py:204
  32.6 2.1 find_slots.1
  34.8 4.3 %all-to-all-start = ((s32[32,1,128]{2,1,0:T(1,128)}), s32[32,1,128]{2,1,0:T(1,128)S(1)}, u32[]{:S(2)}, u32[]{:S(2)}) async-start(s32[32,1,128]{2,1,0:T(1,128)} %bitcast.19), calls=%async_computation | async-start | bytes 32768 | tf_op jit(solution)/shard_map/all_to_all | solution.py:402
  39.1 0.0 collective-permute-done.left_ref
  39.1 0.0 copy-start.5
  39.1 0.0 collective-permute-done.1.right_ref
  39.1 0.0 copy-start.6
  39.2 0.7 copy-done.5
  39.8 0.1 copy-done.6
  39.9 30.5 %outer_block.1 = bf16[4096,256]{1,0:T(8,128)(2,1)} custom-call(s32[1,2048]{1,0:T(1,128)} %get-tuple-element.16.index_ref, bf16[512,256]{1,0:T(8,128)(2,1)} %copy-done.5, bf16[2048,256]{1,0:T(8,128)(2,1)} %own_ref.3, bf16[512,256]{1,0:T(8,128)(2,1)} %copy-done.6, bf16[1024,256]{1,0:T(8,128)(2,1)} %inner_block.1.inner_ref, bf16[256,768]{1,0:T(8,128)(2,1)} %qkv_ref.3, ...), custom_call_target="tpu_custom_call" | custom-call | tf_op jit(solution)/shard_map/outer_block/pallas_call | solution.py:224
  70.4 0.0 all-to-all-done
  70.4 0.0 copy-start.8
  70.4 0.0 copy-start.7
  70.4 0.6 copy-done.8
  71.0 5.8 %all-to-all-start.1 = ((bf16[32,128,256]{2,1,0:T(8,128)(2,1)}), bf16[32,128,256]{2,1,0:T(8,128)(2,1)S(1)}, u32[]{:S(2)}, u32[]{:S(2)}) async-start(bf16[32,128,256]{2,1,0:T(8,128)(2,1)} %bitcast.16), calls=%async_computation.1 | async-start | bytes 4194304 | tf_op jit(solution)/shard_map/all_to_all | solution.py:406
  76.8 0.0 copy-done.7
  76.9 48.2 %all-to-all-done.1 = bf16[32,128,256]{2,1,0:T(8,128)(2,1)S(1)} async-done(((bf16[32,128,256]{2,1,0:T(8,128)(2,1)}), bf16[32,128,256]{2,1,0:T(8,128)(2,1)S(1)}, u32[]{:S(2)}, u32[]{:S(2)}) %all-to-all-start.1) | async-done | bytes 2097184 | tf_op jit(solution)/shard_map/all_to_all | solution.py:406
  125.1 0.0 copy-start
  125.1 1.3 copy-done
  126.4 7.5 %settle.1 = (bf16[2048,256]{1,0:T(8,128)(2,1)}, bf16[1280,256]{1,0:T(8,128)(2,1)}, bf16[1280,256]{1,0:T(8,128)(2,1)}, bf16[768,256]{1,0:T(8,128)(2,1)}, bf16[768,256]{1,0:T(8,128)(2,1)}) custom-call(s32[32,128]{1,0:T(8,128)} %bitcast.18, bf16[4096,256]{1,0:T(8,128)(2,1)} %bitcast.15), custom_call_target="tpu_custom_call" | custom-call | tf_op jit(solution)/shard_map/settle/pallas_call | solution.py:267
  133.9 3.2 %collective-permute-start.2 = (bf16[1280,256]{1,0:T(8,128)(2,1)}, bf16[1280,256]{1,0:T(8,128)(2,1)S(1)}, u32[]{:S(2)}, u32[]{:S(2)}) collective-permute-start(bf16[1280,256]{1,0:T(8,128)(2,1)} %get-tuple-element.18), channel_id=1, source_target_pairs={{0,1},{1,2},{2,3},{3,4},{4,5},{5,6},{6,7},{7,8},{8,9},{9,10},{10,1... | collective-permute-start | bytes 1966088 | tf_op jit(solution)/shard_map/ppermute | solution.py:415
  137.1 4.1 %collective-permute-start.3 = (bf16[1280,256]{1,0:T(8,128)(2,1)}, bf16[1280,256]{1,0:T(8,128)(2,1)S(1)}, u32[]{:S(2)}, u32[]{:S(2)}) collective-permute-start(bf16[1280,256]{1,0:T(8,128)(2,1)} %get-tuple-element.20), channel_id=1, source_target_pairs={{1,0},{2,1},{3,2},{4,3},{5,4},{6,5},{7,6},{8,7},{9,8},{10,9},{11,1... | collective-permute-start | bytes 1966088 | tf_op jit(solution)/shard_map/ppermute | solution.py:416
  141.3 1.9 collective-permute-start.4
  143.2 5.4 %collective-permute-start.5 = (bf16[768,256]{1,0:T(8,128)(2,1)}, bf16[768,256]{1,0:T(8,128)(2,1)S(1)}, u32[]{:S(2)}, u32[]{:S(2)}) collective-permute-start(bf16[768,256]{1,0:T(8,128)(2,1)} %get-tuple-element.22), channel_id=1, source_target_pairs={{1,0},{2,1},{3,2},{4,3},{5,4},{6,5},{7,6},{8,7},{9,8},{10,9},{11,1... | collective-permute-start | bytes 1179656 | tf_op jit(solution)/shard_map/ppermute | solution.py:418
  148.7 0.7 reshape.33.index_ref
  149.4 0.1 reshape.26
  149.5 0.1 copy.13
  149.6 0.8 reshape.27.index_ref
  150.4 4.4 %collective-permute-done.2.refs_0_ = bf16[1280,256]{1,0:T(8,128)(2,1)S(1)} collective-permute-done((bf16[1280,256]{1,0:T(8,128)(2,1)}, bf16[1280,256]{1,0:T(8,128)(2,1)S(1)}, u32[]{:S(2)}, u32[]{:S(2)}) %collective-permute-start.2) | collective-permute-done | bytes 655392 | tf_op jit(solution)/shard_map/ppermute | solution.py:415
  154.9 0.0 copy-start.1
  154.9 14.0 %collective-permute-done.3.refs_2_ = bf16[1280,256]{1,0:T(8,128)(2,1)S(1)} collective-permute-done((bf16[1280,256]{1,0:T(8,128)(2,1)}, bf16[1280,256]{1,0:T(8,128)(2,1)S(1)}, u32[]{:S(2)}, u32[]{:S(2)}) %collective-permute-start.3) | collective-permute-done | bytes 655392 | tf_op jit(solution)/shard_map/ppermute | solution.py:416
  168.8 0.0 copy-start.2
  168.8 0.0 copy-done.1
  168.8 0.8 copy-done.2
  169.7 16.1 %position_conv.2.refs_5_ = bf16[512,256]{1,0:T(8,128)(2,1)} custom-call(s32[1,1,12288]{2,1,0:T(1,128)} %reshape.33.index_ref, bf16[1280,256]{1,0:T(8,128)(2,1)} %copy-done.1, bf16[2048,256]{1,0:T(8,128)(2,1)} %get-tuple-element.19.refs_1_, bf16[1280,256]{1,0:T(8,128)(2,1)} %copy-done.2, bf16[6912,256]{1,0:T(8,128)(2,1)} %refs_6_.1, bf16[256,256]{1,0:T(8,128)(2,1)} %refs_7_.1), custom_call_target="tpu_custom_call" | custom-call | tf_op jit(solution)/shard_map/position_conv/pallas_call | solution.py:361
  185.8 0.0 collective-permute-done.4.refs_3_
  185.8 0.0 copy-start.3
  185.8 0.0 collective-permute-done.5.refs_4_
  185.8 0.7 copy-done.3
  186.6 0.0 copy-start.4
  186.6 0.8 copy-done.4
  187.3 41.7 %position_conv.3 = bf16[2048,256]{1,0:T(8,128)(2,1)} custom-call(s32[3,1,12288]{2,1,0:T(1,128)} %reshape.27.index_ref, bf16[1280,256]{1,0:T(8,128)(2,1)} %copy-done.1, bf16[2048,256]{1,0:T(8,128)(2,1)} %get-tuple-element.19.refs_1_, bf16[1280,256]{1,0:T(8,128)(2,1)} %copy-done.2, bf16[768,256]{1,0:T(8,128)(2,1)} %copy-done.3, bf16[768,256]{1,0:T(8,128)(2,1)} %copy-done.4, ...), custom_call_target="tpu_custom_call" | custom-call | tf_op jit(solution)/shard_map/position_conv/pallas_call | solution.py:361
  (5 shorter events, 0.1 us)
Async XLA Ops:
  1.1 38.0 %collective-permute-start = (bf16[512,256]{1,0:T(8,128)(2,1)S(1)}, bf16[512,256]{1,0:T(8,128)(2,1)S(1)}, u32[]{:S(2)}, u32[]{:S(2)}) collective-permute-start(bf16[512,256]{1,0:T(8,128)(2,1)S(1)} %get-tuple-element.24), channel_id=1, source_target_pairs={{0,1},{1,2},{2,3},{3,4},{4,5},{5,6},{6,7},{7,8},{8,9},{9,10},{10,1... | collective-permute-start | bytes 786440 | tf_op jit(solution)/shard_map/ppermute | solution.py:397
  3.3 35.9 %collective-permute-start.1 = (bf16[512,256]{1,0:T(8,128)(2,1)S(1)}, bf16[512,256]{1,0:T(8,128)(2,1)S(1)}, u32[]{:S(2)}, u32[]{:S(2)}) collective-permute-start(bf16[512,256]{1,0:T(8,128)(2,1)S(1)} %get-tuple-element.23), channel_id=1, source_target_pairs={{1,0},{2,1},{3,2},{4,3},{5,4},{6,5},{7,6},{8,7},{9,8},{10,9},{11,1... | collective-permute-start | bytes 786440 | tf_op jit(solution)/shard_map/ppermute | solution.py:398
  34.8 35.6 %all-to-all-start = ((s32[32,1,128]{2,1,0:T(1,128)}), s32[32,1,128]{2,1,0:T(1,128)S(1)}, u32[]{:S(2)}, u32[]{:S(2)}) async-start(s32[32,1,128]{2,1,0:T(1,128)} %bitcast.19), calls=%async_computation | async-start | bytes 32768 | tf_op jit(solution)/shard_map/all_to_all | solution.py:402
  39.1 0.7 copy-start.5
  39.1 0.8 copy-start.6
  70.4 0.6 copy-start.8
  70.4 6.4 %copy-start.7 = (s32[2048,27]{0,1:T(8,128)S(1)}, s32[2048,27]{0,1:T(8,128)}, u32[]{:S(2)}) copy-start(s32[2048,27]{0,1:T(8,128)} %param.17) | copy-start | bytes 663556
  71.0 54.1 %all-to-all-start.1 = ((bf16[32,128,256]{2,1,0:T(8,128)(2,1)}), bf16[32,128,256]{2,1,0:T(8,128)(2,1)S(1)}, u32[]{:S(2)}, u32[]{:S(2)}) async-start(bf16[32,128,256]{2,1,0:T(8,128)(2,1)} %bitcast.16), calls=%async_computation.1 | async-start | bytes 4194304 | tf_op jit(solution)/shard_map/all_to_all | solution.py:406
  125.1 1.3 copy-start
  133.9 20.9 %collective-permute-start.2 = (bf16[1280,256]{1,0:T(8,128)(2,1)}, bf16[1280,256]{1,0:T(8,128)(2,1)S(1)}, u32[]{:S(2)}, u32[]{:S(2)}) collective-permute-start(bf16[1280,256]{1,0:T(8,128)(2,1)} %get-tuple-element.18), channel_id=1, source_target_pairs={{0,1},{1,2},{2,3},{3,4},{4,5},{5,6},{6,7},{7,8},{8,9},{9,10},{10,1... | collective-permute-start | bytes 1966088 | tf_op jit(solution)/shard_map/ppermute | solution.py:415
  137.1 31.7 %collective-permute-start.3 = (bf16[1280,256]{1,0:T(8,128)(2,1)}, bf16[1280,256]{1,0:T(8,128)(2,1)S(1)}, u32[]{:S(2)}, u32[]{:S(2)}) collective-permute-start(bf16[1280,256]{1,0:T(8,128)(2,1)} %get-tuple-element.20), channel_id=1, source_target_pairs={{1,0},{2,1},{3,2},{4,3},{5,4},{6,5},{7,6},{8,7},{9,8},{10,9},{11,1... | collective-permute-start | bytes 1966088 | tf_op jit(solution)/shard_map/ppermute | solution.py:416
  141.3 44.5 %collective-permute-start.4 = (bf16[768,256]{1,0:T(8,128)(2,1)}, bf16[768,256]{1,0:T(8,128)(2,1)S(1)}, u32[]{:S(2)}, u32[]{:S(2)}) collective-permute-start(bf16[768,256]{1,0:T(8,128)(2,1)} %get-tuple-element.21), channel_id=1, source_target_pairs={{0,1},{1,2},{2,3},{3,4},{4,5},{5,6},{6,7},{7,8},{8,9},{9,10},{10,1... | collective-permute-start | bytes 1179656 | tf_op jit(solution)/shard_map/ppermute | solution.py:417
  143.2 42.6 %collective-permute-start.5 = (bf16[768,256]{1,0:T(8,128)(2,1)}, bf16[768,256]{1,0:T(8,128)(2,1)S(1)}, u32[]{:S(2)}, u32[]{:S(2)}) collective-permute-start(bf16[768,256]{1,0:T(8,128)(2,1)} %get-tuple-element.22), channel_id=1, source_target_pairs={{1,0},{2,1},{3,2},{4,3},{5,4},{6,5},{7,6},{8,7},{9,8},{10,9},{11,1... | collective-permute-start | bytes 1179656 | tf_op jit(solution)/shard_map/ppermute | solution.py:418
  154.9 14.0 %copy-start.1 = (bf16[1280,256]{1,0:T(8,128)(2,1)}, bf16[1280,256]{1,0:T(8,128)(2,1)S(1)}, u32[]{:S(2)}) copy-start(bf16[1280,256]{1,0:T(8,128)(2,1)S(1)} %collective-permute-done.2.refs_0_) | copy-start | bytes 1966084
  168.8 0.9 copy-start.2
  185.8 0.7 copy-start.3
  186.6 0.8 copy-start.4

commit v5 on v4

--- a/solution.py
+++ b/solution.py
@@ -285,7 +285,7 @@
 def conv_kernel(segment, starts, stores, sources, kept, rows, index_ref, *refs):
     parts, refs = refs[: len(sources)], refs[len(sources) :]
     olds, refs = refs[: len(kept)], refs[len(kept) :]
-    weight_ref, linear_ref, out_ref, table, ping, pong, operand = refs
+    weight_ref, linear_ref, out_ref, table, ping, pong, summed = refs
     step = pl.program_id(0)
     width = out_ref.shape[1]
     offsets = weight_ref.shape[0] // width
@@ -293,6 +293,7 @@
     moved = offsets - 3
     block = 2 * segment
     sides = width // LANES
+    units = 2
 
     @pl.when(step == 0)
     def _():
@@ -307,38 +308,59 @@
 
     begins = [pl.multiple_of(pick(step, [pair[piece] for pair in starts]), segment) for piece in range(2)]
     ends = [pl.multiple_of(pick(step, [pair[piece] for pair in stores]), segment) for piece in range(2)]
-    for span, offset in enumerate((0, middle, offsets - 1)):
-        for piece, begin in enumerate(begins):
-            for side in range(sides):
-                operand[
-                    piece * segment : (piece + 1) * segment,
-                    offset * width + side * LANES : offset * width + (side + 1) * LANES,
-                ] = table[pl.ds(2 * (span * rows + begin) + side, segment, stride=2), :].astype(jnp.bfloat16)
 
     def fetch(order, buffer, row):
         for other in range(row, row + CHUNK):
             source = pl.multiple_of(index_ref[0, 0, order * block + other], 2)
             buffer[2 * other : 2 * other + 2, :] = table[pl.ds(source, 2), :]
 
-    def settle_columns(order, buffer, row):
-        offset = order + jnp.where(order < middle - 1, 1, 2)
-        column = pl.multiple_of(offset * width, width)
-        halves = [buffer[pl.ds(2 * row + side, CHUNK, stride=2), :].astype(jnp.bfloat16) for side in range(sides)]
-        operand[row : row + CHUNK, pl.ds(column, width)] = jnp.concatenate(halves, axis=1)
-
-    def body(pair, carry):
-        for turn, (filled, other) in enumerate(((ping, pong), (pong, ping))):
-            order = 2 * pair + turn
-            for row in range(0, block, CHUNK):
-                fetch(order, filled, row)
-                settle_columns(jnp.maximum(order - 1, 0), other, row)
-        return carry
-
-    lax.fori_loop(0, moved // 2, body, 0)
-    for row in range(0, block, CHUNK):
-        settle_columns(jnp.int32(moved - 1), pong, row)
-    conv = dot(operand[...], weight_ref[...]).astype(jnp.bfloat16)
-    normed = layer_norm(dot(conv, linear_ref[...]))
+    def moved_rows(buffer, row):
+        return [buffer[pl.ds(2 * row + side, CHUNK, stride=2), :] for side in range(sides)]
+
+    def span_rows(span, row):
+        begin = 2 * (span * rows + begins[row // segment] + row % segment)
+        return [table[pl.ds(begin + side, CHUNK, stride=2), :] for side in range(sides)]
+
+    def column(order):
+        return order + jnp.where(order < middle - 1, 1, 2)
+
+    def accumulate(*sums):
+        def stage(offset, staging, take, order=None, buffer=None):
+            weight = weight_ref[pl.ds(pl.multiple_of(offset * width, width), width), :]
+            for unit in range(units):
+                pltpu.matmul_push_rhs(weight, staging, unit)
+            for place, row in enumerate(range(0, block, CHUNK)):
+                if buffer is not None:
+                    fetch(order, buffer, row)
+                left = jnp.concatenate([half.astype(jnp.bfloat16) for half in take(row)], axis=1)
+                pltpu.matmul_acc_lhs(sums[place], left, load_staged_rhs=staging if place < units else None)
+
+        for place, row in enumerate(range(0, block, CHUNK)):
+            summed[row : row + CHUNK, :] = pltpu.matmul_pop(sums[place])
+        stage(0, 0, functools.partial(span_rows, 0), 0, ping)
+        stage(middle, 1, functools.partial(span_rows, 1))
+        stage(offsets - 1, 0, functools.partial(span_rows, 2))
+
+        def body(pair, carry):
+            order = 2 * pair
+            stage(column(order), 1, functools.partial(moved_rows, ping), order + 1, pong)
+            stage(column(order + 1), 0, functools.partial(moved_rows, pong), order + 2, ping)
+            return carry
+
+        lax.fori_loop(0, moved // 2 - 1, body, 0)
+        stage(column(jnp.int32(moved - 2)), 1, functools.partial(moved_rows, ping), moved - 1, pong)
+        stage(column(jnp.int32(moved - 1)), 0, functools.partial(moved_rows, pong))
+        for place, row in enumerate(range(0, block, CHUNK)):
+            if place < units:
+                pltpu.matmul_push_rhs(linear_ref[...], 1, place)
+            conv = pltpu.matmul_pop(sums[place]).astype(jnp.bfloat16)
+            pltpu.matmul_acc_lhs(sums[place], conv, load_staged_rhs=1 if place < units else None)
+        for place, row in enumerate(range(0, block, CHUNK)):
+            summed[row : row + CHUNK, :] = pltpu.matmul_pop(sums[place])
+
+    chunks = range(block // CHUNK)
+    pl.run_scoped(accumulate, *[pltpu.ACC(place % units)((CHUNK, width), jnp.float32) for place in chunks])
+    normed = layer_norm(summed[...])
     for piece in range(2):
         begin = 2 * (rows + begins[piece])
         own = [table[pl.ds(begin + side, segment, stride=2), :] for side in range(sides)]
@@ -369,9 +391,9 @@
             pltpu.VMEM((6 * rows + 8, LANES), jnp.float32),
             pltpu.VMEM((4 * segment, LANES), jnp.float32),
             pltpu.VMEM((4 * segment, LANES), jnp.float32),
-            pltpu.VMEM((2 * segment, offsets * channels), jnp.bfloat16),
+            pltpu.VMEM((2 * segment, channels), jnp.float32),
         ],
-        compiler_params=pltpu.CompilerParams(vmem_limit_bytes=56 << 20),
+        compiler_params=pltpu.CompilerParams(vmem_limit_bytes=20 << 20),
         name="position_conv",
     )(index, *parts, *olds, weight, linear)
 

time: 230 us -> 226 us (0.983)
  waiting for transfers between devices: 66.6 us -> 59 us
  local copies, waits for them, and re-layouts: 7.77 us -> 13.3 us
  Pallas kernels: 125 us -> 120 us
  other arithmetic: 0.08 us -> 2.93 us
    pallas_call x2, Pallas kernels: 57.8 us -> 52.6 us  [position_conv(): pl.pallas_call(functools.partial(conv_kernel, segment, starts, stores, so...]
    ppermute x1, waiting for transfers between devices: 4.44 us -> 0.01 us  [on_device(): left_near = lax.ppermute(upper_near, AXES, ring_up[:-1])]
    reshape x3, local copies, waits for them, and re-layouts: 1.62 us -> 4.92 us  [position_conv(): index.reshape(steps, 2 * segment, offsets - 3).transpose(0, 2, 1)]
    ppermute x1, waiting for transfers between devices: 14 us -> 11.5 us  [on_device(): right_near = lax.ppermute(lower_near, AXES, ring_down[:-1])]
    unnamed x18 -> x26, local copies, waits for them, and re-layouts: 5.02 us -> 5.64 us
  transfers between devices with their start and end apart: 8 -> 8, of which waited for: 3 -> 2; matrix products, arithmetic and copies ran while one was open for 1% -> 4% of each run, Pallas kernels for 33% -> 32%
where the time goes in v5:
time: 226 us; the launch traced here: 225 us
  Pallas kernels  120 us (53%)
  waiting for transfers between devices  59 us (26%)
  starting transfers between devices  29.7 us (13%)
  local copies, waits for them, and re-layouts  13.3 us (6%)
  other arithmetic  2.93 us (1%)
    pallas_call x2, Pallas kernels, position_conv(): pl.pallas_call(functools.partial(conv_kernel, segment, starts, stores, so...  52.6 us
    all_to_all x1, waiting for transfers between devices, on_device(): lax.all_to_all(send.reshape(devices, capacity, channels), AXES, split_axi...  47.5 us
    pallas_call x1, Pallas kernels, outer_block(): pl.pallas_call(outer_kernel, out_shape=jax.ShapeDtypeStruct((slots, chann...  30.5 us
    pallas_call x1, Pallas kernels, inner_block(): pl.pallas_call(inner_kernel, out_shape=jax.ShapeDtypeStruct((count, chann...  26.7 us
    ppermute x1, waiting for transfers between devices, on_device(): right_near = lax.ppermute(lower_near, AXES, ring_down[:-1])  11.5 us
    pallas_call x1, Pallas kernels, settle(): pl.pallas_call(functools.partial(settle_kernel, spans), out_shape=tuple((...  7.67 us
    all_to_all x1, starting transfers between devices, on_device(): lax.all_to_all(send.reshape(devices, capacity, channels), AXES, split_axi...  5.83 us
    unnamed x26, local copies, waits for them, and re-layouts  5.64 us
  transfers between devices with their start and end apart: 8, of which 2 were waited for; matrix products, arithmetic and copies ran while one was open for 4% of the time, Pallas kernels for 32%

profile of v5, /device:TPU:1, one launch (start us, length us, event | category | flops | bytes accessed | tf_op | source)
XLA Modules:
  0.0 224.7 jit_solution(16141740343981585137)
XLA Ops:
  0.0 1.1 fusion.3
  1.1 2.2 collective-permute-start
  3.3 2.7 %collective-permute-start.1 = (bf16[512,256]{1,0:T(8,128)(2,1)S(1)}, bf16[512,256]{1,0:T(8,128)(2,1)S(1)}, u32[]{:S(2)}, u32[]{:S(2)}) collective-permute-start(bf16[512,256]{1,0:T(8,128)(2,1)S(1)} %get-tuple-element.23), channel_id=1, source_target_pairs={{1,0},{2,1},{3,2},{4,3},{5,4},{6,5},{7,6},{8,7},{9,8},{10,9},{11,1... | collective-permute-start | bytes 786440 | tf_op jit(solution)/shard_map/ppermute | solution.py:420
  5.9 26.7 %inner_block.1.inner_ref = bf16[1024,256]{1,0:T(8,128)(2,1)} custom-call(bf16[2048,256]{1,0:T(8,128)(2,1)} %own_ref.3, bf16[256,768]{1,0:T(8,128)(2,1)} %qkv_ref.3, bf16[256,256]{1,0:T(8,128)(2,1)} %proj_ref.3, bf16[256,1024]{1,0:T(8,128)(2,1)} %up_ref.3, bf16[1024,256]{1,0:T(8,128)(2,1)} %down_ref.3), custom_call_target="tpu_custom_call" | custom-call | tf_op jit(solution)/shard_map/inner_block/pallas_call | solution.py:204
  32.6 2.2 find_slots.1
  34.8 4.3 %all-to-all-start = ((s32[32,1,128]{2,1,0:T(1,128)}), s32[32,1,128]{2,1,0:T(1,128)S(1)}, u32[]{:S(2)}, u32[]{:S(2)}) async-start(s32[32,1,128]{2,1,0:T(1,128)} %bitcast.19), calls=%async_computation | async-start | bytes 32768 | tf_op jit(solution)/shard_map/all_to_all | solution.py:424
  39.1 0.0 collective-permute-done.left_ref
  39.1 0.0 copy-start.9
  39.1 0.0 collective-permute-done.1.right_ref
  39.1 0.0 copy-start.10
  39.2 0.7 copy-done.9
  39.8 0.1 copy-done.10
  39.9 30.5 %outer_block.1 = bf16[4096,256]{1,0:T(8,128)(2,1)} custom-call(s32[1,2048]{1,0:T(1,128)} %get-tuple-element.16.index_ref, bf16[512,256]{1,0:T(8,128)(2,1)} %copy-done.9, bf16[2048,256]{1,0:T(8,128)(2,1)} %own_ref.3, bf16[512,256]{1,0:T(8,128)(2,1)} %copy-done.10, bf16[1024,256]{1,0:T(8,128)(2,1)} %inner_block.1.inner_ref, bf16[256,768]{1,0:T(8,128)(2,1)} %qkv_ref.3, ...), custom_call_target="tpu_custom_call" | custom-call | tf_op jit(solution)/shard_map/outer_block/pallas_call | solution.py:224
  70.4 0.0 all-to-all-done
  70.4 0.0 copy-start.12
  70.4 0.0 copy-start.11
  70.4 0.6 copy-done.12
  71.0 5.8 %all-to-all-start.1 = ((bf16[32,128,256]{2,1,0:T(8,128)(2,1)}), bf16[32,128,256]{2,1,0:T(8,128)(2,1)S(1)}, u32[]{:S(2)}, u32[]{:S(2)}) async-start(bf16[32,128,256]{2,1,0:T(8,128)(2,1)} %bitcast.16), calls=%async_computation.1 | async-start | bytes 4194304 | tf_op jit(solution)/shard_map/all_to_all | solution.py:428
  76.8 0.0 copy-done.11
  76.8 0.7 select_multiply_fusion
  77.6 47.5 %all-to-all-done.1 = bf16[32,128,256]{2,1,0:T(8,128)(2,1)S(1)} async-done(((bf16[32,128,256]{2,1,0:T(8,128)(2,1)}), bf16[32,128,256]{2,1,0:T(8,128)(2,1)S(1)}, u32[]{:S(2)}, u32[]{:S(2)}) %all-to-all-start.1) | async-done | bytes 2097184 | tf_op jit(solution)/shard_map/all_to_all | solution.py:428
  125.1 0.0 copy-start.5
  125.1 0.0 copy-start.8
  125.1 1.3 copy-done.5
  126.4 0.0 copy-start
  126.4 7.7 %settle.1 = (bf16[2048,256]{1,0:T(8,128)(2,1)}, bf16[1280,256]{1,0:T(8,128)(2,1)}, bf16[1280,256]{1,0:T(8,128)(2,1)}, bf16[768,256]{1,0:T(8,128)(2,1)}, bf16[768,256]{1,0:T(8,128)(2,1)}) custom-call(s32[32,128]{1,0:T(8,128)} %bitcast.18, bf16[4096,256]{1,0:T(8,128)(2,1)} %bitcast.15), custom_call_target="tpu_custom_call" | custom-call | tf_op jit(solution)/shard_map/settle/pallas_call | solution.py:267
  134.1 3.2 %collective-permute-start.2 = (bf16[1280,256]{1,0:T(8,128)(2,1)}, bf16[1280,256]{1,0:T(8,128)(2,1)}, u32[]{:S(2)}, u32[]{:S(2)}) collective-permute-start(bf16[1280,256]{1,0:T(8,128)(2,1)} %get-tuple-element.18), channel_id=1, source_target_pairs={{0,1},{1,2},{2,3},{3,4},{4,5},{5,6},{6,7},{7,8},{8,9},{9,10},{10,1... | collective-permute-start | bytes 1966088 | tf_op jit(solution)/shard_map/ppermute | solution.py:437
  137.3 4.1 %collective-permute-start.3 = (bf16[1280,256]{1,0:T(8,128)(2,1)}, bf16[1280,256]{1,0:T(8,128)(2,1)}, u32[]{:S(2)}, u32[]{:S(2)}) collective-permute-start(bf16[1280,256]{1,0:T(8,128)(2,1)} %get-tuple-element.20), channel_id=1, source_target_pairs={{1,0},{2,1},{3,2},{4,3},{5,4},{6,5},{7,6},{8,7},{9,8},{10,9},{11,1... | collective-permute-start | bytes 1966088 | tf_op jit(solution)/shard_map/ppermute | solution.py:438
  141.5 0.0 copy-done.8
  141.5 0.0 copy-start.6
  141.5 0.0 copy-start.7
  141.5 1.9 collective-permute-start.4
  143.4 5.4 %collective-permute-start.5 = (bf16[768,256]{1,0:T(8,128)(2,1)}, bf16[768,256]{1,0:T(8,128)(2,1)}, u32[]{:S(2)}, u32[]{:S(2)}) collective-permute-start(bf16[768,256]{1,0:T(8,128)(2,1)} %get-tuple-element.22), channel_id=1, source_target_pairs={{1,0},{2,1},{3,2},{4,3},{5,4},{6,5},{7,6},{8,7},{9,8},{10,9},{11,1... | collective-permute-start | bytes 1179656 | tf_op jit(solution)/shard_map/ppermute | solution.py:440
  148.9 0.0 copy-done.6
  148.9 0.0 copy-done.7
  148.9 0.6 fusion.2
  149.5 1.5 reshape.33.index_ref
  151.0 0.9 fusion.1
  151.9 0.7 pad_add_fusion
  152.6 1.7 reshape.26
  154.3 1.6 copy.13
  155.9 1.7 reshape.27.index_ref
  157.7 0.0 collective-permute-done.2.refs_0_
  157.7 11.5 %collective-permute-done.3.refs_2_ = bf16[1280,256]{1,0:T(8,128)(2,1)} collective-permute-done((bf16[1280,256]{1,0:T(8,128)(2,1)}, bf16[1280,256]{1,0:T(8,128)(2,1)}, u32[]{:S(2)}, u32[]{:S(2)}) %collective-permute-start.3) | collective-permute-done | bytes 655392 | tf_op jit(solution)/shard_map/ppermute | solution.py:438
  169.1 0.0 copy-done
  169.1 0.0 copy-start.1
  169.1 1.2 copy-done.1
  170.3 0.0 copy-start.3
  170.3 0.9 copy-done.3
  171.2 0.0 copy-start.4
  171.2 0.8 copy-done.4
  172.0 0.0 copy-start.2
  172.0 13.3 %position_conv.2.refs_5_ = bf16[512,256]{1,0:T(8,128)(2,1)S(1)} custom-call(s32[1,1,12288]{2,1,0:T(1,128)S(1)} %copy-done.4, bf16[1280,256]{1,0:T(8,128)(2,1)} %collective-permute-done.2.refs_0_, bf16[2048,256]{1,0:T(8,128)(2,1)S(1)} %copy-done.1, bf16[1280,256]{1,0:T(8,128)(2,1)} %collective-permute-done.3.refs_2_, bf16[6912,256]{1,0:T(8,128)(2,1)S(1)} %copy-done, ...), custom_call_target="tpu_custom_call" | custom-call | tf_op jit(solution)/shard_map/position_conv/pallas_call | solution.py:383
  185.4 0.0 collective-permute-done.4.refs_3_
  185.4 0.0 collective-permute-done.5.refs_4_
  185.4 0.0 copy-done.2
  185.4 39.3 %position_conv.3 = bf16[2048,256]{1,0:T(8,128)(2,1)} custom-call(s32[3,1,12288]{2,1,0:T(1,128)S(1)} %copy-done.2, bf16[1280,256]{1,0:T(8,128)(2,1)} %collective-permute-done.2.refs_0_, bf16[2048,256]{1,0:T(8,128)(2,1)S(1)} %copy-done.1, bf16[1280,256]{1,0:T(8,128)(2,1)} %collective-permute-done.3.refs_2_, bf16[768,256]{1,0:T(8,128)(2,1)} %collective-permute-done.4.refs_3_, ...), custom_call_target="tpu_custom_call" | custom-call | tf_op jit(solution)/shard_map/position_conv/pallas_call | solution.py:383
  (1 shorter events, 0.0 us)
Async XLA Ops:
  1.1 38.1 %collective-permute-start = (bf16[512,256]{1,0:T(8,128)(2,1)S(1)}, bf16[512,256]{1,0:T(8,128)(2,1)S(1)}, u32[]{:S(2)}, u32[]{:S(2)}) collective-permute-start(bf16[512,256]{1,0:T(8,128)(2,1)S(1)} %get-tuple-element.24), channel_id=1, source_target_pairs={{0,1},{1,2},{2,3},{3,4},{4,5},{5,6},{6,7},{7,8},{8,9},{9,10},{10,1... | collective-permute-start | bytes 786440 | tf_op jit(solution)/shard_map/ppermute | solution.py:419
  3.3 35.9 %collective-permute-start.1 = (bf16[512,256]{1,0:T(8,128)(2,1)S(1)}, bf16[512,256]{1,0:T(8,128)(2,1)S(1)}, u32[]{:S(2)}, u32[]{:S(2)}) collective-permute-start(bf16[512,256]{1,0:T(8,128)(2,1)S(1)} %get-tuple-element.23), channel_id=1, source_target_pairs={{1,0},{2,1},{3,2},{4,3},{5,4},{6,5},{7,6},{8,7},{9,8},{10,9},{11,1... | collective-permute-start | bytes 786440 | tf_op jit(solution)/shard_map/ppermute | solution.py:420
  34.8 35.6 %all-to-all-start = ((s32[32,1,128]{2,1,0:T(1,128)}), s32[32,1,128]{2,1,0:T(1,128)S(1)}, u32[]{:S(2)}, u32[]{:S(2)}) async-start(s32[32,1,128]{2,1,0:T(1,128)} %bitcast.19), calls=%async_computation | async-start | bytes 32768 | tf_op jit(solution)/shard_map/all_to_all | solution.py:424
  39.1 0.7 copy-start.9
  39.1 0.8 copy-start.10
  70.4 0.6 copy-start.12
  70.4 6.4 %copy-start.11 = (s32[2048,27]{0,1:T(8,128)S(1)}, s32[2048,27]{0,1:T(8,128)}, u32[]{:S(2)}) copy-start(s32[2048,27]{0,1:T(8,128)} %param.17) | copy-start | bytes 663556
  71.0 54.1 %all-to-all-start.1 = ((bf16[32,128,256]{2,1,0:T(8,128)(2,1)}), bf16[32,128,256]{2,1,0:T(8,128)(2,1)S(1)}, u32[]{:S(2)}, u32[]{:S(2)}) async-start(bf16[32,128,256]{2,1,0:T(8,128)(2,1)} %bitcast.16), calls=%async_computation.1 | async-start | bytes 4194304 | tf_op jit(solution)/shard_map/all_to_all | solution.py:428
  125.1 1.3 copy-start.5
  125.1 16.4 %copy-start.8 = (s32[2048,27]{0,1:T(8,128)S(1)}, s32[2048,27]{0,1:T(8,128)}, u32[]{:S(2)}) copy-start(s32[2048,27]{0,1:T(8,128)} %select_multiply_fusion) | copy-start | bytes 663556
  126.4 42.7 %copy-start = (bf16[6912,256]{1,0:T(8,128)(2,1)S(1)}, bf16[6912,256]{1,0:T(8,128)(2,1)}, u32[]{:S(2)}) copy-start(bf16[6912,256]{1,0:T(8,128)(2,1)} %refs_6_.1) | copy-start | bytes 10616836
  134.1 23.6 %collective-permute-start.2 = (bf16[1280,256]{1,0:T(8,128)(2,1)}, bf16[1280,256]{1,0:T(8,128)(2,1)}, u32[]{:S(2)}, u32[]{:S(2)}) collective-permute-start(bf16[1280,256]{1,0:T(8,128)(2,1)} %get-tuple-element.18), channel_id=1, source_target_pairs={{0,1},{1,2},{2,3},{3,4},{4,5},{5,6},{6,7},{7,8},{8,9},{9,10},{10,1... | collective-permute-start | bytes 1966088 | tf_op jit(solution)/shard_map/ppermute | solution.py:437
  137.3 31.8 %collective-permute-start.3 = (bf16[1280,256]{1,0:T(8,128)(2,1)}, bf16[1280,256]{1,0:T(8,128)(2,1)}, u32[]{:S(2)}, u32[]{:S(2)}) collective-permute-start(bf16[1280,256]{1,0:T(8,128)(2,1)} %get-tuple-element.20), channel_id=1, source_target_pairs={{1,0},{2,1},{3,2},{4,3},{5,4},{6,5},{7,6},{8,7},{9,8},{10,9},{11,1... | collective-permute-start | bytes 1966088 | tf_op jit(solution)/shard_map/ppermute | solution.py:438
  141.5 7.4 %copy-start.6 = (s32[2048,12]{0,1:T(8,128)}, s32[2048,12]{0,1:T(8,128)S(1)}, u32[]{:S(2)}) copy-start(s32[2048,12]{0,1:T(8,128)S(1)} %get-tuple-element.27) | copy-start | bytes 294916
  141.5 7.4 %copy-start.7 = (s32[2048,12]{0,1:T(8,128)}, s32[2048,12]{0,1:T(8,128)S(1)}, u32[]{:S(2)}) copy-start(s32[2048,12]{0,1:T(8,128)S(1)} %get-tuple-element.28) | copy-start | bytes 294916
  141.5 43.9 %collective-permute-start.4 = (bf16[768,256]{1,0:T(8,128)(2,1)}, bf16[768,256]{1,0:T(8,128)(2,1)}, u32[]{:S(2)}, u32[]{:S(2)}) collective-permute-start(bf16[768,256]{1,0:T(8,128)(2,1)} %get-tuple-element.21), channel_id=1, source_target_pairs={{0,1},{1,2},{2,3},{3,4},{4,5},{5,6},{6,7},{7,8},{8,9},{9,10},{10,1... | collective-permute-start | bytes 1179656 | tf_op jit(solution)/shard_map/ppermute | solution.py:439
  143.4 42.0 %collective-permute-start.5 = (bf16[768,256]{1,0:T(8,128)(2,1)}, bf16[768,256]{1,0:T(8,128)(2,1)}, u32[]{:S(2)}, u32[]{:S(2)}) collective-permute-start(bf16[768,256]{1,0:T(8,128)(2,1)} %get-tuple-element.22), channel_id=1, source_target_pairs={{1,0},{2,1},{3,2},{4,3},{5,4},{6,5},{7,6},{8,7},{9,8},{10,9},{11,1... | collective-permute-start | bytes 1179656 | tf_op jit(solution)/shard_map/ppermute | solution.py:440
  169.1 1.2 copy-start.1
  170.3 0.9 copy-start.3
  171.2 0.8 copy-start.4
  172.0 13.4 %copy-start.2 = (s32[3,1,12288]{2,1,0:T(1,128)S(1)}, s32[3,1,12288]{2,1,0:T(1,128)}, u32[]{:S(2)}) copy-start(s32[3,1,12288]{2,1,0:T(1,128)} %reshape.27.index_ref) | copy-start | bytes 442372

commit v6 on v5

--- a/solution.py
+++ b/solution.py
@@ -101,15 +101,18 @@
         keys = key[lanes, pl.ds(start, PATCH)]
         values = value[pl.ds(start, PATCH), lanes]
         total = None
-        for head in range(per_group):
-            mine = head_of == head
-            scores = dot(jnp.where(mine, queries, jnp.zeros_like(queries)), keys)
-            peak = jnp.max(scores, axis=1, keepdims=True)
-            weights = jnp.exp2((scores - peak) * scale).astype(jnp.bfloat16)
-            ones = jnp.broadcast_to(mine.astype(jnp.float32).astype(jnp.bfloat16), values.shape)
-            both = jnp.concatenate([jnp.where(mine, values, jnp.zeros_like(values)), ones], axis=1)
-            result = dot(weights, both)
-            total = result if total is None else total + result
+        for head in range(0, per_group, 2):
+            masks = [head_of == head + turn for turn in range(2)]
+            stacked = jnp.concatenate([jnp.where(mine, queries, jnp.zeros_like(queries)) for mine in masks], axis=0)
+            both_scores = dot(stacked, keys)
+            for turn, mine in enumerate(masks):
+                scores = both_scores[turn * half : (turn + 1) * half]
+                peak = jnp.max(scores, axis=1, keepdims=True)
+                weights = jnp.exp2((scores - peak) * scale).astype(jnp.bfloat16)
+                ones = jnp.broadcast_to(mine.astype(jnp.float32).astype(jnp.bfloat16), values.shape)
+                both = jnp.concatenate([jnp.where(mine, values, jnp.zeros_like(values)), ones], axis=1)
+                result = dot(weights, both)
+                total = result if total is None else total + result
         pieces.append((total[:, :LANES] / total[:, LANES:]).astype(jnp.bfloat16))
     mixed = jnp.concatenate(pieces, axis=1)
     after = (residual.astype(jnp.float32) + dot(mixed, proj_ref[...])).astype(jnp.bfloat16)
@@ -241,35 +244,50 @@
 
 def settle_kernel(spans, place_ref, got_ref, *refs):
     outs, (pairs, table) = refs[: len(spans)], refs[len(spans) :]
+    step = pl.program_id(0)
     slots = got_ref.shape[0]
     capacity = place_ref.shape[1]
+    sources = slots // capacity
     for side in range(2):
         pairs[pl.ds(side, slots, stride=2), :] = got_ref[:, side * LANES : (side + 1) * LANES].astype(jnp.float32)
 
     def body(source, carry):
         base = pl.multiple_of(source * (2 * capacity), 2 * capacity)
         for slot in range(capacity):
-            target = pl.multiple_of(place_ref[source, slot] + 6, 2)
+            target = pl.multiple_of(place_ref[step * sources + source, slot] + 6, 2)
             table[pl.ds(target, 2), :] = pairs[pl.ds(base + 2 * slot, 2), :]
         return carry
 
-    lax.fori_loop(0, place_ref.shape[0], body, 0)
-    for (first, count), out_ref in zip(spans, outs):
+    lax.fori_loop(0, sources, body, 0)
+
+    @pl.when(step == pl.num_programs(0) - 1)
+    def _():
+        whole = outs[0]
         for side in range(2):
-            out_ref[:, side * LANES : (side + 1) * LANES] = table[
-                pl.ds(8 + 2 * first + side, count, stride=2), :
+            whole[:, side * LANES : (side + 1) * LANES] = table[
+                pl.ds(8 + side, whole.shape[0], stride=2), :
             ].astype(jnp.bfloat16)
+        for (first, count), out_ref in zip(spans[1:], outs[1:]):
+            out_ref[...] = whole[first : first + count, :]
 
 
 def settle(place, got, rows, spans):
     slots, channels = got.shape
+    steps = 8
     vmem = pl.BlockSpec(memory_space=pltpu.VMEM)
     return pl.pallas_call(
         functools.partial(settle_kernel, spans),
         out_shape=tuple(jax.ShapeDtypeStruct((count, channels), jnp.bfloat16) for _, count in spans),
-        in_specs=[pl.BlockSpec(memory_space=pltpu.SMEM), vmem],
+        grid=(steps,),
+        in_specs=[
+            pl.BlockSpec(memory_space=pltpu.SMEM),
+            pl.BlockSpec((slots // steps, channels), lambda step: (step, 0)),
+        ],
         out_specs=(vmem,) * len(spans),
-        scratch_shapes=[pltpu.VMEM((2 * slots, LANES), jnp.float32), pltpu.VMEM((2 * rows + 8, LANES), jnp.float32)],
+        scratch_shapes=[
+            pltpu.VMEM((2 * slots // steps, LANES), jnp.float32),
+            pltpu.VMEM((2 * rows + 8, LANES), jnp.float32),
+        ],
         compiler_params=pltpu.CompilerParams(vmem_limit_bytes=56 << 20),
         name="settle",
     )(place, got)

time: 226 us -> 227 us (level)
  no operation moved by 1% of the time
where the time goes in v6:
time: 227 us; the launch traced here: 226 us
  Pallas kernels  121 us (53%)
  waiting for transfers between devices  59 us (26%)
  starting transfers between devices  29.7 us (13%)
  local copies, waits for them, and re-layouts  13.3 us (6%)
  other arithmetic  2.93 us (1%)
    pallas_call x2, Pallas kernels, position_conv(): pl.pallas_call(functools.partial(conv_kernel, segment, starts, stores, so...  52.5 us
    all_to_all x1, waiting for transfers between devices, on_device(): lax.all_to_all(send.reshape(devices, capacity, channels), AXES, split_axi...  47.5 us
    pallas_call x1, Pallas kernels, outer_block(): pl.pallas_call(outer_kernel, out_shape=jax.ShapeDtypeStruct((slots, chann...  30.6 us
    pallas_call x1, Pallas kernels, inner_block(): pl.pallas_call(inner_kernel, out_shape=jax.ShapeDtypeStruct((count, chann...  26.9 us
    ppermute x1, waiting for transfers between devices, on_device(): right_near = lax.ppermute(lower_near, AXES, ring_down[:-1])  11.5 us
    pallas_call x1, Pallas kernels, settle(): pl.pallas_call(functools.partial(settle_kernel, spans), out_shape=tuple((...  8.42 us
    all_to_all x1, starting transfers between devices, on_device(): lax.all_to_all(send.reshape(devices, capacity, channels), AXES, split_axi...  5.83 us
    unnamed x26, local copies, waits for them, and re-layouts  5.64 us
  transfers between devices with their start and end apart: 8, of which 2 were waited for; matrix products, arithmetic and copies ran while one was open for 4% of the time, Pallas kernels for 32%

profile of v6, /device:TPU:1, one launch (start us, length us, event | category | flops | bytes accessed | tf_op | source)
XLA Modules:
  0.0 225.7 jit_solution(11931273776613325349)
XLA Ops:
  0.0 1.1 fusion.3
  1.1 2.2 collective-permute-start
  3.3 2.7 %collective-permute-start.1 = (bf16[512,256]{1,0:T(8,128)(2,1)S(1)}, bf16[512,256]{1,0:T(8,128)(2,1)S(1)}, u32[]{:S(2)}, u32[]{:S(2)}) collective-permute-start(bf16[512,256]{1,0:T(8,128)(2,1)S(1)} %get-tuple-element.23), channel_id=1, source_target_pairs={{1,0},{2,1},{3,2},{4,3},{5,4},{6,5},{7,6},{8,7},{9,8},{10,9},{11,1... | collective-permute-start | bytes 786440 | tf_op jit(solution)/shard_map/ppermute | solution.py:438
  5.9 26.9 %inner_block.1.inner_ref = bf16[1024,256]{1,0:T(8,128)(2,1)} custom-call(bf16[2048,256]{1,0:T(8,128)(2,1)} %own_ref.3, bf16[256,768]{1,0:T(8,128)(2,1)} %qkv_ref.3, bf16[256,256]{1,0:T(8,128)(2,1)} %proj_ref.3, bf16[256,1024]{1,0:T(8,128)(2,1)} %up_ref.3, bf16[1024,256]{1,0:T(8,128)(2,1)} %down_ref.3), custom_call_target="tpu_custom_call" | custom-call | tf_op jit(solution)/shard_map/inner_block/pallas_call | solution.py:207
  32.8 2.2 find_slots.1
  34.9 4.3 %all-to-all-start = ((s32[32,1,128]{2,1,0:T(1,128)}), s32[32,1,128]{2,1,0:T(1,128)S(1)}, u32[]{:S(2)}, u32[]{:S(2)}) async-start(s32[32,1,128]{2,1,0:T(1,128)} %bitcast.19), calls=%async_computation | async-start | bytes 32768 | tf_op jit(solution)/shard_map/all_to_all | solution.py:442
  39.3 0.0 collective-permute-done.left_ref
  39.3 0.0 copy-start.9
  39.3 0.0 collective-permute-done.1.right_ref
  39.3 0.0 copy-start.10
  39.3 0.7 copy-done.9
  40.0 0.1 copy-done.10
  40.1 30.6 %outer_block.1 = bf16[4096,256]{1,0:T(8,128)(2,1)} custom-call(s32[1,2048]{1,0:T(1,128)} %get-tuple-element.16.index_ref, bf16[512,256]{1,0:T(8,128)(2,1)} %copy-done.9, bf16[2048,256]{1,0:T(8,128)(2,1)} %own_ref.3, bf16[512,256]{1,0:T(8,128)(2,1)} %copy-done.10, bf16[1024,256]{1,0:T(8,128)(2,1)} %inner_block.1.inner_ref, bf16[256,768]{1,0:T(8,128)(2,1)} %qkv_ref.3, ...), custom_call_target="tpu_custom_call" | custom-call | tf_op jit(solution)/shard_map/outer_block/pallas_call | solution.py:227
  70.7 0.0 all-to-all-done
  70.7 0.0 copy-start.12
  70.7 0.0 copy-start.11
  70.7 0.6 copy-done.12
  71.3 5.8 %all-to-all-start.1 = ((bf16[32,128,256]{2,1,0:T(8,128)(2,1)}), bf16[32,128,256]{2,1,0:T(8,128)(2,1)S(1)}, u32[]{:S(2)}, u32[]{:S(2)}) async-start(bf16[32,128,256]{2,1,0:T(8,128)(2,1)} %bitcast.16), calls=%async_computation.1 | async-start | bytes 4194304 | tf_op jit(solution)/shard_map/all_to_all | solution.py:446
  77.2 0.0 copy-done.11
  77.2 0.7 select_multiply_fusion
  77.9 47.5 %all-to-all-done.1 = bf16[32,128,256]{2,1,0:T(8,128)(2,1)S(1)} async-done(((bf16[32,128,256]{2,1,0:T(8,128)(2,1)}), bf16[32,128,256]{2,1,0:T(8,128)(2,1)S(1)}, u32[]{:S(2)}, u32[]{:S(2)}) %all-to-all-start.1) | async-done | bytes 2097184 | tf_op jit(solution)/shard_map/all_to_all | solution.py:446
  125.4 0.0 copy-start.5
  125.4 0.0 copy-start.8
  125.4 1.3 copy-done.5
  126.8 0.0 copy-start
  126.8 8.4 %settle.1 = (bf16[2048,256]{1,0:T(8,128)(2,1)}, bf16[1280,256]{1,0:T(8,128)(2,1)}, bf16[1280,256]{1,0:T(8,128)(2,1)}, bf16[768,256]{1,0:T(8,128)(2,1)}, bf16[768,256]{1,0:T(8,128)(2,1)}) custom-call(s32[32,128]{1,0:T(8,128)} %bitcast.18, bf16[4096,256]{1,0:T(8,128)(2,1)} %bitcast.15), custom_call_target="tpu_custom_call" | custom-call | tf_op jit(solution)/shard_map/settle/pallas_call | solution.py:278
  135.2 3.2 %collective-permute-start.2 = (bf16[1280,256]{1,0:T(8,128)(2,1)}, bf16[1280,256]{1,0:T(8,128)(2,1)}, u32[]{:S(2)}, u32[]{:S(2)}) collective-permute-start(bf16[1280,256]{1,0:T(8,128)(2,1)} %get-tuple-element.18), channel_id=1, source_target_pairs={{0,1},{1,2},{2,3},{3,4},{4,5},{5,6},{6,7},{7,8},{8,9},{9,10},{10,1... | collective-permute-start | bytes 1966088 | tf_op jit(solution)/shard_map/ppermute | solution.py:455
  138.4 4.1 %collective-permute-start.3 = (bf16[1280,256]{1,0:T(8,128)(2,1)}, bf16[1280,256]{1,0:T(8,128)(2,1)}, u32[]{:S(2)}, u32[]{:S(2)}) collective-permute-start(bf16[1280,256]{1,0:T(8,128)(2,1)} %get-tuple-element.20), channel_id=1, source_target_pairs={{1,0},{2,1},{3,2},{4,3},{5,4},{6,5},{7,6},{8,7},{9,8},{10,9},{11,1... | collective-permute-start | bytes 1966088 | tf_op jit(solution)/shard_map/ppermute | solution.py:456
  142.5 0.0 copy-done.8
  142.6 0.0 copy-start.6
  142.6 0.0 copy-start.7
  142.6 1.9 collective-permute-start.4
  144.5 5.4 %collective-permute-start.5 = (bf16[768,256]{1,0:T(8,128)(2,1)}, bf16[768,256]{1,0:T(8,128)(2,1)}, u32[]{:S(2)}, u32[]{:S(2)}) collective-permute-start(bf16[768,256]{1,0:T(8,128)(2,1)} %get-tuple-element.22), channel_id=1, source_target_pairs={{1,0},{2,1},{3,2},{4,3},{5,4},{6,5},{7,6},{8,7},{9,8},{10,9},{11,1... | collective-permute-start | bytes 1179656 | tf_op jit(solution)/shard_map/ppermute | solution.py:458
  150.0 0.0 copy-done.6
  150.0 0.0 copy-done.7
  150.0 0.6 fusion.2
  150.6 1.5 reshape.33.index_ref
  152.1 0.9 fusion.1
  153.0 0.7 pad_add_fusion
  153.7 1.7 reshape.26
  155.4 1.6 copy.13
  157.0 1.7 reshape.27.index_ref
  158.7 0.0 collective-permute-done.2.refs_0_
  158.7 11.5 %collective-permute-done.3.refs_2_ = bf16[1280,256]{1,0:T(8,128)(2,1)} collective-permute-done((bf16[1280,256]{1,0:T(8,128)(2,1)}, bf16[1280,256]{1,0:T(8,128)(2,1)}, u32[]{:S(2)}, u32[]{:S(2)}) %collective-permute-start.3) | collective-permute-done | bytes 655392 | tf_op jit(solution)/shard_map/ppermute | solution.py:456
  170.2 0.0 copy-done
  170.2 0.0 copy-start.1
  170.2 1.2 copy-done.1
  171.4 0.0 copy-start.3
  171.4 0.9 copy-done.3
  172.3 0.0 copy-start.4
  172.3 0.8 copy-done.4
  173.1 0.0 copy-start.2
  173.1 13.3 %position_conv.2.refs_5_ = bf16[512,256]{1,0:T(8,128)(2,1)S(1)} custom-call(s32[1,1,12288]{2,1,0:T(1,128)S(1)} %copy-done.4, bf16[1280,256]{1,0:T(8,128)(2,1)} %collective-permute-done.2.refs_0_, bf16[2048,256]{1,0:T(8,128)(2,1)S(1)} %copy-done.1, bf16[1280,256]{1,0:T(8,128)(2,1)} %collective-permute-done.3.refs_2_, bf16[6912,256]{1,0:T(8,128)(2,1)S(1)} %copy-done, ...), custom_call_target="tpu_custom_call" | custom-call | tf_op jit(solution)/shard_map/position_conv/pallas_call | solution.py:401
  186.5 0.0 collective-permute-done.4.refs_3_
  186.5 0.0 collective-permute-done.5.refs_4_
  186.5 0.0 copy-done.2
  186.5 39.2 %position_conv.3 = bf16[2048,256]{1,0:T(8,128)(2,1)} custom-call(s32[3,1,12288]{2,1,0:T(1,128)S(1)} %copy-done.2, bf16[1280,256]{1,0:T(8,128)(2,1)} %collective-permute-done.2.refs_0_, bf16[2048,256]{1,0:T(8,128)(2,1)S(1)} %copy-done.1, bf16[1280,256]{1,0:T(8,128)(2,1)} %collective-permute-done.3.refs_2_, bf16[768,256]{1,0:T(8,128)(2,1)} %collective-permute-done.4.refs_3_, ...), custom_call_target="tpu_custom_call" | custom-call | tf_op jit(solution)/shard_map/position_conv/pallas_call | solution.py:401
  (1 shorter events, 0.0 us)
Async XLA Ops:
  1.1 38.2 %collective-permute-start = (bf16[512,256]{1,0:T(8,128)(2,1)S(1)}, bf16[512,256]{1,0:T(8,128)(2,1)S(1)}, u32[]{:S(2)}, u32[]{:S(2)}) collective-permute-start(bf16[512,256]{1,0:T(8,128)(2,1)S(1)} %get-tuple-element.24), channel_id=1, source_target_pairs={{0,1},{1,2},{2,3},{3,4},{4,5},{5,6},{6,7},{7,8},{8,9},{9,10},{10,1... | collective-permute-start | bytes 786440 | tf_op jit(solution)/shard_map/ppermute | solution.py:437
  3.3 36.0 %collective-permute-start.1 = (bf16[512,256]{1,0:T(8,128)(2,1)S(1)}, bf16[512,256]{1,0:T(8,128)(2,1)S(1)}, u32[]{:S(2)}, u32[]{:S(2)}) collective-permute-start(bf16[512,256]{1,0:T(8,128)(2,1)S(1)} %get-tuple-element.23), channel_id=1, source_target_pairs={{1,0},{2,1},{3,2},{4,3},{5,4},{6,5},{7,6},{8,7},{9,8},{10,9},{11,1... | collective-permute-start | bytes 786440 | tf_op jit(solution)/shard_map/ppermute | solution.py:438
  34.9 35.8 %all-to-all-start = ((s32[32,1,128]{2,1,0:T(1,128)}), s32[32,1,128]{2,1,0:T(1,128)S(1)}, u32[]{:S(2)}, u32[]{:S(2)}) async-start(s32[32,1,128]{2,1,0:T(1,128)} %bitcast.19), calls=%async_computation | async-start | bytes 32768 | tf_op jit(solution)/shard_map/all_to_all | solution.py:442
  39.3 0.7 copy-start.9
  39.3 0.8 copy-start.10
  70.7 0.6 copy-start.12
  70.7 6.4 %copy-start.11 = (s32[2048,27]{0,1:T(8,128)S(1)}, s32[2048,27]{0,1:T(8,128)}, u32[]{:S(2)}) copy-start(s32[2048,27]{0,1:T(8,128)} %param.17) | copy-start | bytes 663556
  71.3 54.1 %all-to-all-start.1 = ((bf16[32,128,256]{2,1,0:T(8,128)(2,1)}), bf16[32,128,256]{2,1,0:T(8,128)(2,1)S(1)}, u32[]{:S(2)}, u32[]{:S(2)}) async-start(bf16[32,128,256]{2,1,0:T(8,128)(2,1)} %bitcast.16), calls=%async_computation.1 | async-start | bytes 4194304 | tf_op jit(solution)/shard_map/all_to_all | solution.py:446
  125.4 1.3 copy-start.5
  125.4 17.1 %copy-start.8 = (s32[2048,27]{0,1:T(8,128)S(1)}, s32[2048,27]{0,1:T(8,128)}, u32[]{:S(2)}) copy-start(s32[2048,27]{0,1:T(8,128)} %select_multiply_fusion) | copy-start | bytes 663556
  126.8 43.4 %copy-start = (bf16[6912,256]{1,0:T(8,128)(2,1)S(1)}, bf16[6912,256]{1,0:T(8,128)(2,1)}, u32[]{:S(2)}) copy-start(bf16[6912,256]{1,0:T(8,128)(2,1)} %refs_6_.1) | copy-start | bytes 10616836
  135.2 23.6 %collective-permute-start.2 = (bf16[1280,256]{1,0:T(8,128)(2,1)}, bf16[1280,256]{1,0:T(8,128)(2,1)}, u32[]{:S(2)}, u32[]{:S(2)}) collective-permute-start(bf16[1280,256]{1,0:T(8,128)(2,1)} %get-tuple-element.18), channel_id=1, source_target_pairs={{0,1},{1,2},{2,3},{3,4},{4,5},{5,6},{6,7},{7,8},{8,9},{9,10},{10,1... | collective-permute-start | bytes 1966088 | tf_op jit(solution)/shard_map/ppermute | solution.py:455
  138.4 31.8 %collective-permute-start.3 = (bf16[1280,256]{1,0:T(8,128)(2,1)}, bf16[1280,256]{1,0:T(8,128)(2,1)}, u32[]{:S(2)}, u32[]{:S(2)}) collective-permute-start(bf16[1280,256]{1,0:T(8,128)(2,1)} %get-tuple-element.20), channel_id=1, source_target_pairs={{1,0},{2,1},{3,2},{4,3},{5,4},{6,5},{7,6},{8,7},{9,8},{10,9},{11,1... | collective-permute-start | bytes 1966088 | tf_op jit(solution)/shard_map/ppermute | solution.py:456
  142.6 7.4 %copy-start.6 = (s32[2048,12]{0,1:T(8,128)}, s32[2048,12]{0,1:T(8,128)S(1)}, u32[]{:S(2)}) copy-start(s32[2048,12]{0,1:T(8,128)S(1)} %get-tuple-element.27) | copy-start | bytes 294916
  142.6 7.4 %copy-start.7 = (s32[2048,12]{0,1:T(8,128)}, s32[2048,12]{0,1:T(8,128)S(1)}, u32[]{:S(2)}) copy-start(s32[2048,12]{0,1:T(8,128)S(1)} %get-tuple-element.28) | copy-start | bytes 294916
  142.6 43.9 %collective-permute-start.4 = (bf16[768,256]{1,0:T(8,128)(2,1)}, bf16[768,256]{1,0:T(8,128)(2,1)}, u32[]{:S(2)}, u32[]{:S(2)}) collective-permute-start(bf16[768,256]{1,0:T(8,128)(2,1)} %get-tuple-element.21), channel_id=1, source_target_pairs={{0,1},{1,2},{2,3},{3,4},{4,5},{5,6},{6,7},{7,8},{8,9},{9,10},{10,1... | collective-permute-start | bytes 1179656 | tf_op jit(solution)/shard_map/ppermute | solution.py:457
  144.5 42.0 %collective-permute-start.5 = (bf16[768,256]{1,0:T(8,128)(2,1)}, bf16[768,256]{1,0:T(8,128)(2,1)}, u32[]{:S(2)}, u32[]{:S(2)}) collective-permute-start(bf16[768,256]{1,0:T(8,128)(2,1)} %get-tuple-element.22), channel_id=1, source_target_pairs={{1,0},{2,1},{3,2},{4,3},{5,4},{6,5},{7,6},{8,7},{9,8},{10,9},{11,1... | collective-permute-start | bytes 1179656 | tf_op jit(solution)/shard_map/ppermute | solution.py:458
  170.2 1.2 copy-start.1
  171.4 0.9 copy-start.3
  172.3 0.8 copy-start.4
  173.1 13.4 %copy-start.2 = (s32[3,1,12288]{2,1,0:T(1,128)S(1)}, s32[3,1,12288]{2,1,0:T(1,128)}, u32[]{:S(2)}) copy-start(s32[3,1,12288]{2,1,0:T(1,128)} %reshape.27.index_ref) | copy-start | bytes 442372

commit v7 on v5

--- a/solution.py
+++ b/solution.py
@@ -285,7 +285,7 @@
 def conv_kernel(segment, starts, stores, sources, kept, rows, index_ref, *refs):
     parts, refs = refs[: len(sources)], refs[len(sources) :]
     olds, refs = refs[: len(kept)], refs[len(kept) :]
-    weight_ref, linear_ref, out_ref, table, ping, pong, summed = refs
+    weight_ref, linear_ref, out_ref, table, ping, pong, summed, arrived, *stages = refs
     step = pl.program_id(0)
     width = out_ref.shape[1]
     offsets = weight_ref.shape[0] // width
@@ -297,7 +297,14 @@
 
     @pl.when(step == 0)
     def _():
-        for (first, count), ref in zip(sources, parts):
+        copies = [
+            pltpu.make_async_copy(ref, stage, arrived.at[place])
+            for place, (ref, stage) in enumerate(zip(parts, stages))
+        ]
+        for copy in copies:
+            copy.start()
+        for (first, count), ref, copy in zip(sources, stages, copies):
+            copy.wait()
             for side in range(sides):
                 table[pl.ds(2 * first + side, count, stride=2), :] = ref[:, side * LANES : (side + 1) * LANES].astype(
                     jnp.float32
@@ -385,14 +392,17 @@
         out_shape=jax.ShapeDtypeStruct((count, channels), jnp.bfloat16),
         grid=(steps,),
         in_specs=[pl.BlockSpec((1, 1, index.shape[2]), lambda step: (step, 0, 0), memory_space=pltpu.SMEM)]
-        + [vmem] * (len(parts) + len(olds) + 2),
+        + [pl.BlockSpec(memory_space=pl.ANY)] * len(parts)
+        + [vmem] * (len(olds) + 2),
         out_specs=vmem,
         scratch_shapes=[
             pltpu.VMEM((6 * rows + 8, LANES), jnp.float32),
             pltpu.VMEM((4 * segment, LANES), jnp.float32),
             pltpu.VMEM((4 * segment, LANES), jnp.float32),
             pltpu.VMEM((2 * segment, channels), jnp.float32),
-        ],
+            pltpu.SemaphoreType.DMA((len(parts),)),
+        ]
+        + [pltpu.VMEM(part.shape, part.dtype) for part in parts],
         compiler_params=pltpu.CompilerParams(vmem_limit_bytes=20 << 20),
         name="position_conv",
     )(index, *parts, *olds, weight, linear)

time: 226 us -> 228 us (level)
  transfers between devices with their start and end apart: 8 -> 8, of which waited for: 2 -> 2; matrix products, arithmetic and copies ran while one was open for 4% -> 4% of each run, Pallas kernels for 32% -> 33%
where the time goes in v7:
time: 228 us; the launch traced here: 227 us
  Pallas kernels  122 us (54%)
  waiting for transfers between devices  59 us (26%)
  starting transfers between devices  29.7 us (13%)
  local copies, waits for them, and re-layouts  13.3 us (6%)
  other arithmetic  2.93 us (1%)
    pallas_call x2, Pallas kernels, position_conv(): pl.pallas_call(functools.partial(conv_kernel, segment, starts, stores, so...  54.8 us
    all_to_all x1, waiting for transfers between devices, on_device(): lax.all_to_all(send.reshape(devices, capacity, channels), AXES, split_axi...  47.5 us
    pallas_call x1, Pallas kernels, outer_block(): pl.pallas_call(outer_kernel, out_shape=jax.ShapeDtypeStruct((slots, chann...  30.5 us
    pallas_call x1, Pallas kernels, inner_block(): pl.pallas_call(inner_kernel, out_shape=jax.ShapeDtypeStruct((count, chann...  26.7 us
    ppermute x1, waiting for transfers between devices, on_device(): right_near = lax.ppermute(lower_near, AXES, ring_down[:-1])  11.5 us
    pallas_call x1, Pallas kernels, settle(): pl.pallas_call(functools.partial(settle_kernel, spans), out_shape=tuple((...  7.67 us
    all_to_all x1, starting transfers between devices, on_device(): lax.all_to_all(send.reshape(devices, capacity, channels), AXES, split_axi...  5.83 us
    unnamed x26, local copies, waits for them, and re-layouts  5.64 us
  transfers between devices with their start and end apart: 8, of which 2 were waited for; matrix products, arithmetic and copies ran while one was open for 4% of the time, Pallas kernels for 33%

profile of v7, /device:TPU:1, one launch (start us, length us, event | category | flops | bytes accessed | tf_op | source)
XLA Modules:
  0.0 227.1 jit_solution(13488383467471311915)
XLA Ops:
  0.0 1.1 fusion.3
  1.1 2.2 collective-permute-start
  3.3 2.7 %collective-permute-start.1 = (bf16[512,256]{1,0:T(8,128)(2,1)S(1)}, bf16[512,256]{1,0:T(8,128)(2,1)S(1)}, u32[]{:S(2)}, u32[]{:S(2)}) collective-permute-start(bf16[512,256]{1,0:T(8,128)(2,1)S(1)} %get-tuple-element.23), channel_id=1, source_target_pairs={{1,0},{2,1},{3,2},{4,3},{5,4},{6,5},{7,6},{8,7},{9,8},{10,9},{11,1... | collective-permute-start | bytes 786440 | tf_op jit(solution)/shard_map/ppermute | solution.py:430
  5.9 26.7 %inner_block.1.inner_ref = bf16[1024,256]{1,0:T(8,128)(2,1)} custom-call(bf16[2048,256]{1,0:T(8,128)(2,1)} %own_ref.3, bf16[256,768]{1,0:T(8,128)(2,1)} %qkv_ref.3, bf16[256,256]{1,0:T(8,128)(2,1)} %proj_ref.3, bf16[256,1024]{1,0:T(8,128)(2,1)} %up_ref.3, bf16[1024,256]{1,0:T(8,128)(2,1)} %down_ref.3), custom_call_target="tpu_custom_call" | custom-call | tf_op jit(solution)/shard_map/inner_block/pallas_call | solution.py:204
  32.6 2.2 find_slots.1
  34.8 4.3 %all-to-all-start = ((s32[32,1,128]{2,1,0:T(1,128)}), s32[32,1,128]{2,1,0:T(1,128)S(1)}, u32[]{:S(2)}, u32[]{:S(2)}) async-start(s32[32,1,128]{2,1,0:T(1,128)} %bitcast.19), calls=%async_computation | async-start | bytes 32768 | tf_op jit(solution)/shard_map/all_to_all | solution.py:434
  39.1 0.0 collective-permute-done.left_ref
  39.1 0.0 copy-start.9
  39.1 0.0 collective-permute-done.1.right_ref
  39.1 0.0 copy-start.10
  39.2 0.7 copy-done.9
  39.8 0.1 copy-done.10
  39.9 30.5 %outer_block.1 = bf16[4096,256]{1,0:T(8,128)(2,1)} custom-call(s32[1,2048]{1,0:T(1,128)} %get-tuple-element.16.index_ref, bf16[512,256]{1,0:T(8,128)(2,1)} %copy-done.9, bf16[2048,256]{1,0:T(8,128)(2,1)} %own_ref.3, bf16[512,256]{1,0:T(8,128)(2,1)} %copy-done.10, bf16[1024,256]{1,0:T(8,128)(2,1)} %inner_block.1.inner_ref, bf16[256,768]{1,0:T(8,128)(2,1)} %qkv_ref.3, ...), custom_call_target="tpu_custom_call" | custom-call | tf_op jit(solution)/shard_map/outer_block/pallas_call | solution.py:224
  70.4 0.0 all-to-all-done
  70.4 0.0 copy-start.12
  70.4 0.0 copy-start.11
  70.4 0.6 copy-done.12
  71.0 5.8 %all-to-all-start.1 = ((bf16[32,128,256]{2,1,0:T(8,128)(2,1)}), bf16[32,128,256]{2,1,0:T(8,128)(2,1)S(1)}, u32[]{:S(2)}, u32[]{:S(2)}) async-start(bf16[32,128,256]{2,1,0:T(8,128)(2,1)} %bitcast.16), calls=%async_computation.1 | async-start | bytes 4194304 | tf_op jit(solution)/shard_map/all_to_all | solution.py:438
  76.8 0.0 copy-done.11
  76.8 0.7 select_multiply_fusion
  77.6 47.5 %all-to-all-done.1 = bf16[32,128,256]{2,1,0:T(8,128)(2,1)S(1)} async-done(((bf16[32,128,256]{2,1,0:T(8,128)(2,1)}), bf16[32,128,256]{2,1,0:T(8,128)(2,1)S(1)}, u32[]{:S(2)}, u32[]{:S(2)}) %all-to-all-start.1) | async-done | bytes 2097184 | tf_op jit(solution)/shard_map/all_to_all | solution.py:438
  125.1 0.0 copy-start.5
  125.1 0.0 copy-start.8
  125.1 1.3 copy-done.5
  126.4 0.0 copy-start
  126.4 7.7 %settle.1 = (bf16[2048,256]{1,0:T(8,128)(2,1)}, bf16[1280,256]{1,0:T(8,128)(2,1)}, bf16[1280,256]{1,0:T(8,128)(2,1)}, bf16[768,256]{1,0:T(8,128)(2,1)}, bf16[768,256]{1,0:T(8,128)(2,1)}) custom-call(s32[32,128]{1,0:T(8,128)} %bitcast.18, bf16[4096,256]{1,0:T(8,128)(2,1)} %bitcast.15), custom_call_target="tpu_custom_call" | custom-call | tf_op jit(solution)/shard_map/settle/pallas_call | solution.py:267
  134.1 3.2 %collective-permute-start.2 = (bf16[1280,256]{1,0:T(8,128)(2,1)}, bf16[1280,256]{1,0:T(8,128)(2,1)}, u32[]{:S(2)}, u32[]{:S(2)}) collective-permute-start(bf16[1280,256]{1,0:T(8,128)(2,1)} %get-tuple-element.18), channel_id=1, source_target_pairs={{0,1},{1,2},{2,3},{3,4},{4,5},{5,6},{6,7},{7,8},{8,9},{9,10},{10,1... | collective-permute-start | bytes 1966088 | tf_op jit(solution)/shard_map/ppermute | solution.py:447
  137.3 4.1 %collective-permute-start.3 = (bf16[1280,256]{1,0:T(8,128)(2,1)}, bf16[1280,256]{1,0:T(8,128)(2,1)}, u32[]{:S(2)}, u32[]{:S(2)}) collective-permute-start(bf16[1280,256]{1,0:T(8,128)(2,1)} %get-tuple-element.20), channel_id=1, source_target_pairs={{1,0},{2,1},{3,2},{4,3},{5,4},{6,5},{7,6},{8,7},{9,8},{10,9},{11,1... | collective-permute-start | bytes 1966088 | tf_op jit(solution)/shard_map/ppermute | solution.py:448
  141.5 0.0 copy-done.8
  141.5 0.0 copy-start.6
  141.5 0.0 copy-start.7
  141.5 1.9 collective-permute-start.4
  143.4 5.4 %collective-permute-start.5 = (bf16[768,256]{1,0:T(8,128)(2,1)}, bf16[768,256]{1,0:T(8,128)(2,1)}, u32[]{:S(2)}, u32[]{:S(2)}) collective-permute-start(bf16[768,256]{1,0:T(8,128)(2,1)} %get-tuple-element.22), channel_id=1, source_target_pairs={{1,0},{2,1},{3,2},{4,3},{5,4},{6,5},{7,6},{8,7},{9,8},{10,9},{11,1... | collective-permute-start | bytes 1179656 | tf_op jit(solution)/shard_map/ppermute | solution.py:450
  148.9 0.0 copy-done.6
  148.9 0.0 copy-done.7
  148.9 0.6 fusion.2
  149.5 1.5 reshape.33.index_ref
  151.0 0.9 fusion.1
  151.9 0.7 pad_add_fusion
  152.6 1.7 reshape.26
  154.3 1.6 copy.13
  155.9 1.7 reshape.27.index_ref
  157.7 0.0 collective-permute-done.2.refs_0_
  157.7 11.5 %collective-permute-done.3.refs_2_ = bf16[1280,256]{1,0:T(8,128)(2,1)} collective-permute-done((bf16[1280,256]{1,0:T(8,128)(2,1)}, bf16[1280,256]{1,0:T(8,128)(2,1)}, u32[]{:S(2)}, u32[]{:S(2)}) %collective-permute-start.3) | collective-permute-done | bytes 655392 | tf_op jit(solution)/shard_map/ppermute | solution.py:448
  169.1 0.0 copy-done
  169.1 0.0 copy-start.1
  169.1 1.2 copy-done.1
  170.3 0.0 copy-start.3
  170.3 0.9 copy-done.3
  171.2 0.0 copy-start.4
  171.2 0.8 copy-done.4
  172.0 0.0 copy-start.2
  172.0 14.6 %position_conv.2.refs_5_ = bf16[512,256]{1,0:T(8,128)(2,1)S(1)} custom-call(s32[1,1,12288]{2,1,0:T(1,128)S(1)} %copy-done.4, bf16[1280,256]{1,0:T(8,128)(2,1)} %collective-permute-done.2.refs_0_, bf16[2048,256]{1,0:T(8,128)(2,1)S(1)} %copy-done.1, bf16[1280,256]{1,0:T(8,128)(2,1)} %collective-permute-done.3.refs_2_, bf16[6912,256]{1,0:T(8,128)(2,1)S(1)} %copy-done, ...), custom_call_target="tpu_custom_call" | custom-call | tf_op jit(solution)/shard_map/position_conv/pallas_call | solution.py:390
  186.6 0.0 collective-permute-done.4.refs_3_
  186.7 0.0 collective-permute-done.5.refs_4_
  186.7 0.0 copy-done.2
  186.7 40.2 %position_conv.3 = bf16[2048,256]{1,0:T(8,128)(2,1)} custom-call(s32[3,1,12288]{2,1,0:T(1,128)S(1)} %copy-done.2, bf16[1280,256]{1,0:T(8,128)(2,1)} %collective-permute-done.2.refs_0_, bf16[2048,256]{1,0:T(8,128)(2,1)S(1)} %copy-done.1, bf16[1280,256]{1,0:T(8,128)(2,1)} %collective-permute-done.3.refs_2_, bf16[768,256]{1,0:T(8,128)(2,1)} %collective-permute-done.4.refs_3_, ...), custom_call_target="tpu_custom_call" | custom-call | tf_op jit(solution)/shard_map/position_conv/pallas_call | solution.py:390
  (1 shorter events, 0.0 us)
Async XLA Ops:
  1.1 38.1 %collective-permute-start = (bf16[512,256]{1,0:T(8,128)(2,1)S(1)}, bf16[512,256]{1,0:T(8,128)(2,1)S(1)}, u32[]{:S(2)}, u32[]{:S(2)}) collective-permute-start(bf16[512,256]{1,0:T(8,128)(2,1)S(1)} %get-tuple-element.24), channel_id=1, source_target_pairs={{0,1},{1,2},{2,3},{3,4},{4,5},{5,6},{6,7},{7,8},{8,9},{9,10},{10,1... | collective-permute-start | bytes 786440 | tf_op jit(solution)/shard_map/ppermute | solution.py:429
  3.3 35.9 %collective-permute-start.1 = (bf16[512,256]{1,0:T(8,128)(2,1)S(1)}, bf16[512,256]{1,0:T(8,128)(2,1)S(1)}, u32[]{:S(2)}, u32[]{:S(2)}) collective-permute-start(bf16[512,256]{1,0:T(8,128)(2,1)S(1)} %get-tuple-element.23), channel_id=1, source_target_pairs={{1,0},{2,1},{3,2},{4,3},{5,4},{6,5},{7,6},{8,7},{9,8},{10,9},{11,1... | collective-permute-start | bytes 786440 | tf_op jit(solution)/shard_map/ppermute | solution.py:430
  34.8 35.6 %all-to-all-start = ((s32[32,1,128]{2,1,0:T(1,128)}), s32[32,1,128]{2,1,0:T(1,128)S(1)}, u32[]{:S(2)}, u32[]{:S(2)}) async-start(s32[32,1,128]{2,1,0:T(1,128)} %bitcast.19), calls=%async_computation | async-start | bytes 32768 | tf_op jit(solution)/shard_map/all_to_all | solution.py:434
  39.1 0.7 copy-start.9
  39.1 0.8 copy-start.10
  70.4 0.6 copy-start.12
  70.4 6.4 %copy-start.11 = (s32[2048,27]{0,1:T(8,128)S(1)}, s32[2048,27]{0,1:T(8,128)}, u32[]{:S(2)}) copy-start(s32[2048,27]{0,1:T(8,128)} %param.17) | copy-start | bytes 663556
  71.0 54.1 %all-to-all-start.1 = ((bf16[32,128,256]{2,1,0:T(8,128)(2,1)}), bf16[32,128,256]{2,1,0:T(8,128)(2,1)S(1)}, u32[]{:S(2)}, u32[]{:S(2)}) async-start(bf16[32,128,256]{2,1,0:T(8,128)(2,1)} %bitcast.16), calls=%async_computation.1 | async-start | bytes 4194304 | tf_op jit(solution)/shard_map/all_to_all | solution.py:438
  125.1 1.3 copy-start.5
  125.1 16.4 %copy-start.8 = (s32[2048,27]{0,1:T(8,128)S(1)}, s32[2048,27]{0,1:T(8,128)}, u32[]{:S(2)}) copy-start(s32[2048,27]{0,1:T(8,128)} %select_multiply_fusion) | copy-start | bytes 663556
  126.4 42.7 %copy-start = (bf16[6912,256]{1,0:T(8,128)(2,1)S(1)}, bf16[6912,256]{1,0:T(8,128)(2,1)}, u32[]{:S(2)}) copy-start(bf16[6912,256]{1,0:T(8,128)(2,1)} %refs_6_.1) | copy-start | bytes 10616836
  134.1 23.6 %collective-permute-start.2 = (bf16[1280,256]{1,0:T(8,128)(2,1)}, bf16[1280,256]{1,0:T(8,128)(2,1)}, u32[]{:S(2)}, u32[]{:S(2)}) collective-permute-start(bf16[1280,256]{1,0:T(8,128)(2,1)} %get-tuple-element.18), channel_id=1, source_target_pairs={{0,1},{1,2},{2,3},{3,4},{4,5},{5,6},{6,7},{7,8},{8,9},{9,10},{10,1... | collective-permute-start | bytes 1966088 | tf_op jit(solution)/shard_map/ppermute | solution.py:447
  137.3 31.8 %collective-permute-start.3 = (bf16[1280,256]{1,0:T(8,128)(2,1)}, bf16[1280,256]{1,0:T(8,128)(2,1)}, u32[]{:S(2)}, u32[]{:S(2)}) collective-permute-start(bf16[1280,256]{1,0:T(8,128)(2,1)} %get-tuple-element.20), channel_id=1, source_target_pairs={{1,0},{2,1},{3,2},{4,3},{5,4},{6,5},{7,6},{8,7},{9,8},{10,9},{11,1... | collective-permute-start | bytes 1966088 | tf_op jit(solution)/shard_map/ppermute | solution.py:448
  141.5 7.4 %copy-start.6 = (s32[2048,12]{0,1:T(8,128)}, s32[2048,12]{0,1:T(8,128)S(1)}, u32[]{:S(2)}) copy-start(s32[2048,12]{0,1:T(8,128)S(1)} %get-tuple-element.27) | copy-start | bytes 294916
  141.5 7.4 %copy-start.7 = (s32[2048,12]{0,1:T(8,128)}, s32[2048,12]{0,1:T(8,128)S(1)}, u32[]{:S(2)}) copy-start(s32[2048,12]{0,1:T(8,128)S(1)} %get-tuple-element.28) | copy-start | bytes 294916
  141.5 45.1 %collective-permute-start.4 = (bf16[768,256]{1,0:T(8,128)(2,1)}, bf16[768,256]{1,0:T(8,128)(2,1)}, u32[]{:S(2)}, u32[]{:S(2)}) collective-permute-start(bf16[768,256]{1,0:T(8,128)(2,1)} %get-tuple-element.21), channel_id=1, source_target_pairs={{0,1},{1,2},{2,3},{3,4},{4,5},{5,6},{6,7},{7,8},{8,9},{9,10},{10,1... | collective-permute-start | bytes 1179656 | tf_op jit(solution)/shard_map/ppermute | solution.py:449
  143.4 43.2 %collective-permute-start.5 = (bf16[768,256]{1,0:T(8,128)(2,1)}, bf16[768,256]{1,0:T(8,128)(2,1)}, u32[]{:S(2)}, u32[]{:S(2)}) collective-permute-start(bf16[768,256]{1,0:T(8,128)(2,1)} %get-tuple-element.22), channel_id=1, source_target_pairs={{1,0},{2,1},{3,2},{4,3},{5,4},{6,5},{7,6},{8,7},{9,8},{10,9},{11,1... | collective-permute-start | bytes 1179656 | tf_op jit(solution)/shard_map/ppermute | solution.py:450
  169.1 1.2 copy-start.1
  170.3 0.9 copy-start.3
  171.2 0.8 copy-start.4
  172.0 14.6 %copy-start.2 = (s32[3,1,12288]{2,1,0:T(1,128)S(1)}, s32[3,1,12288]{2,1,0:T(1,128)}, u32[]{:S(2)}) copy-start(s32[3,1,12288]{2,1,0:T(1,128)} %reshape.27.index_ref) | copy-start | bytes 442372
